TPU v7x, 256 devices: a whole 4x4x8 slice. The times are simulated.
256 devices in a mesh: batch: 16 (over y, x_hi, core), feat: 16 (over z, x_lo).
Axes of the slice: x: 4 (x_hi: 2, x_lo: 2; x = x_hi * 2 + x_lo), y: 4, z: 8, core: 2. Of those that a mesh axis runs over, the one named last changes fastest.
Arguments:
- embedding: bfloat16 [1024, 131072], P('feat', 'batch'), may hold values from -6 to 6
- self_weight: bfloat16 [1024, 128], P('feat'), may hold values from -0.1875 to 0.1875
- neighbor_weight: bfloat16 [1024, 128], P('feat'), may hold values from -0.1875 to 0.1875
- up_weight: bfloat16 [128, 1024], replicated, may hold values from -0.5 to 0.5
- down_weight: bfloat16 [1024, 128], replicated, may hold values from -0.1875 to 0.1875
- source_tiles: int32 [2, 8, 64], P(None, None, 'batch'), may hold values from 0 to 7
- neighbor_rows: int32 [2, 8, 16, 16384], P(None, None, None, 'batch'), may hold values from 0 to 1023
- slot_mask: int32 [2, 8, 16384], P(None, None, 'batch'), may hold values 0 or 1
- dest_rows: int32 [2, 16384], P(None, 'batch'), may hold values from 0 to 8191
- owner_order: int32 [2, 16, 1024], P(None, 'batch'), may hold values from 0 to 1023, each once within a row
- output_grad: bfloat16 [2, 16384, 128], P(None, ('batch', 'feat')), may hold values from -16 to 16
Outputs:
- embedding_grad: float32 [1024, 131072], P('feat', 'batch')
- self_grad: float32 [1024, 128], P('feat')
- neighbor_grad: float32 [1024, 128], P('feat')
- up_grad: float32 [128, 1024], replicated
- down_grad: float32 [1024, 128], replicated
Inputs may be any that keep to these rules, and one draw needn't show every extreme that they name: `source_tiles`: numbers of tiles within the group's own 8 source tiles. `neighbor_rows`: rows within the slot's source tile. `dest_rows`: rows within the group's own table. `owner_order`: each of a group's 1024 destinations once per microbatch.
All inputs are finite; a program needn't handle non-finite values. No bound on the sum of `slot_mask` on one device may be relied on, other than what follows from the above.
Results may differ from a plain program's by a relative error of at most 0.006.
Values may be sent and summed in bfloat16 or wider, within the bound.
A program may use at most 128 MiB of HBM per device.

v0:
```python
import math

import jax
import jax.numpy as jnp
from jax import lax
from jax.sharding import PartitionSpec as P

H = 128
TD = 256
TS = 1024
K = 8
NB = 16


def cut_along(x, dim, devices):
    shape = x.shape
    pieces = x.reshape(*shape[:dim], devices, shape[dim] // devices, *shape[dim + 1 :])
    return jnp.moveaxis(pieces, dim, 0)


def summed_on_arrival(x, axis, dim):
    pieces = cut_along(x, dim, lax.axis_size(axis))
    arrived = lax.all_to_all(pieces, axis, split_axis=0, concat_axis=0, tiled=True)
    return arrived.sum(axis=0)


def in_order(pieces, dim):
    pieces = jnp.moveaxis(pieces, 0, dim)
    shape = pieces.shape
    return pieces.reshape(*shape[:dim], shape[dim] * shape[dim + 1], *shape[dim + 2 :])


def copy_for_each(x, axis):
    devices = lax.axis_size(axis)
    return lax.all_to_all(jnp.broadcast_to(x[None], (devices, *x.shape)), axis, 0, 0, tiled=True)


def gathered_copies(x, axis, dim):
    return in_order(copy_for_each(x, axis), dim)


def in_one(arrays, axis):
    line, at, gathered = (jnp.concatenate([a.reshape(-1) for a in arrays]), 0, [])
    running = lax.psum(line, axis)
    for a in arrays:
        gathered.append(running[at : at + a.size].reshape(a.shape))
        at += a.size
    return tuple(gathered)


def over_copies(x, axis):
    everything = copy_for_each(x, axis)
    return jnp.sum(everything, axis=0)


def packed_total(arrays, axis):
    ends = [0]
    for a in arrays:
        ends.append(ends[-1] + a.size)
    running = over_copies(jnp.concatenate([a.ravel() for a in arrays]), axis)
    return tuple((running[b:e].reshape(a.shape) for a, b, e in zip(arrays, ends, ends[1:])))


def gelu_slope(values):
    result, pullback = jax.vjp(jax.nn.gelu, values)
    return (result, pullback(jnp.ones_like(values))[0])


def adjacency(rows_micro, valid_micro):
    positions = jnp.arange(TS, dtype=jnp.int32)
    matches = (rows_micro[:, :, :, None] == positions[None, None, None, :]).astype(jnp.int32)
    hits = jnp.sum(matches, axis=1)
    return (hits * valid_micro[:, :, None]).astype(jnp.bfloat16)


def mlp_pass(hidden, target, up_weight, down_weight):
    first_value, first_slope = gelu_slope(hidden)
    first_act = first_value.astype(jnp.bfloat16)
    inner_pre = jnp.dot(first_act, up_weight, preferred_element_type=jnp.float32)
    inner_value, inner_slope = gelu_slope(inner_pre)
    inner_act = inner_value.astype(jnp.bfloat16)
    down_part = jnp.dot(inner_act.T, target, preferred_element_type=jnp.float32)
    inner_grad = (
        jnp.dot(target, down_weight.T, preferred_element_type=jnp.float32) * inner_slope
    ).astype(jnp.bfloat16)
    up_part = jnp.dot(first_act.T, inner_grad, preferred_element_type=jnp.float32)
    hidden_grad = (
        jnp.dot(inner_grad, up_weight.T, preferred_element_type=jnp.float32) * first_slope
    ).astype(jnp.bfloat16)
    return (hidden_grad, up_part, down_part)


def local(
    embedding,
    self_weight,
    neighbor_weight,
    up_weight,
    down_weight,
    source_tiles,
    neighbor_rows,
    slot_mask,
    dest_rows,
    owner_order,
    output_grad,
):
    feat_total = lax.axis_size("feat")
    batch_total = lax.axis_size("batch")
    columns = embedding.shape[0]
    source_total = embedding.shape[1]
    micro_total = source_tiles.shape[0]
    tile_total = source_tiles.shape[2]
    dest_total = dest_rows.shape[1]
    owned_rows = dest_total // feat_total
    agg_scale = 1.0 / math.sqrt(K * NB)
    norm_factor = 1.0 / math.sqrt(micro_total * dest_total * batch_total)
    table_tiles = embedding.reshape(columns, -1, TS)
    table_grad = jnp.zeros(table_tiles.shape, jnp.float32)
    self_sum = jnp.zeros((columns, H), jnp.float32)
    neighbor_sum = jnp.zeros((columns, H), jnp.float32)
    up_sum = jnp.zeros(up_weight.shape, jnp.float32)
    down_sum = jnp.zeros(down_weight.shape, jnp.float32)
    tile_steps = jnp.arange(tile_total, dtype=jnp.int32)
    for micro_index in range(micro_total):
        tile_ids = source_tiles[micro_index]
        counts_all = adjacency(neighbor_rows[micro_index], slot_mask[micro_index]).reshape(
            K, tile_total, TD, TS
        )

        def aggregate_tile(tile_index, tile_ids=tile_ids, counts_all=counts_all):
            counts = lax.dynamic_index_in_dim(counts_all, tile_index, 1, keepdims=False)
            picked = lax.dynamic_index_in_dim(tile_ids, tile_index, 1, keepdims=False)
            pieces = table_tiles[:, picked]
            summed = jnp.einsum("kds,cks->dc", counts, pieces, preferred_element_type=jnp.float32)
            return (summed * agg_scale).astype(jnp.bfloat16)

        gathered = lax.map(aggregate_tile, tile_steps).reshape(dest_total, columns)
        own_rows = embedding[:, dest_rows[micro_index]].T
        row_order = owner_order[micro_index, 0]
        ordered_own = own_rows[row_order]
        ordered_agg = gathered[row_order]

        def partial_rows(row_start, row_count, ordered_own=ordered_own, ordered_agg=ordered_agg):
            return jnp.dot(ordered_own, self_weight, preferred_element_type=jnp.float32) + jnp.dot(
                ordered_agg, neighbor_weight, preferred_element_type=jnp.float32
            )

        hidden = summed_on_arrival(
            partial_rows(jnp.int32(0), owned_rows * lax.axis_size("feat")), "feat", 0
        )
        owner_grad, up_part, down_part = mlp_pass(
            hidden, output_grad[micro_index], up_weight, down_weight
        )
        ordered_grad = gathered_copies(owner_grad, "feat", 0)
        up_sum = up_sum + up_part
        down_sum = down_sum + down_part
        hidden_grad = jnp.zeros((dest_total, H), jnp.bfloat16).at[row_order].set(ordered_grad)
        self_sum = self_sum + jnp.dot(own_rows.T, hidden_grad, preferred_element_type=jnp.float32)
        neighbor_sum = neighbor_sum + jnp.dot(
            gathered.T, hidden_grad, preferred_element_type=jnp.float32
        )
        back_grad = (
            jnp.dot(hidden_grad, neighbor_weight.T, preferred_element_type=jnp.float32)
            .astype(jnp.bfloat16)
            .reshape(tile_total, TD, columns)
        )

        def spread_tile(
            carried, tile_index, tile_ids=tile_ids, counts_all=counts_all, back_grad=back_grad
        ):
            counts = lax.dynamic_index_in_dim(counts_all, tile_index, 1, keepdims=False)
            picked = lax.dynamic_index_in_dim(tile_ids, tile_index, 1, keepdims=False)
            back_tile = lax.dynamic_index_in_dim(back_grad, tile_index, 0, keepdims=False)
            spread = (
                jnp.einsum("kds,dc->cks", counts, back_tile, preferred_element_type=jnp.float32)
                * agg_scale
            )
            return (carried.at[:, picked].add(spread), None)

        table_grad, unused = lax.scan(spread_tile, table_grad, tile_steps)
        own_grad = jnp.dot(self_weight, hidden_grad.T, preferred_element_type=jnp.float32)
        flat_grad = (
            table_grad.reshape(columns, source_total).at[:, dest_rows[micro_index]].add(own_grad)
        )
        table_grad = flat_grad.reshape(table_tiles.shape)
    up_sum, down_sum = in_one((up_sum, down_sum), ("batch", "feat"))
    self_sum, neighbor_sum = packed_total((self_sum, neighbor_sum), "batch")
    return (
        table_grad.reshape(embedding.shape),
        self_sum * norm_factor,
        neighbor_sum * norm_factor,
        up_sum * norm_factor,
        down_sum * norm_factor,
    )


def solution(mesh):
    in_specs = (
        P("feat", "batch"),
        P("feat", None),
        P("feat", None),
        P(),
        P(),
        P(None, None, "batch"),
        P(None, None, None, "batch"),
        P(None, None, "batch"),
        P(None, "batch"),
        P(None, "batch", None),
        P(None, ("batch", "feat"), None),
    )
    out_specs = (P("feat", "batch"), P("feat", None), P("feat", None), P(), P())
    return jax.shard_map(local, mesh=mesh, in_specs=in_specs, out_specs=out_specs, check_vma=False)
```

profile of v0, /device:TPU:1, one launch (start us, length us, event | category | flops | bytes accessed | tf_op | source)
XLA Modules:
  0.0 615.0 jit_solution(13062124381768402570)
XLA Ops:
  16.5 80.5 %convert_reduce_fusion.1 = s32[8,1024,1024]{2,1,0:T(8,128)} fusion(s32[8,16,1024]{2,1,0:T(8,128)S(1)} %get-tuple-element.321), kind=kLoop, calls=%fused_computation.64 | loop fusion | flops 394264576 | bytes 34078720 | tf_op jit(solution)/shard_map/reduce_sum | solution.py:72
  97.0 12.4 %multiply_convert_fusion.1 = bf16[8,4,256,1024]{3,2,1,0:T(8,128)(2,1)S(1)} fusion(s32[8,4,256,1024]{3,2,1,0:T(8,128)} %bitcast.242, s32[8,4,256]{2,1,0:T(4,128)S(1)} %copy.89), kind=kLoop, calls=%fused_computation.67 | loop fusion | flops 16777216 | bytes 50364416 | tf_op jit(solution)/shard_map/convert_element_type | solution.py:73
  109.5 6.7 %copy.90 = bf16[8,4,256,1024]{3,2,0,1:T(8,128)(2,1)} copy(bf16[8,4,256,1024]{3,2,1,0:T(8,128)(2,1)S(1)} %multiply_convert_fusion.1) | data formatting | bytes 33554432 | tf_op jit(solution)/shard_map/while | solution.py:136
  116.3 28.2 %while.40 = (s32[]{:T(128)}, bf16[4,256,64]{1,2,0:T(8,128)(2,1)S(1)}, s32[4]{0:T(128)S(1)}, bf16[8,4,256,1024]{3,2,0,1:T(8,128)(2,1)}, s32[8,4]{0,1:T(4,128)}, /...) while((s32[]{:T(128)}, bf16[4,256,64]{1,2,0:T(8,128)(2,1)S(1)}, s32[4]{0:T(128)S(1)}, ...), condition=%wide.region_2.3_spmd, body=%wide.region_1.2_spmd.sunk | while | flops 268469280 | bytes 7377183 | solution.py:136
  144.8 4.7 gather_fusion.2
  157.2 10.1 %all-to-all-start = ((f32[16,64,128]{2,1,0:T(8,128)}), f32[16,64,128]{2,1,0:T(8,128)}, u32[]{:S(2)}, u32[]{:S(2)}) async-start(f32[16,64,128]{2,1,0:T(8,128)} %bitcast.34), calls=%async_computation | async-start | bytes 1048576 | tf_op jit(solution)/shard_map/all_to_all | solution.py:23
  167.3 80.5 %convert_reduce_fusion = s32[8,1024,1024]{2,1,0:T(8,128)} fusion(s32[8,16,1024]{2,1,0:T(8,128)S(1)} %copy-done.4), kind=kLoop, calls=%fused_computation.62 | loop fusion | flops 394264576 | bytes 34078720 | tf_op jit(solution)/shard_map/reduce_sum | solution.py:72
  247.8 12.4 %multiply_convert_fusion = bf16[8,4,256,1024]{3,2,1,0:T(8,128)(2,1)S(1)} fusion(s32[8,4,256,1024]{3,2,1,0:T(8,128)} %bitcast.243, s32[8,4,256]{2,1,0:T(4,128)S(1)} %copy.98), kind=kLoop, calls=%fused_computation.66 | loop fusion | flops 16777216 | bytes 50364416 | tf_op jit(solution)/shard_map/convert_element_type | solution.py:73
  260.3 6.7 %copy.99 = bf16[8,4,256,1024]{3,2,0,1:T(8,128)(2,1)} copy(bf16[8,4,256,1024]{3,2,1,0:T(8,128)(2,1)S(1)} %multiply_convert_fusion) | data formatting | bytes 33554432 | tf_op jit(solution)/shard_map/while | solution.py:136
  267.0 29.5 %while.42 = (s32[]{:T(128)}, bf16[4,256,64]{1,2,0:T(8,128)(2,1)S(1)}, s32[4]{0:T(128)S(1)}, bf16[8,4,256,1024]{3,2,0,1:T(8,128)(2,1)}, s32[8,4]{0,1:T(4,128)}, /...) while((s32[]{:T(128)}, bf16[4,256,64]{1,2,0:T(8,128)(2,1)S(1)}, ...), condition=%wide.region_11.12_spmd, body=%wide.region_10.11_spmd.sunk | while | flops 268469280 | bytes 7377183 | solution.py:136
  296.5 4.7 gather_fusion.5
  309.8 7.5 %all-to-all-start.2 = ((f32[16,64,128]{2,1,0:T(8,128)}), f32[16,64,128]{2,1,0:T(8,128)S(1)}, u32[]{:S(2)}, u32[]{:S(2)}) async-start(f32[16,64,128]{2,1,0:T(8,128)} %bitcast.48), calls=%async_computation.2 | async-start | bytes 1048576 | tf_op jit(solution)/shard_map/all_to_all | solution.py:23
  319.6 13.0 %all-to-all-done.2 = f32[16,64,128]{2,1,0:T(8,128)S(1)} async-done(((f32[16,64,128]{2,1,0:T(8,128)}), f32[16,64,128]{2,1,0:T(8,128)S(1)}, u32[]{:S(2)}, u32[]{:S(2)}) %all-to-all-start.2) | async-done | bytes 524320 | tf_op jit(solution)/shard_map/all_to_all | solution.py:23
  333.3 4.4 all-to-all-start.1
  341.2 6.2 %all-to-all-done.1 = bf16[16,64,128]{2,1,0:T(8,128)(2,1)} async-done(((bf16[16,64,128]{2,1,0:T(8,128)(2,1)}), bf16[16,64,128]{2,1,0:T(8,128)(2,1)}, u32[]{:S(2)}, u32[]{:S(2)}) %all-to-all-start.1) | async-done | bytes 262176 | tf_op jit(solution)/shard_map/all_to_all | solution.py:35
  348.2 4.2 all-to-all-start.3
  352.4 3.8 scatter_custom_fusion.2
  358.6 45.3 %while.41 = (s32[]{:T(128)}, f32[64,8,1024]{2,0,1:T(8,128)}, s32[4]{0:T(128)}, s32[8,4]{0,1:T(4,128)}, bf16[4,256,64]{1,2,0:T(8,128)(2,1)S(1)}, /*index=5*/bf16[...) while((s32[]{:T(128)}, f32[64,8,1024]{2,0,1:T(8,128)}, s32[4]{0:T(128)}, s32[8,4]{0,1:T(4,128)}, ...), condition=%wide.region_7.8_spmd, body=%wide.region_5.7_spmd.sunk | while | flops 269484064 | bytes 12616951 | solution.py:179
  365.6 4.3 scatter_fusion
  377.0 4.3 scatter_fusion
  388.3 4.3 scatter_fusion
  399.6 4.3 scatter_fusion
  408.8 9.5 %scatter_fusion.2 = f32[64,8192]{0,1:T(8,128)} fusion(f32[64,8192]{0,1:T(8,128)} %bitcast.246, s32[1024]{0:T(1024)S(1)} %bitcast.263, f32[1024,64]{1,0:T(8,128)S(1)} %fusion.129), kind=kCustom, calls=%fused_computation.11 | custom fusion | flops 65536 | bytes 790528 | tf_op jit(solution)/shard_map/scatter-add | solution.py:182
  418.3 3.8 copy.102
  428.8 10.2 %all-to-all-start.4 = ((f32[16,1,16384]{2,1,0:T(1,128)}), f32[16,1,16384]{2,1,0:T(1,128)}, u32[]{:S(2)}, u32[]{:S(2)}) async-start(f32[16,1,16384]{2,1,0:T(1,128)} %broadcast_in_dim.21), calls=%async_computation.4 | async-start | bytes 2097152 | tf_op jit(solution)/shard_map/all_to_all | solution.py:35
  439.1 41.6 %while.43 = (s32[]{:T(128)}, f32[64,8,1024]{2,0,1:T(8,128)}, s32[4]{0:T(128)S(1)}, s32[8,4]{0,1:T(4,128)}, bf16[4,256,64]{1,2,0:T(8,128)(2,1)S(1)}, /*index=5*/b...) while((s32[]{:T(128)}, f32[64,8,1024]{2,0,1:T(8,128)}, s32[4]{0:T(128)S(1)}, ...), condition=%wide.region_16.17_spmd, body=%wide.region_14.16_spmd.sunk | while | flops 269484064 | bytes 12616951 | solution.py:179
  445.3 4.3 scatter_fusion.1
  455.7 4.2 scatter_fusion.1
  466.1 4.3 scatter_fusion.1
  476.6 4.1 scatter_fusion.1
  484.7 9.5 %scatter_fusion.3 = f32[64,8192]{0,1:T(8,128)} fusion(f32[64,8192]{0,1:T(8,128)} %bitcast.245, s32[1024]{0:T(1024)S(1)} %bitcast.261, f32[1024,64]{1,0:T(8,128)S(1)} %fusion.131), kind=kCustom, calls=%fused_computation.13 | custom fusion | flops 65536 | bytes 790528 | tf_op jit(solution)/shard_map/scatter-add | solution.py:182
  498.0 104.6 %all-reduce.2.cloned.1.call-done = f32[262144]{0:T(1024)} async-done(((f32[262144]{0:T(1024)}), f32[262144]{0:T(1024)}) %all-reduce.2.cloned.1.call-update) | async-done | bytes 1048592 | tf_op jit(solution)/shard_map/psum | solution.py:44
  (171 shorter events, 141.8 us)
Async XLA Ops:
  7.2 311.2 %copy-start = (bf16[128,1024]{1,0:T(8,128)(2,1)S(1)}, bf16[128,1024]{1,0:T(8,128)(2,1)}, u32[]{:S(2)}) copy-start(bf16[128,1024]{1,0:T(8,128)(2,1)} %param.22) | copy-start | bytes 786436
  9.8 87.2 %copy-start.16 = (s32[1024,1]{0,1:T(1,128)}, s32[1024,1]{0,1:T(1,128)S(1)}, u32[]{:S(2)}) copy-start(s32[1024,1]{0,1:T(1,128)S(1)} %get-tuple-element.329) | copy-start | bytes 12292
  13.9 0.6 copy-start.13
  16.5 80.5 %copy-start.10 = (s32[2,8,1024]{2,1,0:T(8,128)S(1)}, s32[2,8,1024]{2,1,0:T(8,128)}, u32[]{:S(2)}) copy-start(s32[2,8,1024]{2,1,0:T(8,128)} %param.26) | copy-start | bytes 196612
  109.5 6.7 %copy-start.3 = (bf16[64,8192]{1,0:T(8,128)(2,1)S(1)}, bf16[64,8192]{1,0:T(8,128)(2,1)}, u32[]{:S(2)}) copy-start(bf16[64,8192]{1,0:T(8,128)(2,1)} %param.19) | copy-start | bytes 3145732
  144.6 11.4 %copy-start.5 = (bf16[64,128]{1,0:T(8,128)(2,1)S(1)}, bf16[64,128]{1,0:T(8,128)(2,1)}, u32[]{:S(2)}) copy-start(bf16[64,128]{1,0:T(8,128)(2,1)} %param.20) | copy-start | bytes 49156
  144.6 11.6 %copy-start.6 = (bf16[64,128]{1,0:T(8,128)(2,1)S(1)}, bf16[64,128]{1,0:T(8,128)(2,1)}, u32[]{:S(2)}) copy-start(bf16[64,128]{1,0:T(8,128)(2,1)} %param.21) | copy-start | bytes 49156
  149.5 17.8 %copy-start.4 = (s32[8,16,1024]{2,1,0:T(8,128)S(1)}, s32[8,16,1024]{2,1,0:T(8,128)}, u32[]{:S(2)}) copy-start(s32[8,16,1024]{2,1,0:T(8,128)} %get-tuple-element.320) | copy-start | bytes 1572868
  157.2 152.6 %all-to-all-start = ((f32[16,64,128]{2,1,0:T(8,128)}), f32[16,64,128]{2,1,0:T(8,128)}, u32[]{:S(2)}, u32[]{:S(2)}) async-start(f32[16,64,128]{2,1,0:T(8,128)} %bitcast.34), calls=%async_computation | async-start | bytes 1048576 | tf_op jit(solution)/shard_map/all_to_all | solution.py:23
  266.9 29.6 %copy-start.11 = (s32[1024,1]{0,1:T(1,128)S(1)}, s32[1024,1]{0,1:T(1,128)}, u32[]{:S(2)}) copy-start(s32[1024,1]{0,1:T(1,128)} %get-tuple-element.326) | copy-start | bytes 12292
  296.5 12.3 %copy-start.7 = (bf16[64,128]{1,0:T(8,128)(2,1)S(1)}, bf16[64,128]{1,0:T(8,128)(2,1)}, u32[]{:S(2)}) copy-start(bf16[64,128]{1,0:T(8,128)(2,1)} %param.21) | copy-start | bytes 49156
  302.1 16.4 %copy-start.15 = (bf16[2,64,128]{2,1,0:T(8,128)(2,1)S(1)}, bf16[2,64,128]{2,1,0:T(8,128)(2,1)}, u32[]{:S(2)}) copy-start(bf16[2,64,128]{2,1,0:T(8,128)(2,1)} %param.29) | copy-start | bytes 98308
  302.1 16.4 %copy-start.17 = (bf16[1024,128]{1,0:T(8,128)(2,1)S(1)}, bf16[1024,128]{1,0:T(8,128)(2,1)}, u32[]{:S(2)}) copy-start(bf16[1024,128]{1,0:T(8,128)(2,1)} %param.23) | copy-start | bytes 786436
  309.8 22.8 %all-to-all-start.2 = ((f32[16,64,128]{2,1,0:T(8,128)}), f32[16,64,128]{2,1,0:T(8,128)S(1)}, u32[]{:S(2)}, u32[]{:S(2)}) async-start(f32[16,64,128]{2,1,0:T(8,128)} %bitcast.48), calls=%async_computation.2 | async-start | bytes 1048576 | tf_op jit(solution)/shard_map/all_to_all | solution.py:23
  333.3 14.1 %all-to-all-start.1 = ((bf16[16,64,128]{2,1,0:T(8,128)(2,1)}), bf16[16,64,128]{2,1,0:T(8,128)(2,1)}, u32[]{:S(2)}, u32[]{:S(2)}) async-start(bf16[16,64,128]{2,1,0:T(8,128)(2,1)} %broadcast_in_dim.18), calls=%async_computation.1 | async-start | bytes 524288 | tf_op jit(solution)/shard_map/all_to_all | solution.py:35
  337.8 264.9 %all-reduce.2.cloned.1.call-start = ((), (), s32[]{:S(2)}) async-start(), calls=%async_computation.5 | async-start | bytes 2097152 | tf_op jit(solution)/shard_map/psum | solution.py:44
  339.3 17.0 %copy-start.8 = (bf16[64,128]{1,0:T(8,128)(2,1)S(1)}, bf16[64,128]{1,0:T(8,128)(2,1)}, u32[]{:S(2)}) copy-start(bf16[64,128]{1,0:T(8,128)(2,1)} %param.21) | copy-start | bytes 49156
  348.2 74.4 %all-to-all-start.3 = ((bf16[16,64,128]{2,1,0:T(8,128)(2,1)}), bf16[16,64,128]{2,1,0:T(8,128)(2,1)}, u32[]{:S(2)}, u32[]{:S(2)}) async-start(bf16[16,64,128]{2,1,0:T(8,128)(2,1)} %broadcast_in_dim.20), calls=%async_computation.3 | async-start | bytes 524288 | tf_op jit(solution)/shard_map/all_to_all | solution.py:35
  356.2 2.3 copy-start.1
  403.9 4.9 copy-start.14
  418.3 3.8 copy-start.2
  418.3 7.9 %copy-start.9 = (bf16[64,128]{1,0:T(8,128)(2,1)S(1)}, bf16[64,128]{1,0:T(8,128)(2,1)}, u32[]{:S(2)}) copy-start(bf16[64,128]{1,0:T(8,128)(2,1)} %param.21) | copy-start | bytes 49156
  428.8 176.8 %all-to-all-start.4 = ((f32[16,1,16384]{2,1,0:T(1,128)}), f32[16,1,16384]{2,1,0:T(1,128)}, u32[]{:S(2)}, u32[]{:S(2)}) async-start(f32[16,1,16384]{2,1,0:T(1,128)} %broadcast_in_dim.21), calls=%async_computation.4 | async-start | bytes 2097152 | tf_op jit(solution)/shard_map/all_to_all | solution.py:35
  480.7 4.0 copy-start.12
Sparse Core Ops, SparseCore 0:
  344.0 258.5 all-reduce.1
where the time goes:
time: 619 us; the launch traced here: 615 us
  other arithmetic  261 us (42%)
  waiting for transfers between devices  124 us (20%)
  local copies, waits for them, and re-layouts  88.5 us (14%)
  matrix products  61.5 us (10%)
  starting transfers between devices  36.5 us (6%)
  loops' own time  28.9 us (5%)
  between operations  14.6 us (2%)
    reduce_sum x2, other arithmetic, adjacency(): hits = jnp.sum(matches, axis=1)  161 us
    psum x1, waiting for transfers between devices, in_one(): running = lax.psum(line, axis)  105 us
    scatter-add x8, other arithmetic, spread_tile(): return (carried.at[:, picked].add(spread), None)  34 us
    dot_general x8, matrix products, aggregate_tile(): jnp.einsum('kds,cks->dc', counts, pieces, preferred_element_type=jnp.floa...  28.7 us
    convert_element_type x2, other arithmetic, adjacency(): return (hits * valid_micro[:, :, None]).astype(jnp.bfloat16)  24.9 us
    dot_general x8, matrix products, spread_tile(): jnp.einsum('kds,dc->cks', counts, back_tile, preferred_element_type=jnp.f...  24.4 us
    scatter-add x2, other arithmetic, local(): table_grad.reshape(columns, source_total).at[:, dest_rows[micro_index]]  19.1 us
    all_to_all x3, starting transfers between devices, copy_for_each(): lax.all_to_all(jnp.broadcast_to(x[None], (devices, *x.shape)), axis, 0, 0...  18.9 us
  transfers between devices with their start and end apart: 6, of which 3 were waited for; matrix products, arithmetic and copies ran while one was open for 43% of the time, Pallas kernels for 0%

commit v1 on v0

v1 whole, which is shorter than its diff:
```python
import functools
import math

import jax
import jax.numpy as jnp
from jax import lax
from jax.experimental import pallas as pl
from jax.experimental.pallas import tpu as pltpu
from jax.sharding import PartitionSpec as P

H = 128
TD = 256
TS = 1024
K = 8
NB = 16
CS = 64


def gelu_slope(values):
    result, pullback = jax.vjp(jax.nn.gelu, values)
    return (result, pullback(jnp.ones_like(values))[0])


def mlp_pass(hidden, target, up_weight, down_weight):
    first_value, first_slope = gelu_slope(hidden)
    first_act = first_value.astype(jnp.bfloat16)
    inner_pre = jnp.dot(first_act, up_weight, preferred_element_type=jnp.float32)
    inner_value, inner_slope = gelu_slope(inner_pre)
    inner_act = inner_value.astype(jnp.bfloat16)
    down_part = jnp.dot(inner_act.T, target, preferred_element_type=jnp.float32)
    inner_grad = (
        jnp.dot(target, down_weight.T, preferred_element_type=jnp.float32) * inner_slope
    ).astype(jnp.bfloat16)
    up_part = jnp.dot(first_act.T, inner_grad, preferred_element_type=jnp.float32)
    hidden_grad = (
        jnp.dot(inner_grad, up_weight.T, preferred_element_type=jnp.float32) * first_slope
    ).astype(jnp.bfloat16)
    return (hidden_grad, up_part, down_part)


def agg_kernel(agg_scale, k_total, nt, tiles_ref, emb_ref, rows_ref, mask_ref, counts_ref, agg_ref, acc_ref):
    k = pl.program_id(2)

    @pl.when(k == 0)
    def _():
        acc_ref[...] = jnp.zeros_like(acc_ref)

    msk = mask_ref[0, 0]

    def chunk(c, carry):
        start = pl.multiple_of(c * CS, CS)
        iota = lax.broadcasted_iota(jnp.int32, (CS, TD), 0) + start
        cnt = jnp.zeros((CS, TD), jnp.int32)
        for j in range(NB):
            cnt = cnt + (rows_ref[0, 0, j : j + 1, :] == iota).astype(jnp.int32)
        counts_ref[0, 0, 0, pl.ds(start, CS), :] = (cnt * msk).astype(jnp.bfloat16)
        return carry

    lax.fori_loop(0, TS // CS, chunk, 0)
    acc_ref[...] += jnp.dot(emb_ref[...], counts_ref[0, 0, 0], preferred_element_type=jnp.float32)

    @pl.when(k == k_total - 1)
    def _():
        agg_ref[0] = (acc_ref[...] * agg_scale).astype(jnp.bfloat16)


def aggregate(embedding, tiles_flat, neighbor_rows, slot_mask, agg_scale):
    columns = embedding.shape[0]
    micro_total, k_total, nb, dest_total = neighbor_rows.shape
    nt = dest_total // TD
    mask4 = slot_mask.reshape(micro_total, k_total, 1, dest_total)
    grid_spec = pltpu.PrefetchScalarGridSpec(
        num_scalar_prefetch=1,
        grid=(micro_total, nt, k_total),
        in_specs=[
            pl.BlockSpec((columns, TS), lambda m, t, k, tiles: (0, tiles[(m * k_total + k) * nt + t])),
            pl.BlockSpec((1, 1, nb, TD), lambda m, t, k, tiles: (m, k, 0, t)),
            pl.BlockSpec((1, 1, 1, TD), lambda m, t, k, tiles: (m, k, 0, t)),
        ],
        out_specs=[
            pl.BlockSpec((1, 1, 1, TS, TD), lambda m, t, k, tiles: (m, k, t, 0, 0)),
            pl.BlockSpec((1, columns, TD), lambda m, t, k, tiles: (m, 0, t)),
        ],
        scratch_shapes=[pltpu.VMEM((columns, TD), jnp.float32)],
    )
    return pl.pallas_call(
        functools.partial(agg_kernel, agg_scale, k_total, nt),
        grid_spec=grid_spec,
        out_shape=[
            jax.ShapeDtypeStruct((micro_total, k_total, nt, TS, TD), jnp.bfloat16),
            jax.ShapeDtypeStruct((micro_total, columns, dest_total), jnp.bfloat16),
        ],
        compiler_params=pltpu.CompilerParams(
            dimension_semantics=("arbitrary", "arbitrary", "arbitrary")
        ),
    )(tiles_flat, embedding, neighbor_rows, mask4)


def spread_kernel(agg_scale, k_total, nt, tiles_ref, counts_ref, back_ref, tg_ref):
    m = pl.program_id(0)
    t = pl.program_id(1)
    k = pl.program_id(2)

    @pl.when((m == 0) & (t == 0) & (k == 0))
    def _():
        tg_ref[...] = jnp.zeros_like(tg_ref)

    tile = tiles_ref[(m * k_total + k) * nt + t]
    start = pl.multiple_of(tile * TS, TS)
    part = jnp.dot(counts_ref[0, 0, 0], back_ref[0], preferred_element_type=jnp.float32)
    tg_ref[pl.ds(start, TS), :] += part * agg_scale


def spread(counts, back, tiles_flat, source_total, agg_scale):
    micro_total, k_total, nt = counts.shape[:3]
    columns = back.shape[2]
    grid_spec = pltpu.PrefetchScalarGridSpec(
        num_scalar_prefetch=1,
        grid=(micro_total, nt, k_total),
        in_specs=[
            pl.BlockSpec((1, 1, 1, TS, TD), lambda m, t, k, tiles: (m, k, t, 0, 0)),
            pl.BlockSpec((1, TD, columns), lambda m, t, k, tiles: (m, t, 0)),
        ],
        out_specs=pl.BlockSpec((source_total, columns), lambda m, t, k, tiles: (0, 0)),
    )
    return pl.pallas_call(
        functools.partial(spread_kernel, agg_scale, k_total, nt),
        grid_spec=grid_spec,
        out_shape=jax.ShapeDtypeStruct((source_total, columns), jnp.float32),
        compiler_params=pltpu.CompilerParams(
            dimension_semantics=("arbitrary", "arbitrary", "arbitrary"),
            vmem_limit_bytes=48 * 1024 * 1024,
        ),
    )(tiles_flat, counts, back)


def local(
    embedding,
    self_weight,
    neighbor_weight,
    up_weight,
    down_weight,
    source_tiles,
    neighbor_rows,
    slot_mask,
    dest_rows,
    owner_order,
    output_grad,
):
    batch_total = lax.axis_size("batch")
    columns, source_total = embedding.shape
    micro_total = source_tiles.shape[0]
    dest_total = dest_rows.shape[1]
    agg_scale = 1.0 / math.sqrt(K * NB)
    norm_factor = 1.0 / math.sqrt(micro_total * dest_total * batch_total)
    tiles_flat = source_tiles.reshape(-1)

    target_all = lax.all_gather(output_grad, "feat", axis=1, tiled=True)
    counts, agg_t = aggregate(embedding, tiles_flat, neighbor_rows, slot_mask, agg_scale)
    table = embedding.T
    own_all = [table[dest_rows[m]] for m in range(micro_total)]
    partial = jnp.stack(
        [
            jnp.dot(own_all[m], self_weight, preferred_element_type=jnp.float32)
            + lax.dot_general(
                agg_t[m], neighbor_weight, (((0,), (0,)), ((), ())),
                preferred_element_type=jnp.float32,
            )
            for m in range(micro_total)
        ]
    )
    hidden_all = lax.psum(partial, "feat")

    up_sum = jnp.zeros(up_weight.shape, jnp.float32)
    down_sum = jnp.zeros(down_weight.shape, jnp.float32)
    self_sum = jnp.zeros((columns, H), jnp.float32)
    neighbor_sum = jnp.zeros((columns, H), jnp.float32)
    backs = []
    own_grads = []
    for m in range(micro_total):
        row_order = owner_order[m, 0]
        target = jnp.zeros(target_all.shape[1:], target_all.dtype).at[row_order].set(target_all[m])
        hidden_grad, up_part, down_part = mlp_pass(hidden_all[m], target, up_weight, down_weight)
        up_sum = up_sum + up_part
        down_sum = down_sum + down_part
        self_sum = self_sum + jnp.dot(own_all[m].T, hidden_grad, preferred_element_type=jnp.float32)
        neighbor_sum = neighbor_sum + jnp.dot(agg_t[m], hidden_grad, preferred_element_type=jnp.float32)
        backs.append(
            jnp.dot(hidden_grad, neighbor_weight.T, preferred_element_type=jnp.float32).astype(jnp.bfloat16)
        )
        own_grads.append(jnp.dot(hidden_grad, self_weight.T, preferred_element_type=jnp.float32))

    sizes = [up_sum.size, down_sum.size, self_sum.size, neighbor_sum.size]
    line = jnp.concatenate([up_sum.ravel(), down_sum.ravel(), self_sum.ravel(), neighbor_sum.ravel()])
    line = lax.psum(line, "batch")
    ends = [0]
    for s in sizes:
        ends.append(ends[-1] + s)
    up_sum = line[ends[0] : ends[1]].reshape(up_weight.shape)
    down_sum = line[ends[1] : ends[2]].reshape(down_weight.shape)
    self_sum = line[ends[2] : ends[3]].reshape(columns, H)
    neighbor_sum = line[ends[3] : ends[4]].reshape(columns, H)

    table_grad = spread(jnp.asarray(counts), jnp.stack(backs), tiles_flat, source_total, agg_scale)
    for m in range(micro_total):
        table_grad = table_grad.at[dest_rows[m]].add(own_grads[m])
    return (
        table_grad.T,
        self_sum * norm_factor,
        neighbor_sum * norm_factor,
        up_sum * norm_factor,
        down_sum * norm_factor,
    )


def solution(mesh):
    in_specs = (
        P("feat", "batch"),
        P("feat", None),
        P("feat", None),
        P(),
        P(),
        P(None, None, "batch"),
        P(None, None, None, "batch"),
        P(None, None, "batch"),
        P(None, "batch"),
        P(None, "batch", None),
        P(None, ("batch", "feat"), None),
    )
    out_specs = (P("feat", "batch"), P("feat", None), P("feat", None), P(), P())
    return jax.shard_map(local, mesh=mesh, in_specs=in_specs, out_specs=out_specs, check_vma=False)
```

time: 619 us -> 482 us (0.78)
  other arithmetic: 261 us -> 25.6 us
  Pallas kernels: 0 us -> 185 us
  local copies, waits for them, and re-layouts: 88.5 us -> 24.7 us
  waiting for transfers between devices: 124 us -> 177 us
  matrix products: 61.5 us -> 19.2 us
  starting transfers between devices: 36.5 us -> 0.08 us
  blocking collectives: 0 us -> 35.3 us
  loops' own time: 28.9 us -> 0 us
    pallas_call x0 -> x2, Pallas kernels: none -> 185 us  [the longest x1 140 us: aggregate(): pl.pallas_call(functools.partial(agg_kernel, agg_scale, k_total, nt), gri...]
    reduce_sum x5 -> x0, other arithmetic: 164 us -> none  [the longest x2 161 us: adjacency(): hits = jnp.sum(matches, axis=1)]
    psum x1 -> x2, waiting for transfers between devices: 105 us -> 177 us  [the longest x1 93.1 us: local(): hidden_all = lax.psum(partial, 'feat')]
    dot_general x26 -> x10, matrix products: 57.8 us -> 3.95 us  [the longest x2 2.33 us: local(): lax.dot_general(agg_t[m], neighbor_weight, (((0,), (0,)), ((), ())), pref...]
    all_to_all x5 -> x0, starting transfers between devices: 36.5 us -> none  [the longest x3 18.9 us: copy_for_each(): lax.all_to_all(jnp.broadcast_to(x[None], (devices, *x.shape)), axis, 0, 0...]
    all_gather x0 -> x1, blocking collectives: none -> 35.3 us  [local(): target_all = lax.all_gather(output_grad, 'feat', axis=1, tiled=True)]
    scatter-add x10 -> x2, other arithmetic: 53.1 us -> 19.1 us  [local(): table_grad = table_grad.at[dest_rows[m]].add(own_grads[m])]
    another operation x4 -> x0, loops' own time: 28.9 us -> none  [the longest x2 14.5 us: local(): gathered = lax.map(aggregate_tile, tile_steps).reshape(dest_total, columns)]
  transfers between devices with their start and end apart: 6 -> 2, of which waited for: 3 -> 2; matrix products, arithmetic and copies ran while one was open for 43% -> 6% of each run, Pallas kernels for 0% -> 9%
where the time goes in v1:
time: 482 us; the launch traced here: 481 us
  Pallas kernels  185 us (38%)
  waiting for transfers between devices  177 us (37%)
  blocking collectives  35.3 us (7%)
  other arithmetic  25.6 us (5%)
  local copies, waits for them, and re-layouts  24.7 us (5%)
  matrix products  19.2 us (4%)
  between operations  14.4 us (3%)
    pallas_call x1, Pallas kernels, aggregate(): pl.pallas_call(functools.partial(agg_kernel, agg_scale, k_total, nt), gri...  140 us
    psum x1, waiting for transfers between devices, local(): hidden_all = lax.psum(partial, 'feat')  93.1 us
    psum x1, waiting for transfers between devices, local(): line = lax.psum(line, 'batch')  83.4 us
    pallas_call x1, Pallas kernels, spread(): pl.pallas_call(functools.partial(spread_kernel, agg_scale, k_total, nt),...  45.6 us
    all_gather x1, blocking collectives, local(): target_all = lax.all_gather(output_grad, 'feat', axis=1, tiled=True)  35.3 us
    scatter-add x2, other arithmetic, local(): table_grad = table_grad.at[dest_rows[m]].add(own_grads[m])  19.1 us
  transfers between devices with their start and end apart: 2, of which 2 were waited for; matrix products, arithmetic and copies ran while one was open for 6% of the time, Pallas kernels for 9%

profile of v1, /device:TPU:1, one launch (start us, length us, event | category | flops | bytes accessed | tf_op | source)
XLA Modules:
  0.0 481.0 jit_solution(2972222206599697273)
XLA Ops:
  7.2 0.8 copy.23
  8.6 0.8 compare_select_fusion.2
  9.5 1.5 reshape.185.mask_ref
  11.0 2.0 copy.24
  13.0 3.2 gather_fusion.1
  16.2 3.2 gather_fusion
  19.9 139.6 %shard_map.146 = (bf16[2,8,4,1024,256]{4,3,2,1,0:T(8,128)(2,1)}, bf16[2,64,1024]{2,1,0:T(8,128)(2,1)}) custom-call(s32[64]{0:T(128)} %reshape.184.tiles_ref, bf16[64,8192]{1,0:T(8,128)(2,1)} %emb_ref.1, s32[2,8,16,1024]{3,2,1,0:T(8,128)} %rows_ref.1, s32[2,8,1,1024]{3,2,1,0:T(1,128)} %reshape.185.mask_ref), custom_call_target="tpu_custom_call" | custom-call | tf_op jit(solution)/shard_map/pallas_call | solution.py:86
  159.5 1.2 fusion.20
  160.6 1.2 fusion.21
  161.8 1.0 pad_maximum_fusion.1
  163.0 35.3 %all_gather.3 = bf16[2,1024,128]{2,1,0:T(8,128)(2,1)S(1)} all-gather(bf16[2,64,128]{2,1,0:T(8,128)(2,1)S(1)} %copy-done.7), channel_id=1, replica_groups=mesh['batch'=16,'feat'=16] {'feat'}, dimensions={1}, use_global_device_ids=true | all-gather | bytes 557056 | tf_op jit(solution)/shard_map/all_gather | solution.py:158
  198.3 3.2 scatter_custom_fusion.1
  201.5 3.4 scatter_custom_fusion
  204.9 93.1 %all-reduce.3.cloned.1.call-done = f32[2,1024,128]{2,1,0:T(8,128)} async-done(((f32[2,1024,128]{2,1,0:T(8,128)}), f32[2,1024,128]{2,1,0:T(8,128)}) %all-reduce.3.cloned.1.call-update) | async-done | bytes 1048592 | tf_op jit(solution)/shard_map/psum | solution.py:172
  298.1 1.8 fusion.66
  299.8 1.7 fusion.16
  301.6 3.0 fusion.7
  304.6 0.8 fusion.23
  305.9 0.7 fusion.67
  306.6 3.0 fusion.15
  309.6 1.7 fusion.19
  311.3 0.8 fusion.24
  313.9 1.1 pad_maximum_fusion
  315.6 45.6 %shard_map.147 = f32[8192,64]{1,0:T(8,128)S(1)} custom-call(s32[64]{0:T(128)S(1)} %copy-done.2, bf16[2,8,4,1024,256]{4,3,2,1,0:T(8,128)(2,1)} %get-tuple-element.7.counts_ref, bf16[2,1024,64]{2,1,0:T(8,128)(2,1)S(1)} %pad_maximum_fusion.2.back_ref), custom_call_target="tpu_custom_call" | custom-call | tf_op jit(solution)/shard_map/pallas_call | solution.py:126
  361.2 1.9 copy-done.1
  363.4 9.5 %scatter_fusion = f32[8192,64]{1,0:T(8,128)} fusion(f32[8192,64]{1,0:T(8,128)} %copy-done.1, s32[1024]{0:T(1024)S(1)} %bitcast.124, f32[1024,64]{1,0:T(8,128)S(1)} %fusion.70), kind=kCustom, calls=%fused_computation.4 | custom fusion | flops 65536 | bytes 790528 | tf_op jit(solution)/shard_map/scatter-add | solution.py:206
  373.1 9.5 %scatter_fusion.1 = f32[8192,64]{1,0:T(8,128)} fusion(f32[8192,64]{1,0:T(8,128)} %scatter_fusion, s32[1024]{0:T(1024)S(1)} %bitcast.122, f32[1024,64]{1,0:T(8,128)S(1)} %fusion.71), kind=kCustom, calls=%fused_computation.5 | custom fusion | flops 65536 | bytes 790528 | tf_op jit(solution)/shard_map/scatter-add | solution.py:206
  382.6 3.8 copy.29
  386.4 83.4 %all-reduce.5.cloned.1.call-done = f32[278528]{0:T(1024)} async-done(((f32[278528]{0:T(1024)}), f32[278528]{0:T(1024)}) %all-reduce.5.cloned.1.call-update) | async-done | bytes 1114128 | tf_op jit(solution)/shard_map/psum | solution.py:195
  469.8 2.1 fusion.41
  471.9 0.9 mul.232
  472.8 1.4 fusion.55
  (41 shorter events, 4.3 us)
Async XLA Ops:
  7.2 290.9 %copy-start = (bf16[128,1024]{1,0:T(8,128)(2,1)S(1)}, bf16[128,1024]{1,0:T(8,128)(2,1)}, u32[]{:S(2)}) copy-start(bf16[128,1024]{1,0:T(8,128)(2,1)} %param.14) | copy-start | bytes 786436
  7.2 12.3 %copy-start.6 = (bf16[64,128]{1,0:T(8,128)(2,1)S(1)}, bf16[64,128]{1,0:T(8,128)(2,1)}, u32[]{:S(2)}) copy-start(bf16[64,128]{1,0:T(8,128)(2,1)} %param.12) | copy-start | bytes 49156
  7.2 290.9 %all-reduce.3.cloned.1.call-start = ((), (), s32[]{:S(2)}) async-start(), calls=%async_computation | async-start | bytes 2097152 | tf_op jit(solution)/shard_map/psum | solution.py:172
  13.0 146.5 %copy-start.5 = (bf16[64,128]{1,0:T(8,128)(2,1)S(1)}, bf16[64,128]{1,0:T(8,128)(2,1)}, u32[]{:S(2)}) copy-start(bf16[64,128]{1,0:T(8,128)(2,1)} %param.13) | copy-start | bytes 49156
  19.7 143.3 %copy-start.8 = (s32[2,1,1024]{2,1,0:T(1,128)S(1)}, s32[2,1,1024]{2,1,0:T(1,128)}, u32[]{:S(2)}) copy-start(s32[2,1,1024]{2,1,0:T(1,128)} %param.20) | copy-start | bytes 24580
  19.7 143.3 %copy-start.7 = (bf16[2,64,128]{2,1,0:T(8,128)(2,1)S(1)}, bf16[2,64,128]{2,1,0:T(8,128)(2,1)}, u32[]{:S(2)}) copy-start(bf16[2,64,128]{2,1,0:T(8,128)(2,1)} %param.21) | copy-start | bytes 98308
  162.9 306.9 %all-reduce.5.cloned.1.call-start = ((), (), s32[]{:S(2)}) async-start(), calls=%async_computation.1 | async-start | bytes 2228224 | tf_op jit(solution)/shard_map/psum | solution.py:195
  299.8 1.7 copy-start.9
  301.6 3.0 copy-start.3
  304.6 1.1 copy-start.4
  313.2 2.4 copy-start.2
  361.2 1.9 copy-start.1
Sparse Core Ops, SparseCore 0:
  163.0 135.0 all-reduce.2
  315.2 154.5 all-reduce.4

commit v2 on v1

--- a/solution.py
+++ b/solution.py
@@ -36,6 +36,22 @@
         jnp.dot(inner_grad, up_weight.T, preferred_element_type=jnp.float32) * first_slope
     ).astype(jnp.bfloat16)
     return (hidden_grad, up_part, down_part)
+
+
+def summed_over(x, axis):
+    n = lax.axis_size(axis)
+    flat = x.reshape(n, -1)
+    mine = lax.all_to_all(flat, axis, 0, 0, tiled=True).reshape(n, -1).sum(axis=0)
+    spread_back = lax.all_to_all(jnp.broadcast_to(mine[None], (n, mine.size)), axis, 0, 0, tiled=True)
+    return spread_back.reshape(x.shape)
+
+
+def gathered_over(x, axis, dim):
+    n = lax.axis_size(axis)
+    pieces = lax.all_to_all(jnp.broadcast_to(x[None], (n, *x.shape)), axis, 0, 0, tiled=True)
+    pieces = jnp.moveaxis(pieces, 0, dim)
+    shape = pieces.shape
+    return pieces.reshape(*shape[:dim], shape[dim] * shape[dim + 1], *shape[dim + 2 :])
 
 
 def agg_kernel(agg_scale, k_total, nt, tiles_ref, emb_ref, rows_ref, mask_ref, counts_ref, agg_ref, acc_ref):
@@ -155,7 +171,7 @@
     norm_factor = 1.0 / math.sqrt(micro_total * dest_total * batch_total)
     tiles_flat = source_tiles.reshape(-1)
 
-    target_all = lax.all_gather(output_grad, "feat", axis=1, tiled=True)
+    target_all = gathered_over(output_grad, "feat", 1)
     counts, agg_t = aggregate(embedding, tiles_flat, neighbor_rows, slot_mask, agg_scale)
     table = embedding.T
     own_all = [table[dest_rows[m]] for m in range(micro_total)]
@@ -169,7 +185,7 @@
             for m in range(micro_total)
         ]
     )
-    hidden_all = lax.psum(partial, "feat")
+    hidden_all = summed_over(partial, "feat")
 
     up_sum = jnp.zeros(up_weight.shape, jnp.float32)
     down_sum = jnp.zeros(down_weight.shape, jnp.float32)
@@ -192,7 +208,7 @@
 
     sizes = [up_sum.size, down_sum.size, self_sum.size, neighbor_sum.size]
     line = jnp.concatenate([up_sum.ravel(), down_sum.ravel(), self_sum.ravel(), neighbor_sum.ravel()])
-    line = lax.psum(line, "batch")
+    line = summed_over(line, "batch")
     ends = [0]
     for s in sizes:
         ends.append(ends[-1] + s)

time: 482 us -> 373 us (0.77)
  waiting for transfers between devices: 177 us -> 32.3 us
  blocking collectives: 35.3 us -> 67 us
  between operations: 14.4 us -> 1.06 us
  starting transfers between devices: 0.08 us -> 13 us
    psum x2 -> x0, waiting for transfers between devices: 177 us -> none  [the longest x1 93.1 us: local(): hidden_all = lax.psum(partial, 'feat')]
    all_to_all x0 -> x2, blocking collectives: none -> 67 us  [summed_over(): lax.all_to_all(flat, axis, 0, 0, tiled=True).reshape(n, -1).sum(axis=0)]
    all_gather x1 -> x0, blocking collectives: 35.3 us -> none  [local(): target_all = lax.all_gather(output_grad, 'feat', axis=1, tiled=True)]
    all_to_all x0 -> x3, waiting for transfers between devices: none -> 32.3 us  [the longest x2 17.7 us: summed_over(): lax.all_to_all(jnp.broadcast_to(mine[None], (n, mine.size)), axis, 0, 0,...]
    all_to_all x0 -> x3, starting transfers between devices: none -> 13 us  [the longest x2 8.31 us: summed_over(): lax.all_to_all(jnp.broadcast_to(mine[None], (n, mine.size)), axis, 0, 0,...]
  transfers between devices with their start and end apart: 2 -> 3, of which waited for: 2 -> 2; matrix products, arithmetic and copies ran while one was open for 6% -> 8% of each run, Pallas kernels for 9% -> 12%
where the time goes in v2:
time: 373 us; the launch traced here: 372 us
  Pallas kernels  185 us (50%)
  blocking collectives  67 us (18%)
  waiting for transfers between devices  32.3 us (9%)
  local copies, waits for them, and re-layouts  28.4 us (8%)
  other arithmetic  26.5 us (7%)
  matrix products  18.1 us (5%)
  starting transfers between devices  13 us (3%)
    pallas_call x1, Pallas kernels, aggregate(): pl.pallas_call(functools.partial(agg_kernel, agg_scale, k_total, nt), gri...  140 us
    all_to_all x2, blocking collectives, summed_over(): lax.all_to_all(flat, axis, 0, 0, tiled=True).reshape(n, -1).sum(axis=0)  67 us
    pallas_call x1, Pallas kernels, spread(): pl.pallas_call(functools.partial(spread_kernel, agg_scale, k_total, nt),...  45.6 us
    scatter-add x2, other arithmetic, local(): table_grad = table_grad.at[dest_rows[m]].add(own_grads[m])  19.1 us
    all_to_all x2, waiting for transfers between devices, summed_over(): lax.all_to_all(jnp.broadcast_to(mine[None], (n, mine.size)), axis, 0, 0,...  17.7 us
    all_to_all x1, waiting for transfers between devices, gathered_over(): lax.all_to_all(jnp.broadcast_to(x[None], (n, *x.shape)), axis, 0, 0, tile...  14.6 us
    unnamed x24, local copies, waits for them, and re-layouts  8.75 us
    all_to_all x2, starting transfers between devices, summed_over(): lax.all_to_all(jnp.broadcast_to(mine[None], (n, mine.size)), axis, 0, 0,...  8.31 us
  transfers between devices with their start and end apart: 3, of which 2 were waited for; matrix products, arithmetic and copies ran while one was open for 8% of the time, Pallas kernels for 12%

profile of v2, /device:TPU:1, one launch (start us, length us, event | category | flops | bytes accessed | tf_op | source)
XLA Modules:
  0.0 371.6 jit_solution(9694740480527181086)
XLA Ops:
  2.9 1.5 reshape.190.mask_ref
  4.4 2.0 copy.47
  6.4 3.2 gather_fusion.1
  9.7 3.2 gather_fusion
  13.3 139.7 %shard_map.146 = (bf16[2,8,4,1024,256]{4,3,2,1,0:T(8,128)(2,1)}, bf16[2,64,1024]{2,1,0:T(8,128)(2,1)}) custom-call(s32[64]{0:T(128)} %reshape.189.tiles_ref, bf16[64,8192]{1,0:T(8,128)(2,1)} %emb_ref.1, s32[2,8,16,1024]{3,2,1,0:T(8,128)} %rows_ref.1, s32[2,8,1,1024]{3,2,1,0:T(1,128)} %reshape.190.mask_ref), custom_call_target="tpu_custom_call" | custom-call | tf_op jit(solution)/shard_map/pallas_call | solution.py:102
  153.0 1.2 fusion.20
  154.2 1.2 fusion.21
  155.5 36.8 %all_to_all.35 = f32[16,1,16384]{2,1,0:T(1,128)S(1)} all-to-all(f32[16,1,16384]{2,1,0:T(1,128)S(1)} %bitcast.97), channel_id=1, replica_groups=mesh['batch'=16,'feat'=16] {'feat'}, dimensions={0} | all-to-all | bytes 2097152 | tf_op jit(solution)/shard_map/all_to_all | solution.py:44
  192.3 0.9 broadcast_in_dim.6
  193.2 4.7 %all-to-all-start = ((bf16[16,2,64,128]{3,2,1,0:T(8,128)(2,1)}), bf16[16,2,64,128]{3,2,1,0:T(8,128)(2,1)S(1)}, u32[]{:S(2)}, u32[]{:S(2)}) async-start(bf16[16,2,64,128]{3,2,1,0:T(8,128)(2,1)} %broadcast_in_dim.6), calls=%async_computation | async-start | bytes 1048576 | tf_op jit(solution)/shard_map/all_to_all | solution.py:51
  198.6 14.6 %all-to-all-done = bf16[16,2,64,128]{3,2,1,0:T(8,128)(2,1)S(1)} async-done(((bf16[16,2,64,128]{3,2,1,0:T(8,128)(2,1)}), bf16[16,2,64,128]{3,2,1,0:T(8,128)(2,1)S(1)}, u32[]{:S(2)}, u32[]{:S(2)}) %all-to-all-start) | async-done | bytes 524320 | tf_op jit(solution)/shard_map/all_to_all | solution.py:51
  213.2 1.8 broadcast_in_dim.7
  214.9 4.4 %all-to-all-start.2 = ((f32[16,1,16384]{2,1,0:T(1,128)}), f32[16,1,16384]{2,1,0:T(1,128)S(1)}, u32[]{:S(2)}, u32[]{:S(2)}) async-start(f32[16,1,16384]{2,1,0:T(1,128)} %broadcast_in_dim.7), calls=%async_computation.2 | async-start | bytes 2097152 | tf_op jit(solution)/shard_map/all_to_all | solution.py:45
  219.4 3.2 scatter_custom_fusion
  222.6 3.4 scatter_custom_fusion.1
  226.1 17.7 %all-to-all-done.2 = f32[16,1,16384]{2,1,0:T(1,128)S(1)} async-done(((f32[16,1,16384]{2,1,0:T(1,128)}), f32[16,1,16384]{2,1,0:T(1,128)S(1)}, u32[]{:S(2)}, u32[]{:S(2)}) %all-to-all-start.2) | async-done | bytes 1048608 | tf_op jit(solution)/shard_map/all_to_all | solution.py:45
  244.5 1.7 fusion.16
  246.3 3.0 fusion.7
  251.9 3.0 fusion.15
  254.9 0.8 fusion.24
  255.7 1.7 fusion.19
  258.7 30.2 %all_to_all.36 = f32[16,1,17408]{2,1,0:T(1,128)S(1)} all-to-all(f32[16,1,17408]{2,1,0:T(1,128)S(1)} %bitcast.96), channel_id=1, replica_groups=mesh['batch'=16,'feat'=16] {'batch'}, dimensions={0} | all-to-all | bytes 2228224 | tf_op jit(solution)/shard_map/all_to_all | solution.py:44
  289.6 1.6 broadcast_in_dim.8
  291.2 3.9 %all-to-all-start.4 = ((f32[16,1,17408]{2,1,0:T(1,128)}), f32[16,1,17408]{2,1,0:T(1,128)S(1)}, u32[]{:S(2)}, u32[]{:S(2)}) async-start(f32[16,1,17408]{2,1,0:T(1,128)} %broadcast_in_dim.8), calls=%async_computation.4 | async-start | bytes 2228224 | tf_op jit(solution)/shard_map/all_to_all | solution.py:45
  295.7 45.6 %shard_map.147 = f32[8192,64]{1,0:T(8,128)S(1)} custom-call(s32[64]{0:T(128)S(1)} %copy-done.3, bf16[2,8,4,1024,256]{4,3,2,1,0:T(8,128)(2,1)} %get-tuple-element.7.counts_ref, bf16[2,1024,64]{2,1,0:T(8,128)(2,1)S(1)} %pad_maximum_fusion.2.back_ref), custom_call_target="tpu_custom_call" | custom-call | tf_op jit(solution)/shard_map/pallas_call | solution.py:142
  341.3 1.9 copy-done.2
  343.4 9.5 %scatter_fusion = f32[8192,64]{1,0:T(8,128)} fusion(f32[8192,64]{1,0:T(8,128)} %copy-done.2, s32[1024]{0:T(1024)S(1)} %bitcast.105, f32[1024,64]{1,0:T(8,128)S(1)} %fusion.69), kind=kCustom, calls=%fused_computation.4 | custom fusion | flops 65536 | bytes 790528 | tf_op jit(solution)/shard_map/scatter-add | solution.py:222
  353.1 9.5 %scatter_fusion.1 = f32[8192,64]{1,0:T(8,128)} fusion(f32[8192,64]{1,0:T(8,128)} %scatter_fusion, s32[1024]{0:T(1024)S(1)} %bitcast.103, f32[1024,64]{1,0:T(8,128)S(1)} %fusion.70), kind=kCustom, calls=%fused_computation.5 | custom fusion | flops 65536 | bytes 790528 | tf_op jit(solution)/shard_map/scatter-add | solution.py:222
  362.7 3.8 %copy.54 = f32[64,8192]{1,0:T(8,128)} copy(f32[64,8192]{0,1:T(8,128)} %bitcast.85) | data formatting | bytes 4194304
  367.2 0.8 slice_multiply_fusion
  368.0 2.6 reduce.2
  370.8 0.8 slice_multiply_fusion.1
  (51 shorter events, 10.4 us)
Async XLA Ops:
  0.6 243.2 %copy-start = (bf16[128,1024]{1,0:T(8,128)(2,1)S(1)}, bf16[128,1024]{1,0:T(8,128)(2,1)}, u32[]{:S(2)}) copy-start(bf16[128,1024]{1,0:T(8,128)(2,1)} %param.14) | copy-start | bytes 786436
  0.6 12.2 %copy-start.6 = (bf16[64,128]{1,0:T(8,128)(2,1)S(1)}, bf16[64,128]{1,0:T(8,128)(2,1)}, u32[]{:S(2)}) copy-start(bf16[64,128]{1,0:T(8,128)(2,1)} %param.12) | copy-start | bytes 49156
  6.4 146.6 %copy-start.5 = (bf16[64,128]{1,0:T(8,128)(2,1)S(1)}, bf16[64,128]{1,0:T(8,128)(2,1)}, u32[]{:S(2)}) copy-start(bf16[64,128]{1,0:T(8,128)(2,1)} %param.13) | copy-start | bytes 49156
  13.3 179.0 %copy-start.7 = (bf16[2,64,128]{2,1,0:T(8,128)(2,1)S(1)}, bf16[2,64,128]{2,1,0:T(8,128)(2,1)}, u32[]{:S(2)}) copy-start(bf16[2,64,128]{2,1,0:T(8,128)(2,1)} %param.21) | copy-start | bytes 98308
  155.4 63.9 %copy-start.8 = (s32[2,1,1024]{2,1,0:T(1,128)S(1)}, s32[2,1,1024]{2,1,0:T(1,128)}, u32[]{:S(2)}) copy-start(s32[2,1,1024]{2,1,0:T(1,128)} %param.20) | copy-start | bytes 24580
  193.2 20.0 %all-to-all-start = ((bf16[16,2,64,128]{3,2,1,0:T(8,128)(2,1)}), bf16[16,2,64,128]{3,2,1,0:T(8,128)(2,1)S(1)}, u32[]{:S(2)}, u32[]{:S(2)}) async-start(bf16[16,2,64,128]{3,2,1,0:T(8,128)(2,1)} %broadcast_in_dim.6), calls=%async_computation | async-start | bytes 1048576 | tf_op jit(solution)/shard_map/all_to_all | solution.py:51
  214.9 28.8 %all-to-all-start.2 = ((f32[16,1,16384]{2,1,0:T(1,128)}), f32[16,1,16384]{2,1,0:T(1,128)S(1)}, u32[]{:S(2)}, u32[]{:S(2)}) async-start(f32[16,1,16384]{2,1,0:T(1,128)} %broadcast_in_dim.7), calls=%async_computation.2 | async-start | bytes 2097152 | tf_op jit(solution)/shard_map/all_to_all | solution.py:45
  244.5 1.7 copy-start.9
  249.3 1.7 copy-start.4
  258.7 37.0 %copy-start.3 = (s32[64]{0:T(128)S(1)}, s32[64]{0:T(128)}, u32[]{:S(2)}) copy-start(s32[64]{0:T(128)} %reshape.189.tiles_ref) | copy-start | bytes 772
  291.2 75.3 %all-to-all-start.4 = ((f32[16,1,17408]{2,1,0:T(1,128)}), f32[16,1,17408]{2,1,0:T(1,128)S(1)}, u32[]{:S(2)}, u32[]{:S(2)}) async-start(f32[16,1,17408]{2,1,0:T(1,128)} %broadcast_in_dim.8), calls=%async_computation.4 | async-start | bytes 2228224 | tf_op jit(solution)/shard_map/all_to_all | solution.py:45
  341.2 1.9 copy-start.2
  362.7 9.0 %copy-start.1 = (bf16[128,1024]{1,0:T(8,128)(2,1)S(1)}, bf16[128,1024]{1,0:T(8,128)(2,1)}, u32[]{:S(2)}) copy-start(bf16[128,1024]{1,0:T(8,128)(2,1)} %param.14) | copy-start | bytes 786436

commit v3 on v2

v3 whole, which is shorter than its diff:
```python
import functools
import math

import jax
import jax.numpy as jnp
from jax import lax
from jax.experimental import pallas as pl
from jax.experimental.pallas import tpu as pltpu
from jax.sharding import PartitionSpec as P

H = 128
TD = 256
TS = 1024
K = 8
NB = 16
CS = 128


def gelu_slope(values):
    result, pullback = jax.vjp(jax.nn.gelu, values)
    return (result, pullback(jnp.ones_like(values))[0])


def mlp_pass(hidden, target, up_weight, down_weight):
    first_value, first_slope = gelu_slope(hidden)
    first_act = first_value.astype(jnp.bfloat16)
    inner_pre = jnp.dot(first_act, up_weight, preferred_element_type=jnp.float32)
    inner_value, inner_slope = gelu_slope(inner_pre)
    inner_act = inner_value.astype(jnp.bfloat16)
    down_part = jnp.dot(inner_act.T, target, preferred_element_type=jnp.float32)
    inner_grad = (
        jnp.dot(target, down_weight.T, preferred_element_type=jnp.float32) * inner_slope
    ).astype(jnp.bfloat16)
    up_part = jnp.dot(first_act.T, inner_grad, preferred_element_type=jnp.float32)
    hidden_grad = (
        jnp.dot(inner_grad, up_weight.T, preferred_element_type=jnp.float32) * first_slope
    ).astype(jnp.bfloat16)
    return (hidden_grad, up_part, down_part)


def summed_over(x, axis):
    n = lax.axis_size(axis)
    flat = x.reshape(n, -1)
    mine = lax.all_to_all(flat, axis, 0, 0, tiled=True).reshape(n, -1).sum(axis=0)
    spread_back = lax.all_to_all(jnp.broadcast_to(mine[None], (n, mine.size)), axis, 0, 0, tiled=True)
    return spread_back.reshape(x.shape)


def gathered_over(x, axis, dim):
    n = lax.axis_size(axis)
    pieces = lax.all_to_all(jnp.broadcast_to(x[None], (n, *x.shape)), axis, 0, 0, tiled=True)
    pieces = jnp.moveaxis(pieces, 0, dim)
    shape = pieces.shape
    return pieces.reshape(*shape[:dim], shape[dim] * shape[dim + 1], *shape[dim + 2 :])


def agg_kernel(agg_scale, k_total, nt, tiles_ref, emb_ref, rows_ref, mask_ref, counts_ref, agg_ref, acc_ref):
    k = pl.program_id(1)

    @pl.when(k == 0)
    def _():
        acc_ref[...] = jnp.zeros_like(acc_ref)

    msk = mask_ref[0, 0].astype(jnp.bfloat16)
    rows = rows_ref[0, 0]
    local_iota = lax.broadcasted_iota(jnp.int32, (CS, TD), 0).astype(jnp.bfloat16)
    one = jnp.ones((CS, TD), jnp.bfloat16)
    zero = jnp.zeros((CS, TD), jnp.bfloat16)

    def chunk(c, carry):
        start = pl.multiple_of(c * CS, CS)
        local = (rows - start).astype(jnp.float32)
        cnt = zero
        for j in range(NB):
            here = local[j : j + 1, :].astype(jnp.bfloat16)
            cnt = cnt + jnp.where(here == local_iota, one, zero)
        counts_ref[0, 0, pl.ds(start, CS), :] = cnt * msk
        return carry

    lax.fori_loop(0, TS // CS, chunk, 0)
    acc_ref[...] += jnp.dot(emb_ref[...], counts_ref[0, 0], preferred_element_type=jnp.float32)

    @pl.when(k == k_total - 1)
    def _():
        agg_ref[...] = (acc_ref[...] * agg_scale).astype(jnp.bfloat16)


def aggregate(embedding, tiles_flat, neighbor_rows, slot_mask, agg_scale):
    columns, source_total = embedding.shape
    k_total, nb, dest_total = neighbor_rows.shape
    nt = dest_total // TD
    mask4 = slot_mask.reshape(k_total, 1, 1, dest_total)
    rows4 = neighbor_rows.reshape(k_total, 1, nb, dest_total)
    grid_spec = pltpu.PrefetchScalarGridSpec(
        num_scalar_prefetch=1,
        grid=(nt, k_total),
        in_specs=[
            pl.BlockSpec((columns, TS), lambda t, k, tiles: (0, tiles[k * nt + t])),
            pl.BlockSpec((1, 1, nb, TD), lambda t, k, tiles: (k, 0, 0, t)),
            pl.BlockSpec((1, 1, 1, TD), lambda t, k, tiles: (k, 0, 0, t)),
        ],
        out_specs=[
            pl.BlockSpec((1, 1, TS, TD), lambda t, k, tiles: (k, t, 0, 0)),
            pl.BlockSpec((columns, TD), lambda t, k, tiles: (0, t)),
        ],
        scratch_shapes=[pltpu.VMEM((columns, TD), jnp.float32)],
    )
    work = k_total * dest_total * TS
    return pl.pallas_call(
        functools.partial(agg_kernel, agg_scale, k_total, nt),
        grid_spec=grid_spec,
        out_shape=[
            jax.ShapeDtypeStruct((k_total, nt, TS, TD), jnp.bfloat16),
            jax.ShapeDtypeStruct((columns, dest_total), jnp.bfloat16),
        ],
        compiler_params=pltpu.CompilerParams(dimension_semantics=("arbitrary", "arbitrary")),
        cost_estimate=pl.CostEstimate(
            flops=2 * columns * work + 4 * nb * work,
            bytes_accessed=2 * work + 2 * columns * source_total,
            transcendentals=0,
        ),
    )(tiles_flat, embedding, rows4, mask4)


def spread_kernel(agg_scale, k_total, nt, tiles_ref, counts_ref, back_ref, tg_in_ref, tg_ref):
    t = pl.program_id(0)
    k = pl.program_id(1)

    @pl.when((t == 0) & (k == 0))
    def _():
        tg_ref[...] = tg_in_ref[...]

    tile = tiles_ref[k * nt + t]
    start = pl.multiple_of(tile * TS, TS)
    part = jnp.dot(counts_ref[0, 0], back_ref[...], preferred_element_type=jnp.float32)
    tg_ref[pl.ds(start, TS), :] += part * agg_scale


def spread(counts, back, tiles_flat, table_grad, agg_scale):
    k_total, nt = counts.shape[:2]
    source_total, columns = table_grad.shape
    grid_spec = pltpu.PrefetchScalarGridSpec(
        num_scalar_prefetch=1,
        grid=(nt, k_total),
        in_specs=[
            pl.BlockSpec((1, 1, TS, TD), lambda t, k, tiles: (k, t, 0, 0)),
            pl.BlockSpec((TD, columns), lambda t, k, tiles: (t, 0)),
            pl.BlockSpec((source_total, columns), lambda t, k, tiles: (0, 0)),
        ],
        out_specs=pl.BlockSpec((source_total, columns), lambda t, k, tiles: (0, 0)),
    )
    work = k_total * nt * TD * TS
    return pl.pallas_call(
        functools.partial(spread_kernel, agg_scale, k_total, nt),
        grid_spec=grid_spec,
        out_shape=jax.ShapeDtypeStruct((source_total, columns), jnp.float32),
        input_output_aliases={3: 0},
        compiler_params=pltpu.CompilerParams(
            dimension_semantics=("arbitrary", "arbitrary"),
            vmem_limit_bytes=48 * 1024 * 1024,
        ),
        cost_estimate=pl.CostEstimate(
            flops=2 * columns * work,
            bytes_accessed=2 * work + 8 * source_total * columns,
            transcendentals=0,
        ),
    )(tiles_flat, counts, back, table_grad)


def local(
    embedding,
    self_weight,
    neighbor_weight,
    up_weight,
    down_weight,
    source_tiles,
    neighbor_rows,
    slot_mask,
    dest_rows,
    owner_order,
    output_grad,
):
    batch_total = lax.axis_size("batch")
    columns, source_total = embedding.shape
    micro_total = source_tiles.shape[0]
    dest_total = dest_rows.shape[1]
    agg_scale = 1.0 / math.sqrt(K * NB)
    norm_factor = 1.0 / math.sqrt(micro_total * dest_total * batch_total)
    tiles_all = source_tiles.reshape(micro_total, -1)

    target_all = gathered_over(output_grad, "feat", 1)
    table = embedding.T
    counts_all, own_all, hidden_all = [], [], []
    for m in range(micro_total):
        counts, agg_t = aggregate(embedding, tiles_all[m], neighbor_rows[m], slot_mask[m], agg_scale)
        own = table[dest_rows[m]]
        partial = jnp.dot(own, self_weight, preferred_element_type=jnp.float32) + lax.dot_general(
            agg_t, neighbor_weight, (((0,), (0,)), ((), ())), preferred_element_type=jnp.float32
        )
        counts_all.append((counts, agg_t))
        own_all.append(own)
        hidden_all.append(summed_over(partial, "feat"))

    up_sum = jnp.zeros(up_weight.shape, jnp.float32)
    down_sum = jnp.zeros(down_weight.shape, jnp.float32)
    self_sum = jnp.zeros((columns, H), jnp.float32)
    neighbor_sum = jnp.zeros((columns, H), jnp.float32)
    backs = []
    own_grads = []
    for m in range(micro_total):
        agg_t = counts_all[m][1]
        row_order = owner_order[m, 0]
        target = jnp.zeros(target_all.shape[1:], target_all.dtype).at[row_order].set(target_all[m])
        hidden_grad, up_part, down_part = mlp_pass(hidden_all[m], target, up_weight, down_weight)
        up_sum = up_sum + up_part
        down_sum = down_sum + down_part
        self_sum = self_sum + jnp.dot(own_all[m].T, hidden_grad, preferred_element_type=jnp.float32)
        neighbor_sum = neighbor_sum + jnp.dot(agg_t, hidden_grad, preferred_element_type=jnp.float32)
        backs.append(
            jnp.dot(hidden_grad, neighbor_weight.T, preferred_element_type=jnp.float32).astype(jnp.bfloat16)
        )
        own_grads.append(jnp.dot(hidden_grad, self_weight.T, preferred_element_type=jnp.float32))

    sizes = [up_sum.size, down_sum.size, self_sum.size, neighbor_sum.size]
    line = jnp.concatenate([up_sum.ravel(), down_sum.ravel(), self_sum.ravel(), neighbor_sum.ravel()])
    line = summed_over(line, "batch")
    ends = [0]
    for s in sizes:
        ends.append(ends[-1] + s)
    up_sum = line[ends[0] : ends[1]].reshape(up_weight.shape)
    down_sum = line[ends[1] : ends[2]].reshape(down_weight.shape)
    self_sum = line[ends[2] : ends[3]].reshape(columns, H)
    neighbor_sum = line[ends[3] : ends[4]].reshape(columns, H)

    table_grad = jnp.zeros((source_total, columns), jnp.float32)
    for m in range(micro_total):
        table_grad = table_grad.at[dest_rows[m]].add(own_grads[m])
    for m in range(micro_total):
        table_grad = spread(counts_all[m][0], backs[m], tiles_all[m], table_grad, agg_scale)
    return (
        table_grad.T,
        self_sum * norm_factor,
        neighbor_sum * norm_factor,
        up_sum * norm_factor,
        down_sum * norm_factor,
    )


def solution(mesh):
    in_specs = (
        P("feat", "batch"),
        P("feat", None),
        P("feat", None),
        P(),
        P(),
        P(None, None, "batch"),
        P(None, None, None, "batch"),
        P(None, None, "batch"),
        P(None, "batch"),
        P(None, "batch", None),
        P(None, ("batch", "feat"), None),
    )
    out_specs = (P("feat", "batch"), P("feat", None), P("feat", None), P(), P())
    return jax.shard_map(local, mesh=mesh, in_specs=in_specs, out_specs=out_specs, check_vma=False)
```

time: 373 us -> 310 us (0.83)
  Pallas kernels: 185 us -> 133 us
  blocking collectives: 67 us -> 31.1 us
  starting transfers between devices: 13 us -> 37.8 us
  local copies, waits for them, and re-layouts: 28.4 us -> 35.8 us
  waiting for transfers between devices: 32.3 us -> 25.2 us
    pallas_call x1 -> x2, Pallas kernels: 140 us -> 85.4 us  [aggregate(): pl.pallas_call(functools.partial(agg_kernel, agg_scale, k_total, nt), gri...]
    all_to_all x2 -> x1, blocking collectives: 67 us -> 31.1 us  [summed_over(): lax.all_to_all(flat, axis, 0, 0, tiled=True).reshape(n, -1).sum(axis=0)]
    all_to_all x0 -> x2, starting transfers between devices: none -> 15.1 us  [summed_over(): lax.all_to_all(flat, axis, 0, 0, tiled=True).reshape(n, -1).sum(axis=0)]
    all_to_all x1, waiting for transfers between devices: 14.6 us -> 0.01 us  [gathered_over(): lax.all_to_all(jnp.broadcast_to(x[None], (n, *x.shape)), axis, 0, 0, tile...]
    all_to_all x0 -> x2, waiting for transfers between devices: none -> 14.2 us  [summed_over(): lax.all_to_all(flat, axis, 0, 0, tiled=True).reshape(n, -1).sum(axis=0)]
    all_to_all x2 -> x3, waiting for transfers between devices: 17.7 us -> 11 us  [summed_over(): lax.all_to_all(jnp.broadcast_to(mine[None], (n, mine.size)), axis, 0, 0,...]
    all_to_all x1, starting transfers between devices: 4.67 us -> 10 us  [gathered_over(): lax.all_to_all(jnp.broadcast_to(x[None], (n, *x.shape)), axis, 0, 0, tile...]
    all_to_all x2 -> x3, starting transfers between devices: 8.31 us -> 12.6 us  [summed_over(): lax.all_to_all(jnp.broadcast_to(mine[None], (n, mine.size)), axis, 0, 0,...]
  transfers between devices with their start and end apart: 3 -> 6, of which waited for: 2 -> 3; matrix products, arithmetic and copies ran while one was open for 8% -> 18% of each run, Pallas kernels for 12% -> 43%
where the time goes in v3:
time: 310 us; the launch traced here: 308 us
  Pallas kernels  133 us (43%)
  starting transfers between devices  37.8 us (12%)
  local copies, waits for them, and re-layouts  35.8 us (12%)
  blocking collectives  31.1 us (10%)
  other arithmetic  25.2 us (8%)
  waiting for transfers between devices  25.2 us (8%)
  matrix products  19.7 us (6%)
    pallas_call x2, Pallas kernels, aggregate(): pl.pallas_call(functools.partial(agg_kernel, agg_scale, k_total, nt), gri...  85.4 us
    pallas_call x2, Pallas kernels, spread(): pl.pallas_call(functools.partial(spread_kernel, agg_scale, k_total, nt),...  47.1 us
    all_to_all x1, blocking collectives, summed_over(): lax.all_to_all(flat, axis, 0, 0, tiled=True).reshape(n, -1).sum(axis=0)  31.1 us
    scatter-add x2, other arithmetic, local(): table_grad = table_grad.at[dest_rows[m]].add(own_grads[m])  18 us
    all_to_all x2, starting transfers between devices, summed_over(): lax.all_to_all(flat, axis, 0, 0, tiled=True).reshape(n, -1).sum(axis=0)  15.1 us
    all_to_all x2, waiting for transfers between devices, summed_over(): lax.all_to_all(flat, axis, 0, 0, tiled=True).reshape(n, -1).sum(axis=0)  14.2 us
    all_to_all x3, starting transfers between devices, summed_over(): lax.all_to_all(jnp.broadcast_to(mine[None], (n, mine.size)), axis, 0, 0,...  12.6 us
    all_to_all x3, waiting for transfers between devices, summed_over(): lax.all_to_all(jnp.broadcast_to(mine[None], (n, mine.size)), axis, 0, 0,...  11 us
  transfers between devices with their start and end apart: 6, of which 3 were waited for; matrix products, arithmetic and copies ran while one was open for 18% of the time, Pallas kernels for 43%

profile of v3, /device:TPU:1, one launch (start us, length us, event | category | flops | bytes accessed | tf_op | source)
XLA Modules:
  0.0 308.4 jit_solution(17339491451115199169)
XLA Ops:
  2.4 10.0 %all-to-all-start = ((bf16[16,2,64,128]{3,2,1,0:T(8,128)(2,1)}), bf16[16,2,64,128]{3,2,1,0:T(8,128)(2,1)S(1)}, u32[]{:S(2)}, u32[]{:S(2)}) async-start(bf16[16,2,64,128]{3,2,1,0:T(8,128)(2,1)} %broadcast_in_dim.10), calls=%async_computation | async-start | bytes 1048576 | tf_op jit(solution)/shard_map/all_to_all | solution.py:51
  16.0 2.0 copy.77
  18.1 3.2 %gather_fusion.1 = bf16[1024,64]{1,0:T(8,128)(2,1)S(1)} fusion(bf16[8192,64]{1,0:T(8,128)(2,1)S(1)} %bitcast.81, s32[1024]{0:T(1024)S(1)} %broadcast_clamp_fusion), kind=kCustom, calls=%fused_computation.1 | custom fusion | bytes 266240 | tf_op jit(solution)/shard_map/gather | solution.py:196
  21.3 2.3 slice_bitcast_fusion
  23.6 42.6 %shard_map.147 = (bf16[8,4,1024,256]{3,2,1,0:T(8,128)(2,1)}, bf16[64,1024]{1,0:T(8,128)(2,1)}) custom-call(s32[32]{0:T(128)} %squeeze.32.tiles_ref, bf16[64,8192]{1,0:T(8,128)(2,1)} %emb_ref.3, s32[8,1,16,1024]{3,2,1,0:T(8,128)} %get-tuple-element.45.rows_ref, s32[8,1,1,1024]{3,2,1,0:T(1,128)} %get-tuple-element.58.mask_ref), custom_call_target="tpu_custom_call" | custom-call | flops 1610612736 | bytes 17825792 | tf_op jit(solution)/shard_map/pallas_call | solution.py:109
  66.4 2.0 convolution_add_fusion
  69.2 7.6 %all-to-all-start.3 = ((f32[16,1,8192]{2,1,0:T(1,128)}), f32[16,1,8192]{2,1,0:T(1,128)S(1)}, u32[]{:S(2)}, u32[]{:S(2)}) async-start(f32[16,1,8192]{2,1,0:T(1,128)} %bitcast.93), calls=%async_computation.3 | async-start | bytes 1048576 | tf_op jit(solution)/shard_map/all_to_all | solution.py:44
  77.4 3.2 %gather_fusion = bf16[1024,64]{1,0:T(8,128)(2,1)S(1)} fusion(bf16[8192,64]{1,0:T(8,128)(2,1)S(1)} %bitcast.82, s32[1024]{0:T(1024)S(1)} %broadcast_clamp_fusion.1), kind=kCustom, calls=%fused_computation | custom fusion | bytes 266240 | tf_op jit(solution)/shard_map/gather | solution.py:196
  80.7 42.8 %shard_map.146 = (bf16[8,4,1024,256]{3,2,1,0:T(8,128)(2,1)}, bf16[64,1024]{1,0:T(8,128)(2,1)}) custom-call(s32[32]{0:T(128)} %squeeze.28.tiles_ref, bf16[64,8192]{1,0:T(8,128)(2,1)} %emb_ref.3, s32[8,1,16,1024]{3,2,1,0:T(8,128)} %get-tuple-element.46.rows_ref, s32[8,1,1,1024]{3,2,1,0:T(1,128)} %get-tuple-element.57.mask_ref), custom_call_target="tpu_custom_call" | custom-call | flops 1610612736 | bytes 17825792 | tf_op jit(solution)/shard_map/pallas_call | solution.py:109
  123.6 2.0 convolution_add_fusion.1
  125.6 7.6 %all-to-all-start.1 = ((f32[16,1,8192]{2,1,0:T(1,128)}), f32[16,1,8192]{2,1,0:T(1,128)S(1)}, u32[]{:S(2)}, u32[]{:S(2)}) async-start(f32[16,1,8192]{2,1,0:T(1,128)} %bitcast.9), calls=%async_computation.1 | async-start | bytes 1048576 | tf_op jit(solution)/shard_map/all_to_all | solution.py:44
  133.5 14.2 %all-to-all-done.1 = f32[16,1,8192]{2,1,0:T(1,128)S(1)} async-done(((f32[16,1,8192]{2,1,0:T(1,128)}), f32[16,1,8192]{2,1,0:T(1,128)S(1)}, u32[]{:S(2)}, u32[]{:S(2)}) %all-to-all-start.1) | async-done | bytes 524320 | tf_op jit(solution)/shard_map/all_to_all | solution.py:44
  149.0 4.4 %all-to-all-start.4 = ((f32[16,1,8192]{2,1,0:T(1,128)}), f32[16,1,8192]{2,1,0:T(1,128)S(1)}, u32[]{:S(2)}, u32[]{:S(2)}) async-start(f32[16,1,8192]{2,1,0:T(1,128)} %broadcast_in_dim.12), calls=%async_computation.4 | async-start | bytes 1048576 | tf_op jit(solution)/shard_map/all_to_all | solution.py:45
  153.5 3.2 %scatter_custom_fusion.1 = bf16[1024,128]{1,0:T(8,128)(2,1)S(1)} fusion(s32[1024]{0:T(1024)S(1)} %bitcast.102, bf16[1024,128]{1,0:T(8,128)(2,1)S(1)} %bitcast.96, bf16[]{:T(256)} %constant.12.clone.1), kind=kCustom, calls=%fused_computation.71 | custom fusion | bytes 262146 | tf_op jit(solution)/shard_map/scatter | solution.py:213
  156.7 3.2 %scatter_custom_fusion = bf16[1024,128]{1,0:T(8,128)(2,1)S(1)} fusion(s32[1024]{0:T(1024)S(1)} %bitcast.101, bf16[1024,128]{1,0:T(8,128)(2,1)S(1)} %bitcast.95, bf16[]{:T(256)} %constant.12.clone.1), kind=kCustom, calls=%fused_computation.73 | custom fusion | bytes 262146 | tf_op jit(solution)/shard_map/scatter | solution.py:213
  160.3 6.5 %all-to-all-done.4 = f32[16,1,8192]{2,1,0:T(1,128)S(1)} async-done(((f32[16,1,8192]{2,1,0:T(1,128)}), f32[16,1,8192]{2,1,0:T(1,128)S(1)}, u32[]{:S(2)}, u32[]{:S(2)}) %all-to-all-start.4) | async-done | bytes 524320 | tf_op jit(solution)/shard_map/all_to_all | solution.py:45
  167.9 4.3 %all-to-all-start.2 = ((f32[16,1,8192]{2,1,0:T(1,128)}), f32[16,1,8192]{2,1,0:T(1,128)S(1)}, u32[]{:S(2)}, u32[]{:S(2)}) async-start(f32[16,1,8192]{2,1,0:T(1,128)} %broadcast_in_dim.11), calls=%async_computation.2 | async-start | bytes 1048576 | tf_op jit(solution)/shard_map/all_to_all | solution.py:45
  173.0 3.0 fusion.15
  177.9 1.7 fusion.18
  179.6 4.5 %all-to-all-done.2 = f32[16,1,8192]{2,1,0:T(1,128)S(1)} async-done(((f32[16,1,8192]{2,1,0:T(1,128)}), f32[16,1,8192]{2,1,0:T(1,128)S(1)}, u32[]{:S(2)}, u32[]{:S(2)}) %all-to-all-start.2) | async-done | bytes 524320 | tf_op jit(solution)/shard_map/all_to_all | solution.py:45
  184.8 3.0 fusion.7
  187.9 1.7 fusion.21
  191.7 31.1 %all_to_all.50 = f32[16,1,17408]{2,1,0:T(1,128)S(1)} all-to-all(f32[16,1,17408]{2,1,0:T(1,128)S(1)} %bitcast.91), channel_id=1, replica_groups=mesh['batch'=16,'feat'=16] {'batch'}, dimensions={0} | all-to-all | bytes 2228224 | tf_op jit(solution)/shard_map/all_to_all | solution.py:44
  225.1 3.9 %all-to-all-start.6 = ((f32[16,1,17408]{2,1,0:T(1,128)}), f32[16,1,17408]{2,1,0:T(1,128)S(1)}, u32[]{:S(2)}, u32[]{:S(2)}) async-start(f32[16,1,17408]{2,1,0:T(1,128)} %broadcast_in_dim.14), calls=%async_computation.6 | async-start | bytes 2228224 | tf_op jit(solution)/shard_map/all_to_all | solution.py:45
  229.6 8.3 %scatter_custom_fusion.2 = f32[8192,64]{1,0:T(8,128)} fusion(s32[1024]{0:T(1024)S(1)} %bitcast.100, f32[1024,64]{1,0:T(8,128)S(1)} %fusion.59, f32[]{:T(128)} %constant.16.clone.1), kind=kCustom, calls=%fused_computation.28 | custom fusion | flops 65536 | bytes 2097156 | tf_op jit(solution)/shard_map/scatter-add | solution.py:237
  238.5 9.7 %scatter_fusion = f32[8192,64]{1,0:T(8,128)} fusion(f32[8192,64]{1,0:T(8,128)} %scatter_custom_fusion.2, s32[1024]{0:T(1024)S(1)} %bitcast.98, f32[1024,64]{1,0:T(8,128)S(1)} %fusion.60), kind=kCustom, calls=%fused_computation.5 | custom fusion | flops 65536 | bytes 790528 | tf_op jit(solution)/shard_map/scatter-add | solution.py:237
  248.2 2.2 copy-done.1
  250.4 23.5 %shard_map.148.tg_in_ref = f32[8192,64]{1,0:T(8,128)S(1)} custom-call(s32[32]{0:T(128)S(1)} %copy-done.3, bf16[8,4,1024,256]{3,2,1,0:T(8,128)(2,1)} %get-tuple-element.11.counts_ref, bf16[1024,64]{1,0:T(8,128)(2,1)S(1)} %copy.84.back_ref, f32[8192,64]{1,0:T(8,128)S(1)} %copy-done.1), custom_call_target="tpu_custom_call", output_to_operand_aliasing={{}: (3, {})} | custom-call | flops 1073741824 | bytes 20971520 | tf_op jit(solution)/shard_map/pallas_call | solution.py:153
  273.9 23.6 %shard_map.149 = f32[8192,64]{1,0:T(8,128)S(1)} custom-call(s32[32]{0:T(128)S(1)} %copy-done.4, bf16[8,4,1024,256]{3,2,1,0:T(8,128)(2,1)} %get-tuple-element.9.counts_ref, bf16[1024,64]{1,0:T(8,128)(2,1)S(1)} %copy.85.back_ref, f32[8192,64]{1,0:T(8,128)S(1)} %shard_map.148.tg_in_ref), custom_call_target="tpu_custom_call", output_to_operand_aliasing={{}: (3, {})} | custom-call | flops 1073741824 | bytes 20971520 | tf_op jit(solution)/shard_map/pallas_call | solution.py:153
  297.5 1.9 copy-done.2
  299.5 3.8 %copy.87 = f32[64,8192]{1,0:T(8,128)} copy(f32[64,8192]{0,1:T(8,128)} %bitcast.80) | data formatting | bytes 4194304
  304.7 2.6 reduce.3
  (72 shorter events, 21.6 us)
Async XLA Ops:
  0.6 171.6 %copy-start = (bf16[128,1024]{1,0:T(8,128)(2,1)S(1)}, bf16[128,1024]{1,0:T(8,128)(2,1)}, u32[]{:S(2)}) copy-start(bf16[128,1024]{1,0:T(8,128)(2,1)} %param.14) | copy-start | bytes 786436
  2.4 66.0 %all-to-all-start = ((bf16[16,2,64,128]{3,2,1,0:T(8,128)(2,1)}), bf16[16,2,64,128]{3,2,1,0:T(8,128)(2,1)S(1)}, u32[]{:S(2)}, u32[]{:S(2)}) async-start(bf16[16,2,64,128]{3,2,1,0:T(8,128)(2,1)} %broadcast_in_dim.10), calls=%async_computation | async-start | bytes 1048576 | tf_op jit(solution)/shard_map/all_to_all | solution.py:51
  21.3 44.9 %copy-start.10 = (bf16[64,128]{1,0:T(8,128)(2,1)S(1)}, bf16[64,128]{1,0:T(8,128)(2,1)}, u32[]{:S(2)}) copy-start(bf16[64,128]{1,0:T(8,128)(2,1)} %param.12) | copy-start | bytes 49156
  21.3 45.1 %copy-start.9 = (bf16[64,128]{1,0:T(8,128)(2,1)S(1)}, bf16[64,128]{1,0:T(8,128)(2,1)}, u32[]{:S(2)}) copy-start(bf16[64,128]{1,0:T(8,128)(2,1)} %param.13) | copy-start | bytes 49156
  68.4 0.8 copy-start.5
  69.2 56.4 %all-to-all-start.3 = ((f32[16,1,8192]{2,1,0:T(1,128)}), f32[16,1,8192]{2,1,0:T(1,128)S(1)}, u32[]{:S(2)}, u32[]{:S(2)}) async-start(f32[16,1,8192]{2,1,0:T(1,128)} %bitcast.93), calls=%async_computation.3 | async-start | bytes 1048576 | tf_op jit(solution)/shard_map/all_to_all | solution.py:44
  80.6 72.7 %copy-start.11 = (s32[2,1,1024]{2,1,0:T(1,128)S(1)}, s32[2,1,1024]{2,1,0:T(1,128)}, u32[]{:S(2)}) copy-start(s32[2,1,1024]{2,1,0:T(1,128)} %param.20) | copy-start | bytes 24580
  80.7 72.7 %copy-start.6 = (bf16[16,2,64,128]{3,2,1,0:T(8,128)(2,1)S(1)}, bf16[16,2,64,128]{3,2,1,0:T(8,128)(2,1)}, u32[]{:S(2)}) copy-start(bf16[16,2,64,128]{3,2,1,0:T(8,128)(2,1)} %copy-done.5) | copy-start | bytes 1572868
  125.6 22.2 %all-to-all-start.1 = ((f32[16,1,8192]{2,1,0:T(1,128)}), f32[16,1,8192]{2,1,0:T(1,128)S(1)}, u32[]{:S(2)}, u32[]{:S(2)}) async-start(f32[16,1,8192]{2,1,0:T(1,128)} %bitcast.9), calls=%async_computation.1 | async-start | bytes 1048576 | tf_op jit(solution)/shard_map/all_to_all | solution.py:44
  149.0 17.8 %all-to-all-start.4 = ((f32[16,1,8192]{2,1,0:T(1,128)}), f32[16,1,8192]{2,1,0:T(1,128)S(1)}, u32[]{:S(2)}, u32[]{:S(2)}) async-start(f32[16,1,8192]{2,1,0:T(1,128)} %broadcast_in_dim.12), calls=%async_computation.4 | async-start | bytes 1048576 | tf_op jit(solution)/shard_map/all_to_all | solution.py:45
  153.5 19.5 %copy-start.12 = (bf16[1024,128]{1,0:T(8,128)(2,1)S(1)}, bf16[1024,128]{1,0:T(8,128)(2,1)}, u32[]{:S(2)}) copy-start(bf16[1024,128]{1,0:T(8,128)(2,1)} %param.15) | copy-start | bytes 786436
  167.9 16.2 %all-to-all-start.2 = ((f32[16,1,8192]{2,1,0:T(1,128)}), f32[16,1,8192]{2,1,0:T(1,128)S(1)}, u32[]{:S(2)}, u32[]{:S(2)}) async-start(f32[16,1,8192]{2,1,0:T(1,128)} %broadcast_in_dim.11), calls=%async_computation.2 | async-start | bytes 1048576 | tf_op jit(solution)/shard_map/all_to_all | solution.py:45
  176.0 1.1 copy-start.8
  179.6 5.2 %copy-start.13 = (bf16[1024,128]{1,0:T(8,128)(2,1)S(1)}, bf16[1024,128]{1,0:T(8,128)(2,1)}, u32[]{:S(2)}) copy-start(bf16[1024,128]{1,0:T(8,128)(2,1)} %param.15) | copy-start | bytes 786436
  189.6 1.7 copy-start.7
  225.1 78.2 %all-to-all-start.6 = ((f32[16,1,17408]{2,1,0:T(1,128)}), f32[16,1,17408]{2,1,0:T(1,128)S(1)}, u32[]{:S(2)}, u32[]{:S(2)}) async-start(f32[16,1,17408]{2,1,0:T(1,128)} %broadcast_in_dim.14), calls=%async_computation.6 | async-start | bytes 2228224 | tf_op jit(solution)/shard_map/all_to_all | solution.py:45
  238.5 9.7 %copy-start.3 = (s32[32]{0:T(128)S(1)}, s32[32]{0:T(128)}, u32[]{:S(2)}) copy-start(s32[32]{0:T(128)} %squeeze.32.tiles_ref) | copy-start | bytes 388
  248.2 2.2 copy-start.1
  250.4 23.5 %copy-start.4 = (s32[32]{0:T(128)S(1)}, s32[32]{0:T(128)}, u32[]{:S(2)}) copy-start(s32[32]{0:T(128)} %squeeze.28.tiles_ref) | copy-start | bytes 388
  297.5 1.9 copy-start.2

commit v4 on v3

--- a/solution.py
+++ b/solution.py
@@ -13,7 +13,7 @@
 TS = 1024
 K = 8
 NB = 16
-CS = 128
+CS = 256
 
 
 def gelu_slope(values):
@@ -74,11 +74,12 @@
         for j in range(NB):
             here = local[j : j + 1, :].astype(jnp.bfloat16)
             cnt = cnt + jnp.where(here == local_iota, one, zero)
-        counts_ref[0, 0, pl.ds(start, CS), :] = cnt * msk
+        cnt = cnt * msk
+        counts_ref[0, 0, pl.ds(start, CS), :] = cnt
+        acc_ref[...] += jnp.dot(emb_ref[:, pl.ds(start, CS)], cnt, preferred_element_type=jnp.float32)
         return carry
 
     lax.fori_loop(0, TS // CS, chunk, 0)
-    acc_ref[...] += jnp.dot(emb_ref[...], counts_ref[0, 0], preferred_element_type=jnp.float32)
 
     @pl.when(k == k_total - 1)
     def _():
@@ -205,21 +206,27 @@
     down_sum = jnp.zeros(down_weight.shape, jnp.float32)
     self_sum = jnp.zeros((columns, H), jnp.float32)
     neighbor_sum = jnp.zeros((columns, H), jnp.float32)
-    backs = []
-    own_grads = []
+    table_grad = jnp.zeros((source_total, columns), jnp.float32)
+    pending = []
     for m in range(micro_total):
+        hidden = hidden_all[m]
+        if m > 0:
+            hidden, table_grad = lax.optimization_barrier((hidden, table_grad))
         agg_t = counts_all[m][1]
         row_order = owner_order[m, 0]
         target = jnp.zeros(target_all.shape[1:], target_all.dtype).at[row_order].set(target_all[m])
-        hidden_grad, up_part, down_part = mlp_pass(hidden_all[m], target, up_weight, down_weight)
+        hidden_grad, up_part, down_part = mlp_pass(hidden, target, up_weight, down_weight)
         up_sum = up_sum + up_part
         down_sum = down_sum + down_part
         self_sum = self_sum + jnp.dot(own_all[m].T, hidden_grad, preferred_element_type=jnp.float32)
         neighbor_sum = neighbor_sum + jnp.dot(agg_t, hidden_grad, preferred_element_type=jnp.float32)
-        backs.append(
-            jnp.dot(hidden_grad, neighbor_weight.T, preferred_element_type=jnp.float32).astype(jnp.bfloat16)
-        )
-        own_grads.append(jnp.dot(hidden_grad, self_weight.T, preferred_element_type=jnp.float32))
+        back = jnp.dot(hidden_grad, neighbor_weight.T, preferred_element_type=jnp.float32).astype(jnp.bfloat16)
+        own_grad = jnp.dot(hidden_grad, self_weight.T, preferred_element_type=jnp.float32)
+        if m + 1 < micro_total:
+            table_grad = spread(counts_all[m][0], back, tiles_all[m], table_grad, agg_scale)
+            table_grad = table_grad.at[dest_rows[m]].add(own_grad)
+        else:
+            pending.append((m, back, own_grad))
 
     sizes = [up_sum.size, down_sum.size, self_sum.size, neighbor_sum.size]
     line = jnp.concatenate([up_sum.ravel(), down_sum.ravel(), self_sum.ravel(), neighbor_sum.ravel()])
@@ -232,11 +239,9 @@
     self_sum = line[ends[2] : ends[3]].reshape(columns, H)
     neighbor_sum = line[ends[3] : ends[4]].reshape(columns, H)
 
-    table_grad = jnp.zeros((source_total, columns), jnp.float32)
-    for m in range(micro_total):
-        table_grad = table_grad.at[dest_rows[m]].add(own_grads[m])
-    for m in range(micro_total):
-        table_grad = spread(counts_all[m][0], backs[m], tiles_all[m], table_grad, agg_scale)
+    for m, back, own_grad in pending:
+        table_grad = spread(counts_all[m][0], back, tiles_all[m], table_grad, agg_scale)
+        table_grad = table_grad.at[dest_rows[m]].add(own_grad)
     return (
         table_grad.T,
         self_sum * norm_factor,

time: 310 us -> 323 us (1.042)
  Pallas kernels: 133 us -> 145 us
  waiting for transfers between devices: 25.2 us -> 19.6 us
  matrix products: 19.7 us -> 23.2 us
    pallas_call x2, Pallas kernels: 85.4 us -> 97.5 us  [aggregate(): pl.pallas_call(functools.partial(agg_kernel, agg_scale, k_total, nt), gri...]
    all_to_all x3, waiting for transfers between devices: 11 us -> 5.39 us  [summed_over(): lax.all_to_all(jnp.broadcast_to(mine[None], (n, mine.size)), axis, 0, 0,...]
    unnamed x31 -> x33, local copies, waits for them, and re-layouts: 10.9 us -> 12.3 us
  transfers between devices with their start and end apart: 6 -> 6, of which waited for: 3 -> 2; matrix products, arithmetic and copies ran while one was open for 18% -> 20% of each run, Pallas kernels for 43% -> 45%
where the time goes in v4:
time: 323 us; the launch traced here: 320 us
  Pallas kernels  145 us (45%)
  local copies, waits for them, and re-layouts  38.5 us (12%)
  starting transfers between devices  37.8 us (12%)
  blocking collectives  29 us (9%)
  other arithmetic  26.4 us (8%)
  matrix products  23.2 us (7%)
  waiting for transfers between devices  19.6 us (6%)
    pallas_call x2, Pallas kernels, aggregate(): pl.pallas_call(functools.partial(agg_kernel, agg_scale, k_total, nt), gri...  97.5 us
    pallas_call x2, Pallas kernels, spread(): pl.pallas_call(functools.partial(spread_kernel, agg_scale, k_total, nt),...  47.2 us
    all_to_all x1, blocking collectives, summed_over(): lax.all_to_all(flat, axis, 0, 0, tiled=True).reshape(n, -1).sum(axis=0)  29 us
    scatter-add x2, other arithmetic, local(): table_grad = table_grad.at[dest_rows[m]].add(own_grad)  19.1 us
    all_to_all x2, starting transfers between devices, summed_over(): lax.all_to_all(flat, axis, 0, 0, tiled=True).reshape(n, -1).sum(axis=0)  15.1 us
    all_to_all x2, waiting for transfers between devices, summed_over(): lax.all_to_all(flat, axis, 0, 0, tiled=True).reshape(n, -1).sum(axis=0)  14.2 us
    all_to_all x3, starting transfers between devices, summed_over(): lax.all_to_all(jnp.broadcast_to(mine[None], (n, mine.size)), axis, 0, 0,...  12.6 us
    unnamed x33, local copies, waits for them, and re-layouts  12.3 us
  transfers between devices with their start and end apart: 6, of which 2 were waited for; matrix products, arithmetic and copies ran while one was open for 20% of the time, Pallas kernels for 45%

profile of v4, /device:TPU:1, one launch (start us, length us, event | category | flops | bytes accessed | tf_op | source)
XLA Modules:
  0.0 320.4 jit_solution(12246136177514036912)
XLA Ops:
  2.4 10.1 %all-to-all-start = ((bf16[16,2,64,128]{3,2,1,0:T(8,128)(2,1)}), bf16[16,2,64,128]{3,2,1,0:T(8,128)(2,1)}, u32[]{:S(2)}, u32[]{:S(2)}) async-start(bf16[16,2,64,128]{3,2,1,0:T(8,128)(2,1)} %broadcast_in_dim.10), calls=%async_computation | async-start | bytes 1048576 | tf_op jit(solution)/shard_map/all_to_all | solution.py:51
  16.1 2.0 copy.77
  18.2 3.2 %gather_fusion.1 = bf16[1024,64]{1,0:T(8,128)(2,1)S(1)} fusion(bf16[8192,64]{1,0:T(8,128)(2,1)S(1)} %bitcast.81, s32[1024]{0:T(1024)S(1)} %broadcast_clamp_fusion), kind=kCustom, calls=%fused_computation.1 | custom fusion | bytes 266240 | tf_op jit(solution)/shard_map/gather | solution.py:197
  21.4 2.3 slice_bitcast_fusion
  23.7 48.7 %shard_map.147 = (bf16[8,4,1024,256]{3,2,1,0:T(8,128)(2,1)}, bf16[64,1024]{1,0:T(8,128)(2,1)}) custom-call(s32[32]{0:T(128)} %squeeze.32.tiles_ref, bf16[64,8192]{1,0:T(8,128)(2,1)} %emb_ref.3, s32[8,1,16,1024]{3,2,1,0:T(8,128)} %get-tuple-element.49.rows_ref, s32[8,1,1,1024]{3,2,1,0:T(1,128)} %get-tuple-element.62.mask_ref), custom_call_target="tpu_custom_call" | custom-call | flops 1610612736 | bytes 17825792 | tf_op jit(solution)/shard_map/pallas_call | solution.py:110
  72.6 2.0 convolution_add_fusion
  74.6 7.5 %all-to-all-start.3 = ((f32[16,1,8192]{2,1,0:T(1,128)}), f32[16,1,8192]{2,1,0:T(1,128)S(1)}, u32[]{:S(2)}, u32[]{:S(2)}) async-start(f32[16,1,8192]{2,1,0:T(1,128)} %bitcast.93), calls=%async_computation.3 | async-start | bytes 1048576 | tf_op jit(solution)/shard_map/all_to_all | solution.py:44
  82.8 3.2 gather_fusion
  86.0 48.8 %shard_map.146 = (bf16[8,4,1024,256]{3,2,1,0:T(8,128)(2,1)}, bf16[64,1024]{1,0:T(8,128)(2,1)}) custom-call(s32[32]{0:T(128)} %squeeze.28.tiles_ref, bf16[64,8192]{1,0:T(8,128)(2,1)} %emb_ref.3, s32[8,1,16,1024]{3,2,1,0:T(8,128)} %get-tuple-element.50.rows_ref, s32[8,1,1,1024]{3,2,1,0:T(1,128)} %get-tuple-element.61.mask_ref), custom_call_target="tpu_custom_call" | custom-call | flops 1610612736 | bytes 17825792 | tf_op jit(solution)/shard_map/pallas_call | solution.py:110
  135.0 2.0 convolution_add_fusion.1
  136.9 7.6 %all-to-all-start.1 = ((f32[16,1,8192]{2,1,0:T(1,128)}), f32[16,1,8192]{2,1,0:T(1,128)S(1)}, u32[]{:S(2)}, u32[]{:S(2)}) async-start(f32[16,1,8192]{2,1,0:T(1,128)} %bitcast.9), calls=%async_computation.1 | async-start | bytes 1048576 | tf_op jit(solution)/shard_map/all_to_all | solution.py:44
  144.9 14.2 %all-to-all-done.1 = f32[16,1,8192]{2,1,0:T(1,128)S(1)} async-done(((f32[16,1,8192]{2,1,0:T(1,128)}), f32[16,1,8192]{2,1,0:T(1,128)S(1)}, u32[]{:S(2)}, u32[]{:S(2)}) %all-to-all-start.1) | async-done | bytes 524320 | tf_op jit(solution)/shard_map/all_to_all | solution.py:44
  160.3 4.4 %all-to-all-start.4 = ((f32[16,1,8192]{2,1,0:T(1,128)}), f32[16,1,8192]{2,1,0:T(1,128)S(1)}, u32[]{:S(2)}, u32[]{:S(2)}) async-start(f32[16,1,8192]{2,1,0:T(1,128)} %broadcast_in_dim.12), calls=%async_computation.4 | async-start | bytes 1048576 | tf_op jit(solution)/shard_map/all_to_all | solution.py:45
  165.9 3.2 %scatter_custom_fusion = bf16[1024,128]{1,0:T(8,128)(2,1)S(1)} fusion(s32[1024]{0:T(1024)S(1)} %bitcast.101, bf16[1024,128]{1,0:T(8,128)(2,1)S(1)} %bitcast.95, bf16[]{:T(256)} %constant.12.clone.1), kind=kCustom, calls=%fused_computation.71 | custom fusion | bytes 262146 | tf_op jit(solution)/shard_map/scatter | solution.py:217
  169.1 3.2 %scatter_custom_fusion.1 = bf16[1024,128]{1,0:T(8,128)(2,1)S(1)} fusion(s32[1024]{0:T(1024)S(1)} %bitcast.100, bf16[1024,128]{1,0:T(8,128)(2,1)S(1)} %bitcast.94, bf16[]{:T(256)} %constant.12.clone.1), kind=kCustom, calls=%fused_computation.69 | custom fusion | bytes 262146 | tf_op jit(solution)/shard_map/scatter | solution.py:217
  172.7 5.4 %all-to-all-done.4 = f32[16,1,8192]{2,1,0:T(1,128)S(1)} async-done(((f32[16,1,8192]{2,1,0:T(1,128)}), f32[16,1,8192]{2,1,0:T(1,128)S(1)}, u32[]{:S(2)}, u32[]{:S(2)}) %all-to-all-start.4) | async-done | bytes 524320 | tf_op jit(solution)/shard_map/all_to_all | solution.py:45
  179.3 4.3 %all-to-all-start.2 = ((f32[16,1,8192]{2,1,0:T(1,128)}), f32[16,1,8192]{2,1,0:T(1,128)S(1)}, u32[]{:S(2)}, u32[]{:S(2)}) async-start(f32[16,1,8192]{2,1,0:T(1,128)} %broadcast_in_dim.11), calls=%async_computation.2 | async-start | bytes 1048576 | tf_op jit(solution)/shard_map/all_to_all | solution.py:45
  184.3 3.0 fusion.7
  189.3 23.6 %shard_map.148 = f32[8192,64]{1,0:T(8,128)S(1)} custom-call(s32[32]{0:T(128)S(1)} %copy-done.5, bf16[8,4,1024,256]{3,2,1,0:T(8,128)(2,1)} %get-tuple-element.13.counts_ref, bf16[1024,64]{1,0:T(8,128)(2,1)S(1)} %copy.83.back_ref, f32[8192,64]{1,0:T(8,128)S(1)} %broadcast_in_dim.13.clone.tg_in_ref), custom_call_target="tpu_custom_call", output_to_operand_aliasing={{}: (3, {})} | custom-call | flops 1073741824 | bytes 20971520 | tf_op jit(solution)/shard_map/pallas_call | solution.py:154
  212.9 1.9 copy-done.1
  214.9 9.6 %scatter_fusion = f32[8192,64]{1,0:T(8,128)} fusion(f32[8192,64]{1,0:T(8,128)} %copy-done.1, s32[1024]{0:T(1024)S(1)} %bitcast.99, f32[1024,64]{1,0:T(8,128)S(1)} %fusion.57), kind=kCustom, calls=%fused_computation.4 | custom fusion | flops 65536 | bytes 790528 | tf_op jit(solution)/shard_map/scatter-add | solution.py:227
  224.6 2.2 fusion.49
  226.8 3.7 %fusion.16 = f32[1024,128]{1,0:T(8,128)S(1)} fusion(bf16[1024,128]{1,0:T(8,128)(2,1)S(1)} %scatter_custom_fusion.1, f32[1024,1024]{1,0:T(8,128)} %copy-done.6), kind=kOutput, calls=%fused_computation.28 | convolution fusion | flops 277872640 | bytes 4980736 | tf_op jit(solution)/shard_map/dot_general | solution.py:30
  231.5 3.0 fusion.15
  238.3 29.0 %all_to_all.50 = f32[16,1,17408]{2,1,0:T(1,128)S(1)} all-to-all(f32[16,1,17408]{2,1,0:T(1,128)S(1)} %bitcast.91), channel_id=1, replica_groups=mesh['batch'=16,'feat'=16] {'batch'}, dimensions={0} | all-to-all | bytes 2228224 | tf_op jit(solution)/shard_map/all_to_all | solution.py:44
  269.6 3.9 %all-to-all-start.6 = ((f32[16,1,17408]{2,1,0:T(1,128)}), f32[16,1,17408]{2,1,0:T(1,128)S(1)}, u32[]{:S(2)}, u32[]{:S(2)}) async-start(f32[16,1,17408]{2,1,0:T(1,128)} %broadcast_in_dim.14), calls=%async_computation.6 | async-start | bytes 2228224 | tf_op jit(solution)/shard_map/all_to_all | solution.py:45
  274.0 2.2 copy-done.2
  276.2 23.6 %shard_map.149 = f32[8192,64]{1,0:T(8,128)S(1)} custom-call(s32[32]{0:T(128)S(1)} %copy-done.4, bf16[8,4,1024,256]{3,2,1,0:T(8,128)(2,1)} %get-tuple-element.11.counts_ref, bf16[1024,64]{1,0:T(8,128)(2,1)S(1)} %copy.85.back_ref, f32[8192,64]{1,0:T(8,128)S(1)} %copy-done.2), custom_call_target="tpu_custom_call", output_to_operand_aliasing={{}: (3, {})} | custom-call | flops 1073741824 | bytes 20971520 | tf_op jit(solution)/shard_map/pallas_call | solution.py:154
  299.8 1.9 copy-done.3
  301.9 9.6 %scatter_fusion.1 = f32[8192,64]{1,0:T(8,128)} fusion(f32[8192,64]{1,0:T(8,128)} %copy-done.3, s32[1024]{0:T(1024)S(1)} %bitcast.97, f32[1024,64]{1,0:T(8,128)S(1)} %fusion.58), kind=kCustom, calls=%fused_computation.5 | custom fusion | flops 65536 | bytes 790528 | tf_op jit(solution)/shard_map/scatter-add | solution.py:244
  311.5 3.8 %copy.88 = f32[64,8192]{1,0:T(8,128)} copy(f32[64,8192]{0,1:T(8,128)} %bitcast.80) | data formatting | bytes 4194304
  316.8 2.6 reduce.3
  (75 shorter events, 23.6 us)
Async XLA Ops:
  0.6 182.9 %copy-start = (bf16[128,1024]{1,0:T(8,128)(2,1)S(1)}, bf16[128,1024]{1,0:T(8,128)(2,1)}, u32[]{:S(2)}) copy-start(bf16[128,1024]{1,0:T(8,128)(2,1)} %param.14) | copy-start | bytes 786436
  2.4 72.2 %all-to-all-start = ((bf16[16,2,64,128]{3,2,1,0:T(8,128)(2,1)}), bf16[16,2,64,128]{3,2,1,0:T(8,128)(2,1)}, u32[]{:S(2)}, u32[]{:S(2)}) async-start(bf16[16,2,64,128]{3,2,1,0:T(8,128)(2,1)} %broadcast_in_dim.10), calls=%async_computation | async-start | bytes 1048576 | tf_op jit(solution)/shard_map/all_to_all | solution.py:51
  21.4 51.0 %copy-start.11 = (bf16[64,128]{1,0:T(8,128)(2,1)S(1)}, bf16[64,128]{1,0:T(8,128)(2,1)}, u32[]{:S(2)}) copy-start(bf16[64,128]{1,0:T(8,128)(2,1)} %param.12) | copy-start | bytes 49156
  21.4 51.2 %copy-start.10 = (bf16[64,128]{1,0:T(8,128)(2,1)S(1)}, bf16[64,128]{1,0:T(8,128)(2,1)}, u32[]{:S(2)}) copy-start(bf16[64,128]{1,0:T(8,128)(2,1)} %param.13) | copy-start | bytes 49156
  74.6 62.4 %all-to-all-start.3 = ((f32[16,1,8192]{2,1,0:T(1,128)}), f32[16,1,8192]{2,1,0:T(1,128)S(1)}, u32[]{:S(2)}, u32[]{:S(2)}) async-start(f32[16,1,8192]{2,1,0:T(1,128)} %bitcast.93), calls=%async_computation.3 | async-start | bytes 1048576 | tf_op jit(solution)/shard_map/all_to_all | solution.py:44
  86.0 78.7 %copy-start.12 = (s32[2,1,1024]{2,1,0:T(1,128)S(1)}, s32[2,1,1024]{2,1,0:T(1,128)}, u32[]{:S(2)}) copy-start(s32[2,1,1024]{2,1,0:T(1,128)} %param.20) | copy-start | bytes 24580
  136.9 22.1 %all-to-all-start.1 = ((f32[16,1,8192]{2,1,0:T(1,128)}), f32[16,1,8192]{2,1,0:T(1,128)S(1)}, u32[]{:S(2)}, u32[]{:S(2)}) async-start(f32[16,1,8192]{2,1,0:T(1,128)} %bitcast.9), calls=%async_computation.1 | async-start | bytes 1048576 | tf_op jit(solution)/shard_map/all_to_all | solution.py:44
  160.3 17.8 %all-to-all-start.4 = ((f32[16,1,8192]{2,1,0:T(1,128)}), f32[16,1,8192]{2,1,0:T(1,128)S(1)}, u32[]{:S(2)}, u32[]{:S(2)}) async-start(f32[16,1,8192]{2,1,0:T(1,128)} %broadcast_in_dim.12), calls=%async_computation.4 | async-start | bytes 1048576 | tf_op jit(solution)/shard_map/all_to_all | solution.py:45
  164.7 19.6 %copy-start.13 = (bf16[1024,128]{1,0:T(8,128)(2,1)S(1)}, bf16[1024,128]{1,0:T(8,128)(2,1)}, u32[]{:S(2)}) copy-start(bf16[1024,128]{1,0:T(8,128)(2,1)} %param.15) | copy-start | bytes 786436
  179.3 51.3 %all-to-all-start.2 = ((f32[16,1,8192]{2,1,0:T(1,128)}), f32[16,1,8192]{2,1,0:T(1,128)S(1)}, u32[]{:S(2)}, u32[]{:S(2)}) async-start(f32[16,1,8192]{2,1,0:T(1,128)} %broadcast_in_dim.11), calls=%async_computation.2 | async-start | bytes 1048576 | tf_op jit(solution)/shard_map/all_to_all | solution.py:45
  184.3 3.0 copy-start.6
  187.3 1.3 copy-start.7
  188.2 1.1 copy-start.5
  212.9 1.9 copy-start.1
  214.9 9.6 %copy-start.9 = (bf16[64,1024]{1,0:T(8,128)(2,1)S(1)}, bf16[64,1024]{1,0:T(8,128)(2,1)}, u32[]{:S(2)}) copy-start(bf16[64,1024]{1,0:T(8,128)(2,1)} %get-tuple-element.14) | copy-start | bytes 393220
  230.5 1.0 copy-start.14
  236.2 1.7 copy-start.8
  238.3 35.7 %copy-start.4 = (s32[32]{0:T(128)S(1)}, s32[32]{0:T(128)}, u32[]{:S(2)}) copy-start(s32[32]{0:T(128)} %squeeze.28.tiles_ref) | copy-start | bytes 388
  269.6 45.7 %all-to-all-start.6 = ((f32[16,1,17408]{2,1,0:T(1,128)}), f32[16,1,17408]{2,1,0:T(1,128)S(1)}, u32[]{:S(2)}, u32[]{:S(2)}) async-start(f32[16,1,17408]{2,1,0:T(1,128)} %broadcast_in_dim.14), calls=%async_computation.6 | async-start | bytes 2228224 | tf_op jit(solution)/shard_map/all_to_all | solution.py:45
  274.0 2.2 copy-start.2
  299.8 2.0 copy-start.3

commit v5 on v4

--- a/solution.py
+++ b/solution.py
@@ -13,7 +13,7 @@
 TS = 1024
 K = 8
 NB = 16
-CS = 256
+CS = 128
 
 
 def gelu_slope(values):
@@ -74,12 +74,11 @@
         for j in range(NB):
             here = local[j : j + 1, :].astype(jnp.bfloat16)
             cnt = cnt + jnp.where(here == local_iota, one, zero)
-        cnt = cnt * msk
-        counts_ref[0, 0, pl.ds(start, CS), :] = cnt
-        acc_ref[...] += jnp.dot(emb_ref[:, pl.ds(start, CS)], cnt, preferred_element_type=jnp.float32)
+        counts_ref[0, 0, pl.ds(start, CS), :] = cnt * msk
         return carry
 
     lax.fori_loop(0, TS // CS, chunk, 0)
+    acc_ref[...] += jnp.dot(emb_ref[...], counts_ref[0, 0], preferred_element_type=jnp.float32)
 
     @pl.when(k == k_total - 1)
     def _():

time: 323 us -> 310 us (0.960)
  Pallas kernels: 145 us -> 133 us
    pallas_call x2, Pallas kernels: 97.5 us -> 85.4 us  [aggregate(): pl.pallas_call(functools.partial(agg_kernel, agg_scale, k_total, nt), gri...]
  transfers between devices with their start and end apart: 6 -> 6, of which waited for: 2 -> 2; matrix products, arithmetic and copies ran while one was open for 20% -> 20% of each run, Pallas kernels for 45% -> 43%
where the time goes in v5:
time: 310 us; the launch traced here: 308 us
  Pallas kernels  133 us (43%)
  local copies, waits for them, and re-layouts  38.5 us (12%)
  starting transfers between devices  37.8 us (12%)
  blocking collectives  29 us (9%)
  other arithmetic  26.4 us (9%)
  matrix products  23.2 us (7%)
  waiting for transfers between devices  19.6 us (6%)
    pallas_call x2, Pallas kernels, aggregate(): pl.pallas_call(functools.partial(agg_kernel, agg_scale, k_total, nt), gri...  85.4 us
    pallas_call x2, Pallas kernels, spread(): pl.pallas_call(functools.partial(spread_kernel, agg_scale, k_total, nt),...  47.2 us
    all_to_all x1, blocking collectives, summed_over(): lax.all_to_all(flat, axis, 0, 0, tiled=True).reshape(n, -1).sum(axis=0)  29 us
    scatter-add x2, other arithmetic, local(): table_grad = table_grad.at[dest_rows[m]].add(own_grad)  19.1 us
    all_to_all x2, starting transfers between devices, summed_over(): lax.all_to_all(flat, axis, 0, 0, tiled=True).reshape(n, -1).sum(axis=0)  15.1 us
    all_to_all x2, waiting for transfers between devices, summed_over(): lax.all_to_all(flat, axis, 0, 0, tiled=True).reshape(n, -1).sum(axis=0)  14.2 us
    all_to_all x3, starting transfers between devices, summed_over(): lax.all_to_all(jnp.broadcast_to(mine[None], (n, mine.size)), axis, 0, 0,...  12.6 us
    unnamed x33, local copies, waits for them, and re-layouts  12.3 us
  transfers between devices with their start and end apart: 6, of which 2 were waited for; matrix products, arithmetic and copies ran while one was open for 20% of the time, Pallas kernels for 43%

profile of v5, /device:TPU:1, one launch (start us, length us, event | category | flops | bytes accessed | tf_op | source)
XLA Modules:
  0.0 308.3 jit_solution(4578850483221939653)
XLA Ops:
  2.4 10.1 %all-to-all-start = ((bf16[16,2,64,128]{3,2,1,0:T(8,128)(2,1)}), bf16[16,2,64,128]{3,2,1,0:T(8,128)(2,1)}, u32[]{:S(2)}, u32[]{:S(2)}) async-start(bf16[16,2,64,128]{3,2,1,0:T(8,128)(2,1)} %broadcast_in_dim.10), calls=%async_computation | async-start | bytes 1048576 | tf_op jit(solution)/shard_map/all_to_all | solution.py:51
  16.1 2.0 copy.77
  18.2 3.2 %gather_fusion.1 = bf16[1024,64]{1,0:T(8,128)(2,1)S(1)} fusion(bf16[8192,64]{1,0:T(8,128)(2,1)S(1)} %bitcast.81, s32[1024]{0:T(1024)S(1)} %broadcast_clamp_fusion), kind=kCustom, calls=%fused_computation.1 | custom fusion | bytes 266240 | tf_op jit(solution)/shard_map/gather | solution.py:196
  21.4 2.3 slice_bitcast_fusion
  23.7 42.6 %shard_map.147 = (bf16[8,4,1024,256]{3,2,1,0:T(8,128)(2,1)}, bf16[64,1024]{1,0:T(8,128)(2,1)}) custom-call(s32[32]{0:T(128)} %squeeze.32.tiles_ref, bf16[64,8192]{1,0:T(8,128)(2,1)} %emb_ref.3, s32[8,1,16,1024]{3,2,1,0:T(8,128)} %get-tuple-element.49.rows_ref, s32[8,1,1,1024]{3,2,1,0:T(1,128)} %get-tuple-element.62.mask_ref), custom_call_target="tpu_custom_call" | custom-call | flops 1610612736 | bytes 17825792 | tf_op jit(solution)/shard_map/pallas_call | solution.py:109
  66.6 2.0 convolution_add_fusion
  68.5 7.5 %all-to-all-start.3 = ((f32[16,1,8192]{2,1,0:T(1,128)}), f32[16,1,8192]{2,1,0:T(1,128)S(1)}, u32[]{:S(2)}, u32[]{:S(2)}) async-start(f32[16,1,8192]{2,1,0:T(1,128)} %bitcast.93), calls=%async_computation.3 | async-start | bytes 1048576 | tf_op jit(solution)/shard_map/all_to_all | solution.py:44
  76.7 3.2 %gather_fusion = bf16[1024,64]{1,0:T(8,128)(2,1)S(1)} fusion(bf16[8192,64]{1,0:T(8,128)(2,1)S(1)} %bitcast.82, s32[1024]{0:T(1024)S(1)} %broadcast_clamp_fusion.1), kind=kCustom, calls=%fused_computation | custom fusion | bytes 266240 | tf_op jit(solution)/shard_map/gather | solution.py:196
  80.0 42.7 %shard_map.146 = (bf16[8,4,1024,256]{3,2,1,0:T(8,128)(2,1)}, bf16[64,1024]{1,0:T(8,128)(2,1)}) custom-call(s32[32]{0:T(128)} %squeeze.28.tiles_ref, bf16[64,8192]{1,0:T(8,128)(2,1)} %emb_ref.3, s32[8,1,16,1024]{3,2,1,0:T(8,128)} %get-tuple-element.50.rows_ref, s32[8,1,1,1024]{3,2,1,0:T(1,128)} %get-tuple-element.61.mask_ref), custom_call_target="tpu_custom_call" | custom-call | flops 1610612736 | bytes 17825792 | tf_op jit(solution)/shard_map/pallas_call | solution.py:109
  122.9 2.0 convolution_add_fusion.1
  124.9 7.6 %all-to-all-start.1 = ((f32[16,1,8192]{2,1,0:T(1,128)}), f32[16,1,8192]{2,1,0:T(1,128)S(1)}, u32[]{:S(2)}, u32[]{:S(2)}) async-start(f32[16,1,8192]{2,1,0:T(1,128)} %bitcast.9), calls=%async_computation.1 | async-start | bytes 1048576 | tf_op jit(solution)/shard_map/all_to_all | solution.py:44
  132.8 14.2 %all-to-all-done.1 = f32[16,1,8192]{2,1,0:T(1,128)S(1)} async-done(((f32[16,1,8192]{2,1,0:T(1,128)}), f32[16,1,8192]{2,1,0:T(1,128)S(1)}, u32[]{:S(2)}, u32[]{:S(2)}) %all-to-all-start.1) | async-done | bytes 524320 | tf_op jit(solution)/shard_map/all_to_all | solution.py:44
  148.2 4.4 %all-to-all-start.4 = ((f32[16,1,8192]{2,1,0:T(1,128)}), f32[16,1,8192]{2,1,0:T(1,128)S(1)}, u32[]{:S(2)}, u32[]{:S(2)}) async-start(f32[16,1,8192]{2,1,0:T(1,128)} %broadcast_in_dim.12), calls=%async_computation.4 | async-start | bytes 1048576 | tf_op jit(solution)/shard_map/all_to_all | solution.py:45
  153.8 3.2 %scatter_custom_fusion = bf16[1024,128]{1,0:T(8,128)(2,1)S(1)} fusion(s32[1024]{0:T(1024)S(1)} %bitcast.101, bf16[1024,128]{1,0:T(8,128)(2,1)S(1)} %bitcast.95, bf16[]{:T(256)} %constant.12.clone.1), kind=kCustom, calls=%fused_computation.71 | custom fusion | bytes 262146 | tf_op jit(solution)/shard_map/scatter | solution.py:216
  157.0 3.2 %scatter_custom_fusion.1 = bf16[1024,128]{1,0:T(8,128)(2,1)S(1)} fusion(s32[1024]{0:T(1024)S(1)} %bitcast.100, bf16[1024,128]{1,0:T(8,128)(2,1)S(1)} %bitcast.94, bf16[]{:T(256)} %constant.12.clone.1), kind=kCustom, calls=%fused_computation.69 | custom fusion | bytes 262146 | tf_op jit(solution)/shard_map/scatter | solution.py:216
  160.6 5.4 %all-to-all-done.4 = f32[16,1,8192]{2,1,0:T(1,128)S(1)} async-done(((f32[16,1,8192]{2,1,0:T(1,128)}), f32[16,1,8192]{2,1,0:T(1,128)S(1)}, u32[]{:S(2)}, u32[]{:S(2)}) %all-to-all-start.4) | async-done | bytes 524320 | tf_op jit(solution)/shard_map/all_to_all | solution.py:45
  167.2 4.3 %all-to-all-start.2 = ((f32[16,1,8192]{2,1,0:T(1,128)}), f32[16,1,8192]{2,1,0:T(1,128)S(1)}, u32[]{:S(2)}, u32[]{:S(2)}) async-start(f32[16,1,8192]{2,1,0:T(1,128)} %broadcast_in_dim.11), calls=%async_computation.2 | async-start | bytes 1048576 | tf_op jit(solution)/shard_map/all_to_all | solution.py:45
  172.2 3.0 fusion.7
  177.2 23.6 %shard_map.148 = f32[8192,64]{1,0:T(8,128)S(1)} custom-call(s32[32]{0:T(128)S(1)} %copy-done.5, bf16[8,4,1024,256]{3,2,1,0:T(8,128)(2,1)} %get-tuple-element.13.counts_ref, bf16[1024,64]{1,0:T(8,128)(2,1)S(1)} %copy.83.back_ref, f32[8192,64]{1,0:T(8,128)S(1)} %broadcast_in_dim.13.clone.tg_in_ref), custom_call_target="tpu_custom_call", output_to_operand_aliasing={{}: (3, {})} | custom-call | flops 1073741824 | bytes 20971520 | tf_op jit(solution)/shard_map/pallas_call | solution.py:153
  200.9 1.9 copy-done.1
  202.8 9.6 %scatter_fusion = f32[8192,64]{1,0:T(8,128)} fusion(f32[8192,64]{1,0:T(8,128)} %copy-done.1, s32[1024]{0:T(1024)S(1)} %bitcast.99, f32[1024,64]{1,0:T(8,128)S(1)} %fusion.57), kind=kCustom, calls=%fused_computation.4 | custom fusion | flops 65536 | bytes 790528 | tf_op jit(solution)/shard_map/scatter-add | solution.py:226
  212.6 2.2 fusion.49
  214.8 3.7 %fusion.16 = f32[1024,128]{1,0:T(8,128)S(1)} fusion(bf16[1024,128]{1,0:T(8,128)(2,1)S(1)} %scatter_custom_fusion.1, f32[1024,1024]{1,0:T(8,128)} %copy-done.6), kind=kOutput, calls=%fused_computation.28 | convolution fusion | flops 277872640 | bytes 4980736 | tf_op jit(solution)/shard_map/dot_general | solution.py:30
  219.4 3.0 fusion.15
  226.2 29.0 %all_to_all.50 = f32[16,1,17408]{2,1,0:T(1,128)S(1)} all-to-all(f32[16,1,17408]{2,1,0:T(1,128)S(1)} %bitcast.91), channel_id=1, replica_groups=mesh['batch'=16,'feat'=16] {'batch'}, dimensions={0} | all-to-all | bytes 2228224 | tf_op jit(solution)/shard_map/all_to_all | solution.py:44
  257.6 3.9 %all-to-all-start.6 = ((f32[16,1,17408]{2,1,0:T(1,128)}), f32[16,1,17408]{2,1,0:T(1,128)S(1)}, u32[]{:S(2)}, u32[]{:S(2)}) async-start(f32[16,1,17408]{2,1,0:T(1,128)} %broadcast_in_dim.14), calls=%async_computation.6 | async-start | bytes 2228224 | tf_op jit(solution)/shard_map/all_to_all | solution.py:45
  261.9 2.2 copy-done.2
  264.1 23.6 %shard_map.149 = f32[8192,64]{1,0:T(8,128)S(1)} custom-call(s32[32]{0:T(128)S(1)} %copy-done.4, bf16[8,4,1024,256]{3,2,1,0:T(8,128)(2,1)} %get-tuple-element.11.counts_ref, bf16[1024,64]{1,0:T(8,128)(2,1)S(1)} %copy.85.back_ref, f32[8192,64]{1,0:T(8,128)S(1)} %copy-done.2), custom_call_target="tpu_custom_call", output_to_operand_aliasing={{}: (3, {})} | custom-call | flops 1073741824 | bytes 20971520 | tf_op jit(solution)/shard_map/pallas_call | solution.py:153
  287.7 1.9 copy-done.3
  289.9 9.6 %scatter_fusion.1 = f32[8192,64]{1,0:T(8,128)} fusion(f32[8192,64]{1,0:T(8,128)} %copy-done.3, s32[1024]{0:T(1024)S(1)} %bitcast.97, f32[1024,64]{1,0:T(8,128)S(1)} %fusion.58), kind=kCustom, calls=%fused_computation.5 | custom fusion | flops 65536 | bytes 790528 | tf_op jit(solution)/shard_map/scatter-add | solution.py:243
  299.4 3.8 %copy.88 = f32[64,8192]{1,0:T(8,128)} copy(f32[64,8192]{0,1:T(8,128)} %bitcast.80) | data formatting | bytes 4194304
  304.7 2.6 reduce.3
  (75 shorter events, 23.6 us)
Async XLA Ops:
  0.6 170.9 %copy-start = (bf16[128,1024]{1,0:T(8,128)(2,1)S(1)}, bf16[128,1024]{1,0:T(8,128)(2,1)}, u32[]{:S(2)}) copy-start(bf16[128,1024]{1,0:T(8,128)(2,1)} %param.14) | copy-start | bytes 786436
  2.4 66.2 %all-to-all-start = ((bf16[16,2,64,128]{3,2,1,0:T(8,128)(2,1)}), bf16[16,2,64,128]{3,2,1,0:T(8,128)(2,1)}, u32[]{:S(2)}, u32[]{:S(2)}) async-start(bf16[16,2,64,128]{3,2,1,0:T(8,128)(2,1)} %broadcast_in_dim.10), calls=%async_computation | async-start | bytes 1048576 | tf_op jit(solution)/shard_map/all_to_all | solution.py:51
  21.4 44.9 %copy-start.11 = (bf16[64,128]{1,0:T(8,128)(2,1)S(1)}, bf16[64,128]{1,0:T(8,128)(2,1)}, u32[]{:S(2)}) copy-start(bf16[64,128]{1,0:T(8,128)(2,1)} %param.12) | copy-start | bytes 49156
  21.4 45.1 %copy-start.10 = (bf16[64,128]{1,0:T(8,128)(2,1)S(1)}, bf16[64,128]{1,0:T(8,128)(2,1)}, u32[]{:S(2)}) copy-start(bf16[64,128]{1,0:T(8,128)(2,1)} %param.13) | copy-start | bytes 49156
  68.5 56.3 %all-to-all-start.3 = ((f32[16,1,8192]{2,1,0:T(1,128)}), f32[16,1,8192]{2,1,0:T(1,128)S(1)}, u32[]{:S(2)}, u32[]{:S(2)}) async-start(f32[16,1,8192]{2,1,0:T(1,128)} %bitcast.93), calls=%async_computation.3 | async-start | bytes 1048576 | tf_op jit(solution)/shard_map/all_to_all | solution.py:44
  79.9 72.7 %copy-start.12 = (s32[2,1,1024]{2,1,0:T(1,128)S(1)}, s32[2,1,1024]{2,1,0:T(1,128)}, u32[]{:S(2)}) copy-start(s32[2,1,1024]{2,1,0:T(1,128)} %param.20) | copy-start | bytes 24580
  124.9 22.1 %all-to-all-start.1 = ((f32[16,1,8192]{2,1,0:T(1,128)}), f32[16,1,8192]{2,1,0:T(1,128)S(1)}, u32[]{:S(2)}, u32[]{:S(2)}) async-start(f32[16,1,8192]{2,1,0:T(1,128)} %bitcast.9), calls=%async_computation.1 | async-start | bytes 1048576 | tf_op jit(solution)/shard_map/all_to_all | solution.py:44
  148.2 17.8 %all-to-all-start.4 = ((f32[16,1,8192]{2,1,0:T(1,128)}), f32[16,1,8192]{2,1,0:T(1,128)S(1)}, u32[]{:S(2)}, u32[]{:S(2)}) async-start(f32[16,1,8192]{2,1,0:T(1,128)} %broadcast_in_dim.12), calls=%async_computation.4 | async-start | bytes 1048576 | tf_op jit(solution)/shard_map/all_to_all | solution.py:45
  152.7 19.6 %copy-start.13 = (bf16[1024,128]{1,0:T(8,128)(2,1)S(1)}, bf16[1024,128]{1,0:T(8,128)(2,1)}, u32[]{:S(2)}) copy-start(bf16[1024,128]{1,0:T(8,128)(2,1)} %param.15) | copy-start | bytes 786436
  167.2 51.3 %all-to-all-start.2 = ((f32[16,1,8192]{2,1,0:T(1,128)}), f32[16,1,8192]{2,1,0:T(1,128)S(1)}, u32[]{:S(2)}, u32[]{:S(2)}) async-start(f32[16,1,8192]{2,1,0:T(1,128)} %broadcast_in_dim.11), calls=%async_computation.2 | async-start | bytes 1048576 | tf_op jit(solution)/shard_map/all_to_all | solution.py:45
  172.2 3.0 copy-start.6
  175.2 1.3 copy-start.7
  176.1 1.1 copy-start.5
  200.9 1.9 copy-start.1
  202.8 9.6 %copy-start.9 = (bf16[64,1024]{1,0:T(8,128)(2,1)S(1)}, bf16[64,1024]{1,0:T(8,128)(2,1)}, u32[]{:S(2)}) copy-start(bf16[64,1024]{1,0:T(8,128)(2,1)} %get-tuple-element.14) | copy-start | bytes 393220
  218.4 1.0 copy-start.14
  224.2 1.7 copy-start.8
  226.2 35.7 %copy-start.4 = (s32[32]{0:T(128)S(1)}, s32[32]{0:T(128)}, u32[]{:S(2)}) copy-start(s32[32]{0:T(128)} %squeeze.28.tiles_ref) | copy-start | bytes 388
  257.6 45.7 %all-to-all-start.6 = ((f32[16,1,17408]{2,1,0:T(1,128)}), f32[16,1,17408]{2,1,0:T(1,128)S(1)}, u32[]{:S(2)}, u32[]{:S(2)}) async-start(f32[16,1,17408]{2,1,0:T(1,128)} %broadcast_in_dim.14), calls=%async_computation.6 | async-start | bytes 2228224 | tf_op jit(solution)/shard_map/all_to_all | solution.py:45
  261.9 2.2 copy-start.2
  287.7 2.0 copy-start.3

commit v6 on v5

--- a/solution.py
+++ b/solution.py
@@ -14,6 +14,7 @@
 K = 8
 NB = 16
 CS = 128
+MESH = pl.DeviceIdType.MESH
 
 
 def gelu_slope(values):
@@ -44,6 +45,65 @@
     mine = lax.all_to_all(flat, axis, 0, 0, tiled=True).reshape(n, -1).sum(axis=0)
     spread_back = lax.all_to_all(jnp.broadcast_to(mine[None], (n, mine.size)), axis, 0, 0, tiled=True)
     return spread_back.reshape(x.shape)
+
+
+def exchange_kernel(axis, n, x_ref, out_ref, recv_ref, send1, recv1, send2, recv2):
+    me = lax.axis_index(axis)
+    other = lax.axis_index("feat" if axis == "batch" else "batch")
+
+    def dev(j):
+        return (j, other) if axis == "batch" else (other, j)
+
+    barrier = pltpu.get_barrier_semaphore()
+    for d in range(1, n):
+        pl.semaphore_signal(barrier, inc=1, device_id=dev(lax.rem(me + d, n)), device_id_type=MESH)
+    pl.semaphore_wait(barrier, n - 1)
+
+    def link(src, dst, send, recv, peer):
+        return pltpu.make_async_remote_copy(
+            src_ref=src, dst_ref=dst, send_sem=send, recv_sem=recv, device_id=dev(peer), device_id_type=MESH
+        )
+
+    for d in range(1, n):
+        peer = lax.rem(me + d, n)
+        link(x_ref.at[peer], recv_ref.at[me], send1.at[d], recv1.at[me], peer).start()
+    for d in range(1, n):
+        peer = lax.rem(me + d, n)
+        src = lax.rem(me + n - d, n)
+        link(x_ref.at[peer], recv_ref.at[me], send1.at[d], recv1.at[me], peer).wait_send()
+        link(x_ref.at[src], recv_ref.at[src], send1.at[d], recv1.at[src], src).wait_recv()
+    acc = x_ref[me]
+    for d in range(1, n):
+        acc = acc + recv_ref[lax.rem(me + n - d, n)]
+    out_ref[me] = acc
+    for d in range(1, n):
+        peer = lax.rem(me + d, n)
+        link(out_ref.at[me], out_ref.at[me], send2.at[d], recv2.at[me], peer).start()
+    for d in range(1, n):
+        peer = lax.rem(me + d, n)
+        src = lax.rem(me + n - d, n)
+        link(out_ref.at[me], out_ref.at[me], send2.at[d], recv2.at[me], peer).wait_send()
+        link(out_ref.at[src], out_ref.at[src], send2.at[d], recv2.at[src], src).wait_recv()
+
+
+def summed_by_kernel(x, axis, collective_id):
+    n = lax.axis_size(axis)
+    pieces = x.reshape(n, -1, 128)
+    out = pl.pallas_call(
+        functools.partial(exchange_kernel, axis, n),
+        out_shape=jax.ShapeDtypeStruct(pieces.shape, pieces.dtype),
+        in_specs=[pl.BlockSpec(memory_space=pltpu.VMEM)],
+        out_specs=pl.BlockSpec(memory_space=pltpu.VMEM),
+        scratch_shapes=[
+            pltpu.VMEM(pieces.shape, pieces.dtype),
+            pltpu.SemaphoreType.DMA((n,)),
+            pltpu.SemaphoreType.DMA((n,)),
+            pltpu.SemaphoreType.DMA((n,)),
+            pltpu.SemaphoreType.DMA((n,)),
+        ],
+        compiler_params=pltpu.CompilerParams(collective_id=collective_id, has_side_effects=True),
+    )(pieces)
+    return out.reshape(x.shape)
 
 
 def gathered_over(x, axis, dim):
@@ -229,7 +289,7 @@
 
     sizes = [up_sum.size, down_sum.size, self_sum.size, neighbor_sum.size]
     line = jnp.concatenate([up_sum.ravel(), down_sum.ravel(), self_sum.ravel(), neighbor_sum.ravel()])
-    line = summed_over(line, "batch")
+    line = summed_by_kernel(line, "batch", 0)
     ends = [0]
     for s in sizes:
         ends.append(ends[-1] + s)

time: 310 us -> 320 us (1.032)
  Pallas kernels: 133 us -> 175 us
  blocking collectives: 29 us -> 0 us
  starting transfers between devices: 37.8 us -> 34 us
    pallas_call x0 -> x1, Pallas kernels: none -> 42.1 us  [summed_by_kernel(): pl.pallas_call(functools.partial(exchange_kernel, axis, n), out_shape=jax...]
    all_to_all x1 -> x0, blocking collectives: 29 us -> none  [summed_over(): lax.all_to_all(flat, axis, 0, 0, tiled=True).reshape(n, -1).sum(axis=0)]
    all_to_all x3 -> x2, starting transfers between devices: 12.6 us -> 8.84 us  [summed_over(): lax.all_to_all(jnp.broadcast_to(mine[None], (n, mine.size)), axis, 0, 0,...]
    all_to_all x3 -> x2, waiting for transfers between devices: 5.39 us -> 6.43 us  [summed_over(): lax.all_to_all(jnp.broadcast_to(mine[None], (n, mine.size)), axis, 0, 0,...]
    unnamed x33 -> x39, local copies, waits for them, and re-layouts: 12.3 us -> 13.1 us
  transfers between devices with their start and end apart: 6 -> 5, of which waited for: 2 -> 2; matrix products, arithmetic and copies ran while one was open for 20% -> 15% of each run, Pallas kernels for 43% -> 34%
where the time goes in v6:
time: 320 us; the launch traced here: 318 us
  Pallas kernels  175 us (55%)
  local copies, waits for them, and re-layouts  38 us (12%)
  starting transfers between devices  34 us (11%)
  other arithmetic  25.8 us (8%)
  matrix products  24 us (8%)
  waiting for transfers between devices  20.5 us (6%)
    pallas_call x2, Pallas kernels, aggregate(): pl.pallas_call(functools.partial(agg_kernel, agg_scale, k_total, nt), gri...  85.4 us
    pallas_call x2, Pallas kernels, spread(): pl.pallas_call(functools.partial(spread_kernel, agg_scale, k_total, nt),...  47.2 us
    pallas_call x1, Pallas kernels, summed_by_kernel(): pl.pallas_call(functools.partial(exchange_kernel, axis, n), out_shape=jax...  42.1 us
    scatter-add x2, other arithmetic, local(): table_grad = table_grad.at[dest_rows[m]].add(own_grad)  19.1 us
    all_to_all x2, starting transfers between devices, summed_over(): lax.all_to_all(flat, axis, 0, 0, tiled=True).reshape(n, -1).sum(axis=0)  15.1 us
    all_to_all x2, waiting for transfers between devices, summed_over(): lax.all_to_all(flat, axis, 0, 0, tiled=True).reshape(n, -1).sum(axis=0)  14.1 us
    unnamed x39, local copies, waits for them, and re-layouts  13.1 us
    all_to_all x1, starting transfers between devices, gathered_over(): lax.all_to_all(jnp.broadcast_to(x[None], (n, *x.shape)), axis, 0, 0, tile...  10 us
  transfers between devices with their start and end apart: 5, of which 2 were waited for; matrix products, arithmetic and copies ran while one was open for 15% of the time, Pallas kernels for 34%

profile of v6, /device:TPU:1, one launch (start us, length us, event | category | flops | bytes accessed | tf_op | source)
XLA Modules:
  0.0 318.1 jit_solution(2910810789397406322)
XLA Ops:
  2.4 10.0 %all-to-all-start = ((bf16[16,2,64,128]{3,2,1,0:T(8,128)(2,1)}), bf16[16,2,64,128]{3,2,1,0:T(8,128)(2,1)S(1)}, u32[]{:S(2)}, u32[]{:S(2)}) async-start(bf16[16,2,64,128]{3,2,1,0:T(8,128)(2,1)} %broadcast_in_dim.8), calls=%async_computation | async-start | bytes 1048576 | tf_op jit(solution)/shard_map/all_to_all | solution.py:111
  16.1 2.0 copy.52
  18.2 3.2 %gather_fusion.1 = bf16[1024,64]{1,0:T(8,128)(2,1)S(1)} fusion(bf16[8192,64]{1,0:T(8,128)(2,1)S(1)} %bitcast.81, s32[1024]{0:T(1024)S(1)} %broadcast_clamp_fusion), kind=kCustom, calls=%fused_computation.1 | custom fusion | bytes 266240 | tf_op jit(solution)/shard_map/gather | solution.py:256
  21.4 2.3 slice_bitcast_fusion
  23.7 42.6 %shard_map.147 = (bf16[8,4,1024,256]{3,2,1,0:T(8,128)(2,1)}, bf16[64,1024]{1,0:T(8,128)(2,1)}) custom-call(s32[32]{0:T(128)} %squeeze.32.tiles_ref, bf16[64,8192]{1,0:T(8,128)(2,1)} %emb_ref.3, s32[8,1,16,1024]{3,2,1,0:T(8,128)} %get-tuple-element.39.rows_ref, s32[8,1,1,1024]{3,2,1,0:T(1,128)} %get-tuple-element.51.mask_ref), custom_call_target="tpu_custom_call" | custom-call | flops 1610612736 | bytes 17825792 | tf_op jit(solution)/shard_map/pallas_call | solution.py:169
  66.5 2.0 convolution_add_fusion
  69.3 7.6 %all-to-all-start.3 = ((f32[16,1,8192]{2,1,0:T(1,128)}), f32[16,1,8192]{2,1,0:T(1,128)S(1)}, u32[]{:S(2)}, u32[]{:S(2)}) async-start(f32[16,1,8192]{2,1,0:T(1,128)} %bitcast.93), calls=%async_computation.3 | async-start | bytes 1048576 | tf_op jit(solution)/shard_map/all_to_all | solution.py:45
  77.5 3.2 %gather_fusion = bf16[1024,64]{1,0:T(8,128)(2,1)S(1)} fusion(bf16[8192,64]{1,0:T(8,128)(2,1)S(1)} %bitcast.82, s32[1024]{0:T(1024)S(1)} %broadcast_clamp_fusion.1), kind=kCustom, calls=%fused_computation | custom fusion | bytes 266240 | tf_op jit(solution)/shard_map/gather | solution.py:256
  80.8 42.7 %shard_map.146 = (bf16[8,4,1024,256]{3,2,1,0:T(8,128)(2,1)}, bf16[64,1024]{1,0:T(8,128)(2,1)}) custom-call(s32[32]{0:T(128)} %squeeze.28.tiles_ref, bf16[64,8192]{1,0:T(8,128)(2,1)} %emb_ref.3, s32[8,1,16,1024]{3,2,1,0:T(8,128)} %get-tuple-element.40.rows_ref, s32[8,1,1,1024]{3,2,1,0:T(1,128)} %get-tuple-element.52.mask_ref), custom_call_target="tpu_custom_call" | custom-call | flops 1610612736 | bytes 17825792 | tf_op jit(solution)/shard_map/pallas_call | solution.py:169
  123.7 2.0 convolution_add_fusion.1
  125.7 7.6 %all-to-all-start.1 = ((f32[16,1,8192]{2,1,0:T(1,128)}), f32[16,1,8192]{2,1,0:T(1,128)S(1)}, u32[]{:S(2)}, u32[]{:S(2)}) async-start(f32[16,1,8192]{2,1,0:T(1,128)} %bitcast.9), calls=%async_computation.1 | async-start | bytes 1048576 | tf_op jit(solution)/shard_map/all_to_all | solution.py:45
  133.6 14.1 %all-to-all-done.1 = f32[16,1,8192]{2,1,0:T(1,128)S(1)} async-done(((f32[16,1,8192]{2,1,0:T(1,128)}), f32[16,1,8192]{2,1,0:T(1,128)S(1)}, u32[]{:S(2)}, u32[]{:S(2)}) %all-to-all-start.1) | async-done | bytes 524320 | tf_op jit(solution)/shard_map/all_to_all | solution.py:45
  148.8 4.5 %all-to-all-start.4 = ((f32[16,1,8192]{2,1,0:T(1,128)}), f32[16,1,8192]{2,1,0:T(1,128)S(1)}, u32[]{:S(2)}, u32[]{:S(2)}) async-start(f32[16,1,8192]{2,1,0:T(1,128)} %broadcast_in_dim.10), calls=%async_computation.4 | async-start | bytes 1048576 | tf_op jit(solution)/shard_map/all_to_all | solution.py:46
  153.5 3.2 %scatter_custom_fusion = bf16[1024,128]{1,0:T(8,128)(2,1)S(1)} fusion(s32[1024]{0:T(1024)S(1)} %bitcast.102, bf16[1024,128]{1,0:T(8,128)(2,1)S(1)} %bitcast.96, bf16[]{:T(256)} %constant.12.clone.1), kind=kCustom, calls=%fused_computation.71 | custom fusion | bytes 262146 | tf_op jit(solution)/shard_map/scatter | solution.py:276
  156.7 3.2 %scatter_custom_fusion.1 = bf16[1024,128]{1,0:T(8,128)(2,1)S(1)} fusion(s32[1024]{0:T(1024)S(1)} %bitcast.101, bf16[1024,128]{1,0:T(8,128)(2,1)S(1)} %bitcast.95, bf16[]{:T(256)} %constant.12.clone.1), kind=kCustom, calls=%fused_computation.69 | custom fusion | bytes 262146 | tf_op jit(solution)/shard_map/scatter | solution.py:276
  160.3 6.4 %all-to-all-done.4 = f32[16,1,8192]{2,1,0:T(1,128)S(1)} async-done(((f32[16,1,8192]{2,1,0:T(1,128)}), f32[16,1,8192]{2,1,0:T(1,128)S(1)}, u32[]{:S(2)}, u32[]{:S(2)}) %all-to-all-start.4) | async-done | bytes 524320 | tf_op jit(solution)/shard_map/all_to_all | solution.py:46
  167.9 4.3 %all-to-all-start.2 = ((f32[16,1,8192]{2,1,0:T(1,128)}), f32[16,1,8192]{2,1,0:T(1,128)S(1)}, u32[]{:S(2)}, u32[]{:S(2)}) async-start(f32[16,1,8192]{2,1,0:T(1,128)} %broadcast_in_dim.9), calls=%async_computation.2 | async-start | bytes 1048576 | tf_op jit(solution)/shard_map/all_to_all | solution.py:46
  173.0 3.0 fusion.7
  178.0 23.5 %shard_map.148 = f32[8192,64]{1,0:T(8,128)S(1)} custom-call(s32[32]{0:T(128)S(1)} %copy-done.5, bf16[8,4,1024,256]{3,2,1,0:T(8,128)(2,1)} %get-tuple-element.13.counts_ref, bf16[1024,64]{1,0:T(8,128)(2,1)S(1)} %copy.58.back_ref, f32[8192,64]{1,0:T(8,128)S(1)} %broadcast_in_dim.11.clone.tg_in_ref), custom_call_target="tpu_custom_call", output_to_operand_aliasing={{}: (3, {})} | custom-call | flops 1073741824 | bytes 20971520 | tf_op jit(solution)/shard_map/pallas_call | solution.py:213
  201.6 1.9 copy-done.1
  203.5 9.6 %scatter_fusion = f32[8192,64]{1,0:T(8,128)} fusion(f32[8192,64]{1,0:T(8,128)} %copy-done.1, s32[1024]{0:T(1024)S(1)} %bitcast.100, f32[1024,64]{1,0:T(8,128)S(1)} %fusion.57), kind=kCustom, calls=%fused_computation.4 | custom fusion | flops 65536 | bytes 790528 | tf_op jit(solution)/shard_map/scatter-add | solution.py:286
  213.2 2.2 fusion.49
  215.4 4.5 %fusion.16 = f32[1024,128]{1,0:T(8,128)} fusion(bf16[1024,128]{1,0:T(8,128)(2,1)S(1)} %scatter_custom_fusion.1, f32[1024,1024]{1,0:T(8,128)} %copy-done.6), kind=kOutput, calls=%fused_computation.28 | convolution fusion | flops 277872640 | bytes 4980736 | tf_op jit(solution)/shard_map/dot_general | solution.py:31
  220.9 3.0 fusion.15
  225.1 1.7 fusion.19
  229.1 42.1 %shard_map.150 = f32[16,136,128]{2,1,0:T(8,128)} custom-call(f32[16,136,128]{2,1,0:T(8,128)} %bitcast.91), custom_call_target="tpu_custom_call" | custom-call | tf_op jit(solution)/shard_map/pallas_call | solution.py:92
  272.6 1.9 slice_multiply_fusion
  276.2 2.2 copy-done.2
  278.3 23.6 %shard_map.149 = f32[8192,64]{1,0:T(8,128)S(1)} custom-call(s32[32]{0:T(128)S(1)} %copy-done.4, bf16[8,4,1024,256]{3,2,1,0:T(8,128)(2,1)} %get-tuple-element.11.counts_ref, bf16[1024,64]{1,0:T(8,128)(2,1)S(1)} %copy.60.back_ref, f32[8192,64]{1,0:T(8,128)S(1)} %copy-done.2), custom_call_target="tpu_custom_call", output_to_operand_aliasing={{}: (3, {})} | custom-call | flops 1073741824 | bytes 20971520 | tf_op jit(solution)/shard_map/pallas_call | solution.py:213
  302.0 1.9 copy-done.3
  303.9 9.5 %scatter_fusion.1 = f32[8192,64]{1,0:T(8,128)} fusion(f32[8192,64]{1,0:T(8,128)} %copy-done.3, s32[1024]{0:T(1024)S(1)} %bitcast.98, f32[1024,64]{1,0:T(8,128)S(1)} %fusion.58), kind=kCustom, calls=%fused_computation.5 | custom fusion | flops 65536 | bytes 790528 | tf_op jit(solution)/shard_map/scatter-add | solution.py:303
  313.4 3.8 %copy.62 = f32[64,8192]{1,0:T(8,128)} copy(f32[64,8192]{0,1:T(8,128)} %bitcast.80) | data formatting | bytes 4194304
  (76 shorter events, 21.6 us)
Async XLA Ops:
  0.6 171.6 %copy-start = (bf16[128,1024]{1,0:T(8,128)(2,1)S(1)}, bf16[128,1024]{1,0:T(8,128)(2,1)}, u32[]{:S(2)}) copy-start(bf16[128,1024]{1,0:T(8,128)(2,1)} %param.14) | copy-start | bytes 786436
  2.4 66.1 %all-to-all-start = ((bf16[16,2,64,128]{3,2,1,0:T(8,128)(2,1)}), bf16[16,2,64,128]{3,2,1,0:T(8,128)(2,1)S(1)}, u32[]{:S(2)}, u32[]{:S(2)}) async-start(bf16[16,2,64,128]{3,2,1,0:T(8,128)(2,1)} %broadcast_in_dim.8), calls=%async_computation | async-start | bytes 1048576 | tf_op jit(solution)/shard_map/all_to_all | solution.py:111
  21.4 44.9 %copy-start.13 = (bf16[64,128]{1,0:T(8,128)(2,1)S(1)}, bf16[64,128]{1,0:T(8,128)(2,1)}, u32[]{:S(2)}) copy-start(bf16[64,128]{1,0:T(8,128)(2,1)} %param.12) | copy-start | bytes 49156
  21.4 45.1 %copy-start.12 = (bf16[64,128]{1,0:T(8,128)(2,1)S(1)}, bf16[64,128]{1,0:T(8,128)(2,1)}, u32[]{:S(2)}) copy-start(bf16[64,128]{1,0:T(8,128)(2,1)} %param.13) | copy-start | bytes 49156
  68.5 0.8 copy-start.8
  69.3 56.4 %all-to-all-start.3 = ((f32[16,1,8192]{2,1,0:T(1,128)}), f32[16,1,8192]{2,1,0:T(1,128)S(1)}, u32[]{:S(2)}, u32[]{:S(2)}) async-start(f32[16,1,8192]{2,1,0:T(1,128)} %bitcast.93), calls=%async_computation.3 | async-start | bytes 1048576 | tf_op jit(solution)/shard_map/all_to_all | solution.py:45
  80.7 72.7 %copy-start.14 = (s32[2,1,1024]{2,1,0:T(1,128)S(1)}, s32[2,1,1024]{2,1,0:T(1,128)}, u32[]{:S(2)}) copy-start(s32[2,1,1024]{2,1,0:T(1,128)} %param.20) | copy-start | bytes 24580
  80.7 72.7 %copy-start.9 = (bf16[16,2,64,128]{3,2,1,0:T(8,128)(2,1)S(1)}, bf16[16,2,64,128]{3,2,1,0:T(8,128)(2,1)}, u32[]{:S(2)}) copy-start(bf16[16,2,64,128]{3,2,1,0:T(8,128)(2,1)} %copy-done.8) | copy-start | bytes 1572868
  125.7 22.0 %all-to-all-start.1 = ((f32[16,1,8192]{2,1,0:T(1,128)}), f32[16,1,8192]{2,1,0:T(1,128)S(1)}, u32[]{:S(2)}, u32[]{:S(2)}) async-start(f32[16,1,8192]{2,1,0:T(1,128)} %bitcast.9), calls=%async_computation.1 | async-start | bytes 1048576 | tf_op jit(solution)/shard_map/all_to_all | solution.py:45
  148.8 17.9 %all-to-all-start.4 = ((f32[16,1,8192]{2,1,0:T(1,128)}), f32[16,1,8192]{2,1,0:T(1,128)S(1)}, u32[]{:S(2)}, u32[]{:S(2)}) async-start(f32[16,1,8192]{2,1,0:T(1,128)} %broadcast_in_dim.10), calls=%async_computation.4 | async-start | bytes 1048576 | tf_op jit(solution)/shard_map/all_to_all | solution.py:46
  153.5 19.5 %copy-start.15 = (bf16[1024,128]{1,0:T(8,128)(2,1)S(1)}, bf16[1024,128]{1,0:T(8,128)(2,1)}, u32[]{:S(2)}) copy-start(bf16[1024,128]{1,0:T(8,128)(2,1)} %param.15) | copy-start | bytes 786436
  167.9 52.0 %all-to-all-start.2 = ((f32[16,1,8192]{2,1,0:T(1,128)}), f32[16,1,8192]{2,1,0:T(1,128)S(1)}, u32[]{:S(2)}, u32[]{:S(2)}) async-start(f32[16,1,8192]{2,1,0:T(1,128)} %broadcast_in_dim.9), calls=%async_computation.2 | async-start | bytes 1048576 | tf_op jit(solution)/shard_map/all_to_all | solution.py:46
  173.0 3.0 copy-start.6
  176.0 1.3 copy-start.7
  176.9 1.2 copy-start.5
  201.6 1.9 copy-start.1
  203.5 9.6 %copy-start.11 = (bf16[64,1024]{1,0:T(8,128)(2,1)S(1)}, bf16[64,1024]{1,0:T(8,128)(2,1)}, u32[]{:S(2)}) copy-start(bf16[64,1024]{1,0:T(8,128)(2,1)} %get-tuple-element.14) | copy-start | bytes 393220
  219.9 0.9 copy-start.16
  223.8 1.3 copy-start.17
  226.9 0.9 copy-start.10
  228.1 48.1 %copy-start.4 = (s32[32]{0:T(128)S(1)}, s32[32]{0:T(128)}, u32[]{:S(2)}) copy-start(s32[32]{0:T(128)} %squeeze.28.tiles_ref) | copy-start | bytes 388
  276.1 2.2 copy-start.2
  302.0 1.9 copy-start.3

commit v7 on v5

--- a/solution.py
+++ b/solution.py
@@ -38,12 +38,19 @@
     return (hidden_grad, up_part, down_part)
 
 
-def summed_over(x, axis):
+def reduced_piece(x, axis):
     n = lax.axis_size(axis)
     flat = x.reshape(n, -1)
-    mine = lax.all_to_all(flat, axis, 0, 0, tiled=True).reshape(n, -1).sum(axis=0)
-    spread_back = lax.all_to_all(jnp.broadcast_to(mine[None], (n, mine.size)), axis, 0, 0, tiled=True)
-    return spread_back.reshape(x.shape)
+    return lax.all_to_all(flat, axis, 0, 0, tiled=True).reshape(n, -1).sum(axis=0)
+
+
+def spread_piece(mine, axis, shape):
+    n = lax.axis_size(axis)
+    return lax.all_to_all(jnp.broadcast_to(mine[None], (n, mine.size)), axis, 0, 0, tiled=True).reshape(shape)
+
+
+def summed_over(x, axis):
+    return spread_piece(reduced_piece(x, axis), axis, x.shape)
 
 
 def gathered_over(x, axis, dim):
@@ -54,7 +61,9 @@
     return pieces.reshape(*shape[:dim], shape[dim] * shape[dim + 1], *shape[dim + 2 :])
 
 
-def agg_kernel(agg_scale, k_total, nt, tiles_ref, emb_ref, rows_ref, mask_ref, counts_ref, agg_ref, acc_ref):
+def agg_kernel(agg_scale, k_total, nt, *refs):
+    tiles_ref, emb_ref, rows_ref, mask_ref = refs[:4]
+    counts_ref, agg_ref, acc_ref = refs[-3:]
     k = pl.program_id(1)
 
     @pl.when(k == 0)
@@ -85,27 +94,35 @@
         agg_ref[...] = (acc_ref[...] * agg_scale).astype(jnp.bfloat16)
 
 
-def aggregate(embedding, tiles_flat, neighbor_rows, slot_mask, agg_scale):
+def aggregate(embedding, tiles_flat, neighbor_rows, slot_mask, agg_scale, t0, t_count, into=None):
     columns, source_total = embedding.shape
     k_total, nb, dest_total = neighbor_rows.shape
     nt = dest_total // TD
     mask4 = slot_mask.reshape(k_total, 1, 1, dest_total)
     rows4 = neighbor_rows.reshape(k_total, 1, nb, dest_total)
+    prefetch = jnp.concatenate([jnp.full((1,), t0, jnp.int32), tiles_flat])
+    in_specs = [
+        pl.BlockSpec((columns, TS), lambda t, k, tiles: (0, tiles[1 + k * nt + tiles[0] + t])),
+        pl.BlockSpec((1, 1, nb, TD), lambda t, k, tiles: (k, 0, 0, tiles[0] + t)),
+        pl.BlockSpec((1, 1, 1, TD), lambda t, k, tiles: (k, 0, 0, tiles[0] + t)),
+    ]
+    operands = [prefetch, embedding, rows4, mask4]
+    aliases = {}
+    if into is not None:
+        in_specs += [pl.BlockSpec(memory_space=pl.ANY), pl.BlockSpec(memory_space=pl.ANY)]
+        operands += list(into)
+        aliases = {4: 0, 5: 1}
     grid_spec = pltpu.PrefetchScalarGridSpec(
         num_scalar_prefetch=1,
-        grid=(nt, k_total),
-        in_specs=[
-            pl.BlockSpec((columns, TS), lambda t, k, tiles: (0, tiles[k * nt + t])),
-            pl.BlockSpec((1, 1, nb, TD), lambda t, k, tiles: (k, 0, 0, t)),
-            pl.BlockSpec((1, 1, 1, TD), lambda t, k, tiles: (k, 0, 0, t)),
-        ],
+        grid=(t_count, k_total),
+        in_specs=in_specs,
         out_specs=[
-            pl.BlockSpec((1, 1, TS, TD), lambda t, k, tiles: (k, t, 0, 0)),
-            pl.BlockSpec((columns, TD), lambda t, k, tiles: (0, t)),
+            pl.BlockSpec((1, 1, TS, TD), lambda t, k, tiles: (k, tiles[0] + t, 0, 0)),
+            pl.BlockSpec((columns, TD), lambda t, k, tiles: (0, tiles[0] + t)),
         ],
         scratch_shapes=[pltpu.VMEM((columns, TD), jnp.float32)],
     )
-    work = k_total * dest_total * TS
+    work = k_total * t_count * TD * TS
     return pl.pallas_call(
         functools.partial(agg_kernel, agg_scale, k_total, nt),
         grid_spec=grid_spec,
@@ -113,13 +130,14 @@
             jax.ShapeDtypeStruct((k_total, nt, TS, TD), jnp.bfloat16),
             jax.ShapeDtypeStruct((columns, dest_total), jnp.bfloat16),
         ],
+        input_output_aliases=aliases,
         compiler_params=pltpu.CompilerParams(dimension_semantics=("arbitrary", "arbitrary")),
         cost_estimate=pl.CostEstimate(
             flops=2 * columns * work + 4 * nb * work,
             bytes_accessed=2 * work + 2 * columns * source_total,
             transcendentals=0,
         ),
-    )(tiles_flat, embedding, rows4, mask4)
+    )(*operands)
 
 
 def spread_kernel(agg_scale, k_total, nt, tiles_ref, counts_ref, back_ref, tg_in_ref, tg_ref):
@@ -190,16 +208,27 @@
 
     target_all = gathered_over(output_grad, "feat", 1)
     table = embedding.T
-    counts_all, own_all, hidden_all = [], [], []
+    nt = dest_total // TD
+    half = nt // 2
+    counts_all, own_all, pieces = [], [], []
     for m in range(micro_total):
-        counts, agg_t = aggregate(embedding, tiles_all[m], neighbor_rows[m], slot_mask[m], agg_scale)
+        first = aggregate(embedding, tiles_all[m], neighbor_rows[m], slot_mask[m], agg_scale, 0, half)
+        if m > 0:
+            first_counts, first_agg, pieces[m - 1] = lax.optimization_barrier(
+                (first[0], first[1], pieces[m - 1])
+            )
+            first = (first_counts, first_agg)
+        counts, agg_t = aggregate(
+            embedding, tiles_all[m], neighbor_rows[m], slot_mask[m], agg_scale, half, nt - half, into=first
+        )
         own = table[dest_rows[m]]
         partial = jnp.dot(own, self_weight, preferred_element_type=jnp.float32) + lax.dot_general(
             agg_t, neighbor_weight, (((0,), (0,)), ((), ())), preferred_element_type=jnp.float32
         )
         counts_all.append((counts, agg_t))
         own_all.append(own)
-        hidden_all.append(summed_over(partial, "feat"))
+        pieces.append(reduced_piece(partial, "feat"))
+    hidden_all = [spread_piece(p, "feat", (dest_total, H)) for p in pieces]
 
     up_sum = jnp.zeros(up_weight.shape, jnp.float32)
     down_sum = jnp.zeros(down_weight.shape, jnp.float32)

time: 310 us -> 319 us (1.029)
  blocking collectives: 29 us -> 54.7 us
  waiting for transfers between devices: 19.6 us -> 7.57 us
  starting transfers between devices: 37.8 us -> 28.1 us
  Pallas kernels: 133 us -> 138 us
    all_to_all x1 -> x2, blocking collectives: 29 us -> 54.7 us  [reduced_piece(): lax.all_to_all(flat, axis, 0, 0, tiled=True).reshape(n, -1).sum(axis=0)]
    all_to_all x5 -> x4, waiting for transfers between devices: 19.6 us -> 7.57 us  [the longest x1 7.56 us: reduced_piece(): lax.all_to_all(flat, axis, 0, 0, tiled=True).reshape(n, -1).sum(axis=0)]
    pallas_call x2 -> x4, Pallas kernels: 85.4 us -> 90.9 us  [aggregate(): pl.pallas_call(functools.partial(agg_kernel, agg_scale, k_total, nt), gri...]
    all_to_all x1, starting transfers between devices: 10.1 us -> 4.98 us  [gathered_over(): lax.all_to_all(jnp.broadcast_to(x[None], (n, *x.shape)), axis, 0, 0, tile...]
    all_to_all x5 -> x4, starting transfers between devices: 27.7 us -> 23.1 us  [the longest x3 15.6 us: spread_piece(): lax.all_to_all(jnp.broadcast_to(mine[None], (n, mine.size)), axis, 0, 0,...]
  transfers between devices with their start and end apart: 6 -> 5, of which waited for: 2 -> 1; matrix products, arithmetic and copies ran while one was open for 20% -> 16% of each run, Pallas kernels for 43% -> 29%
where the time goes in v7:
time: 319 us; the launch traced here: 317 us
  Pallas kernels  138 us (43%)
  blocking collectives  54.7 us (17%)
  local copies, waits for them, and re-layouts  37.2 us (12%)
  starting transfers between devices  28.1 us (9%)
  other arithmetic  27.2 us (9%)
  matrix products  23.2 us (7%)
  waiting for transfers between devices  7.57 us (2%)
    pallas_call x4, Pallas kernels, aggregate(): pl.pallas_call(functools.partial(agg_kernel, agg_scale, k_total, nt), gri...  90.9 us
    all_to_all x2, blocking collectives, reduced_piece(): lax.all_to_all(flat, axis, 0, 0, tiled=True).reshape(n, -1).sum(axis=0)  54.7 us
    pallas_call x2, Pallas kernels, spread(): pl.pallas_call(functools.partial(spread_kernel, agg_scale, k_total, nt),...  47.1 us
    scatter-add x2, other arithmetic, local(): table_grad = table_grad.at[dest_rows[m]].add(own_grad)  19.2 us
    all_to_all x3, starting transfers between devices, spread_piece(): lax.all_to_all(jnp.broadcast_to(mine[None], (n, mine.size)), axis, 0, 0,...  15.6 us
    unnamed x33, local copies, waits for them, and re-layouts  12.8 us
    all_to_all x1, waiting for transfers between devices, reduced_piece(): lax.all_to_all(flat, axis, 0, 0, tiled=True).reshape(n, -1).sum(axis=0)  7.56 us
    all_to_all x1, starting transfers between devices, reduced_piece(): lax.all_to_all(flat, axis, 0, 0, tiled=True).reshape(n, -1).sum(axis=0)  7.55 us
  transfers between devices with their start and end apart: 5, of which 1 were waited for; matrix products, arithmetic and copies ran while one was open for 16% of the time, Pallas kernels for 29%

profile of v7, /device:TPU:1, one launch (start us, length us, event | category | flops | bytes accessed | tf_op | source)
XLA Modules:
  0.0 317.0 jit_solution(11297744601079576085)
XLA Ops:
  2.5 2.3 slice_bitcast_fusion
  5.6 2.0 copy.81
  8.3 3.2 %gather_fusion = bf16[1024,64]{1,0:T(8,128)(2,1)S(1)} fusion(bf16[8192,64]{1,0:T(8,128)(2,1)S(1)} %bitcast.79, s32[1024]{0:T(1024)S(1)} %broadcast_clamp_fusion.1), kind=kCustom, calls=%fused_computation | custom fusion | bytes 266240 | tf_op jit(solution)/shard_map/gather | solution.py:224
  12.4 22.7 %shard_map.147 = (bf16[8,4,1024,256]{3,2,1,0:T(8,128)(2,1)}, bf16[64,1024]{1,0:T(8,128)(2,1)}) custom-call(s32[33]{0:T(128)} %get-tuple-element.75.refs_0_, bf16[64,8192]{1,0:T(8,128)(2,1)} %refs_1_.7, s32[8,1,16,1024]{3,2,1,0:T(8,128)} %get-tuple-element.63.refs_2_, s32[8,1,1,1024]{3,2,1,0:T(1,128)} %get-tuple-element.81.refs_3_), custom_call_target="tpu_custom_call" | custom-call | flops 805306368 | bytes 9437184 | tf_op jit(solution)/shard_map/pallas_call | solution.py:126
  35.1 22.8 %shard_map.148 = (bf16[8,4,1024,256]{3,2,1,0:T(8,128)(2,1)}, bf16[64,1024]{1,0:T(8,128)(2,1)}) custom-call(s32[33]{0:T(128)} %get-tuple-element.76.refs_0_, bf16[64,8192]{1,0:T(8,128)(2,1)} %refs_1_.7, s32[8,1,16,1024]{3,2,1,0:T(8,128)} %get-tuple-element.63.refs_2_, ...), custom_call_target="tpu_custom_call", output_to_operand_aliasing={{0}: (4, {}), {1}: (5, {})} | custom-call | flops 805306368 | bytes 9437184 | tf_op jit(solution)/shard_map/pallas_call | solution.py:126
  59.1 25.5 %all_to_all.50 = f32[16,1,8192]{2,1,0:T(1,128)S(1)} all-to-all(f32[16,1,8192]{2,1,0:T(1,128)S(1)} %bitcast.91), channel_id=1, replica_groups=mesh['batch'=16,'feat'=16] {'feat'}, dimensions={0} | all-to-all | bytes 1048576 | tf_op jit(solution)/shard_map/all_to_all | solution.py:44
  85.5 5.0 %all-to-all-start.1 = ((bf16[16,2,64,128]{3,2,1,0:T(8,128)(2,1)}), bf16[16,2,64,128]{3,2,1,0:T(8,128)(2,1)}, u32[]{:S(2)}, u32[]{:S(2)}) async-start(bf16[16,2,64,128]{3,2,1,0:T(8,128)(2,1)} %broadcast_in_dim.10), calls=%async_computation.1 | async-start | bytes 1048576 | tf_op jit(solution)/shard_map/all_to_all | solution.py:58
  90.5 3.2 %gather_fusion.1 = bf16[1024,64]{1,0:T(8,128)(2,1)S(1)} fusion(bf16[8192,64]{1,0:T(8,128)(2,1)S(1)} %bitcast.80, s32[1024]{0:T(1024)S(1)} %broadcast_clamp_fusion), kind=kCustom, calls=%fused_computation.1 | custom fusion | bytes 266240 | tf_op jit(solution)/shard_map/gather | solution.py:224
  93.7 22.7 %shard_map.146 = (bf16[8,4,1024,256]{3,2,1,0:T(8,128)(2,1)}, bf16[64,1024]{1,0:T(8,128)(2,1)}) custom-call(s32[33]{0:T(128)} %get-tuple-element.80.refs_0_, bf16[64,8192]{1,0:T(8,128)(2,1)} %refs_1_.7, s32[8,1,16,1024]{3,2,1,0:T(8,128)} %get-tuple-element.64.refs_2_, s32[8,1,1,1024]{3,2,1,0:T(1,128)} %get-tuple-element.82.refs_3_), custom_call_target="tpu_custom_call" | custom-call | flops 805306368 | bytes 9437184 | tf_op jit(solution)/shard_map/pallas_call | solution.py:126
  118.0 7.5 %all-to-all-start.4 = ((f32[16,1,8192]{2,1,0:T(1,128)}), f32[16,1,8192]{2,1,0:T(1,128)S(1)}, u32[]{:S(2)}, u32[]{:S(2)}) async-start(f32[16,1,8192]{2,1,0:T(1,128)} %broadcast_in_dim.12), calls=%async_computation.4 | async-start | bytes 1048576 | tf_op jit(solution)/shard_map/all_to_all | solution.py:49
  126.8 3.2 %scatter_custom_fusion.1 = bf16[1024,128]{1,0:T(8,128)(2,1)S(1)} fusion(s32[1024]{0:T(1024)S(1)} %bitcast.99, bf16[1024,128]{1,0:T(8,128)(2,1)S(1)} %bitcast.93, bf16[]{:T(256)} %constant.19.clone.1), kind=kCustom, calls=%fused_computation.69 | custom fusion | bytes 262146 | tf_op jit(solution)/shard_map/scatter | solution.py:245
  130.0 3.2 %scatter_custom_fusion = bf16[1024,128]{1,0:T(8,128)(2,1)S(1)} fusion(s32[1024]{0:T(1024)S(1)} %bitcast.98, bf16[1024,128]{1,0:T(8,128)(2,1)S(1)} %bitcast.92, bf16[]{:T(256)} %constant.19.clone.1), kind=kCustom, calls=%fused_computation.71 | custom fusion | bytes 262146 | tf_op jit(solution)/shard_map/scatter | solution.py:245
  133.3 22.7 %shard_map.149 = (bf16[8,4,1024,256]{3,2,1,0:T(8,128)(2,1)}, bf16[64,1024]{1,0:T(8,128)(2,1)}) custom-call(s32[33]{0:T(128)} %get-tuple-element.79.refs_0_, bf16[64,8192]{1,0:T(8,128)(2,1)} %refs_1_.7, s32[8,1,16,1024]{3,2,1,0:T(8,128)} %get-tuple-element.64.refs_2_, ...), custom_call_target="tpu_custom_call", output_to_operand_aliasing={{0}: (4, {}), {1}: (5, {})} | custom-call | flops 805306368 | bytes 9437184 | tf_op jit(solution)/shard_map/pallas_call | solution.py:126
  156.0 2.0 convolution_add_fusion
  158.0 7.6 %all-to-all-start.2 = ((f32[16,1,8192]{2,1,0:T(1,128)}), f32[16,1,8192]{2,1,0:T(1,128)S(1)}, u32[]{:S(2)}, u32[]{:S(2)}) async-start(f32[16,1,8192]{2,1,0:T(1,128)} %bitcast.14), calls=%async_computation.2 | async-start | bytes 1048576 | tf_op jit(solution)/shard_map/all_to_all | solution.py:44
  166.3 3.0 fusion.7
  171.5 7.6 %all-to-all-done.2 = f32[16,1,8192]{2,1,0:T(1,128)S(1)} async-done(((f32[16,1,8192]{2,1,0:T(1,128)}), f32[16,1,8192]{2,1,0:T(1,128)S(1)}, u32[]{:S(2)}, u32[]{:S(2)}) %all-to-all-start.2) | async-done | bytes 524320 | tf_op jit(solution)/shard_map/all_to_all | solution.py:44
  180.6 4.2 %all-to-all-start.3 = ((f32[16,1,8192]{2,1,0:T(1,128)}), f32[16,1,8192]{2,1,0:T(1,128)S(1)}, u32[]{:S(2)}, u32[]{:S(2)}) async-start(f32[16,1,8192]{2,1,0:T(1,128)} %broadcast_in_dim.11), calls=%async_computation.3 | async-start | bytes 1048576 | tf_op jit(solution)/shard_map/all_to_all | solution.py:49
  185.0 23.5 %shard_map.150 = f32[8192,64]{1,0:T(8,128)S(1)} custom-call(s32[32]{0:T(128)S(1)} %squeeze.32.tiles_ref, bf16[8,4,1024,256]{3,2,1,0:T(8,128)(2,1)} %get-tuple-element.27.counts_ref, bf16[1024,64]{1,0:T(8,128)(2,1)S(1)} %copy.87.back_ref, f32[8192,64]{1,0:T(8,128)S(1)} %broadcast_in_dim.13.clone.tg_in_ref), custom_call_target="tpu_custom_call", output_to_operand_aliasing={{}: (3, {})} | custom-call | flops 1073741824 | bytes 20971520 | tf_op jit(solution)/shard_map/pallas_call | solution.py:171
  208.6 2.0 copy-done.1
  210.5 9.6 %scatter_fusion = f32[8192,64]{1,0:T(8,128)} fusion(f32[8192,64]{1,0:T(8,128)} %copy-done.1, s32[1024]{0:T(1024)S(1)} %bitcast.97, f32[1024,64]{1,0:T(8,128)S(1)} %fusion.57), kind=kCustom, calls=%fused_computation.4 | custom fusion | flops 65536 | bytes 790528 | tf_op jit(solution)/shard_map/scatter-add | solution.py:255
  220.3 2.2 fusion.49
  222.5 4.5 %fusion.16 = f32[1024,128]{1,0:T(8,128)} fusion(bf16[1024,128]{1,0:T(8,128)(2,1)S(1)} %scatter_custom_fusion.1, f32[1024,1024]{1,0:T(8,128)} %copy-done.4), kind=kOutput, calls=%fused_computation.28 | convolution fusion | flops 277872640 | bytes 4980736 | tf_op jit(solution)/shard_map/dot_general | solution.py:30
  227.9 3.0 fusion.15
  234.8 29.2 %all_to_all.51 = f32[16,1,17408]{2,1,0:T(1,128)S(1)} all-to-all(f32[16,1,17408]{2,1,0:T(1,128)S(1)} %bitcast.89), channel_id=1, replica_groups=mesh['batch'=16,'feat'=16] {'batch'}, dimensions={0} | all-to-all | bytes 2228224 | tf_op jit(solution)/shard_map/all_to_all | solution.py:44
  266.3 3.9 %all-to-all-start.6 = ((f32[16,1,17408]{2,1,0:T(1,128)}), f32[16,1,17408]{2,1,0:T(1,128)S(1)}, u32[]{:S(2)}, u32[]{:S(2)}) async-start(f32[16,1,17408]{2,1,0:T(1,128)} %broadcast_in_dim.14), calls=%async_computation.6 | async-start | bytes 2228224 | tf_op jit(solution)/shard_map/all_to_all | solution.py:49
  270.6 2.2 copy-done.2
  272.8 23.5 %shard_map.151 = f32[8192,64]{1,0:T(8,128)S(1)} custom-call(s32[32]{0:T(128)S(1)} %squeeze.30.tiles_ref, bf16[8,4,1024,256]{3,2,1,0:T(8,128)(2,1)} %get-tuple-element.25.counts_ref, bf16[1024,64]{1,0:T(8,128)(2,1)S(1)} %copy.89.back_ref, f32[8192,64]{1,0:T(8,128)S(1)} %copy-done.2), custom_call_target="tpu_custom_call", output_to_operand_aliasing={{}: (3, {})} | custom-call | flops 1073741824 | bytes 20971520 | tf_op jit(solution)/shard_map/pallas_call | solution.py:171
  296.3 2.0 copy-done.3
  298.5 9.6 %scatter_fusion.1 = f32[8192,64]{1,0:T(8,128)} fusion(f32[8192,64]{1,0:T(8,128)} %copy-done.3, s32[1024]{0:T(1024)S(1)} %bitcast.95, f32[1024,64]{1,0:T(8,128)S(1)} %fusion.58), kind=kCustom, calls=%fused_computation.5 | custom fusion | flops 65536 | bytes 790528 | tf_op jit(solution)/shard_map/scatter-add | solution.py:272
  308.0 3.8 %copy.92 = f32[64,8192]{1,0:T(8,128)} copy(f32[64,8192]{0,1:T(8,128)} %bitcast.78) | data formatting | bytes 4194304
  313.3 2.7 reduce.3
  (77 shorter events, 24.0 us)
Async XLA Ops:
  0.6 164.9 %copy-start = (bf16[128,1024]{1,0:T(8,128)(2,1)S(1)}, bf16[128,1024]{1,0:T(8,128)(2,1)}, u32[]{:S(2)}) copy-start(bf16[128,1024]{1,0:T(8,128)(2,1)} %param.14) | copy-start | bytes 786436
  0.6 10.9 %copy-start.9 = (bf16[64,128]{1,0:T(8,128)(2,1)S(1)}, bf16[64,128]{1,0:T(8,128)(2,1)}, u32[]{:S(2)}) copy-start(bf16[64,128]{1,0:T(8,128)(2,1)} %param.12) | copy-start | bytes 49156
  35.1 22.8 %copy-start.8 = (bf16[64,128]{1,0:T(8,128)(2,1)S(1)}, bf16[64,128]{1,0:T(8,128)(2,1)}, u32[]{:S(2)}) copy-start(bf16[64,128]{1,0:T(8,128)(2,1)} %param.13) | copy-start | bytes 49156
  35.1 49.5 %copy-start.10 = (bf16[2,64,128]{2,1,0:T(8,128)(2,1)S(1)}, bf16[2,64,128]{2,1,0:T(8,128)(2,1)}, u32[]{:S(2)}) copy-start(bf16[2,64,128]{2,1,0:T(8,128)(2,1)} %param.21) | copy-start | bytes 98308
  85.5 40.0 %copy-start.11 = (s32[2,1,1024]{2,1,0:T(1,128)S(1)}, s32[2,1,1024]{2,1,0:T(1,128)}, u32[]{:S(2)}) copy-start(s32[2,1,1024]{2,1,0:T(1,128)} %param.20) | copy-start | bytes 24580
  85.5 31.3 %all-to-all-start.1 = ((bf16[16,2,64,128]{3,2,1,0:T(8,128)(2,1)}), bf16[16,2,64,128]{3,2,1,0:T(8,128)(2,1)}, u32[]{:S(2)}, u32[]{:S(2)}) async-start(bf16[16,2,64,128]{3,2,1,0:T(8,128)(2,1)} %broadcast_in_dim.10), calls=%async_computation.1 | async-start | bytes 1048576 | tf_op jit(solution)/shard_map/all_to_all | solution.py:58
  118.0 40.0 %all-to-all-start.4 = ((f32[16,1,8192]{2,1,0:T(1,128)}), f32[16,1,8192]{2,1,0:T(1,128)S(1)}, u32[]{:S(2)}, u32[]{:S(2)}) async-start(f32[16,1,8192]{2,1,0:T(1,128)} %broadcast_in_dim.12), calls=%async_computation.4 | async-start | bytes 1048576 | tf_op jit(solution)/shard_map/all_to_all | solution.py:49
  156.0 10.3 %copy-start.12 = (bf16[1024,128]{1,0:T(8,128)(2,1)S(1)}, bf16[1024,128]{1,0:T(8,128)(2,1)}, u32[]{:S(2)}) copy-start(bf16[1024,128]{1,0:T(8,128)(2,1)} %param.15) | copy-start | bytes 786436
  158.0 21.0 %all-to-all-start.2 = ((f32[16,1,8192]{2,1,0:T(1,128)}), f32[16,1,8192]{2,1,0:T(1,128)S(1)}, u32[]{:S(2)}, u32[]{:S(2)}) async-start(f32[16,1,8192]{2,1,0:T(1,128)} %bitcast.14), calls=%async_computation.2 | async-start | bytes 1048576 | tf_op jit(solution)/shard_map/all_to_all | solution.py:44
  166.3 3.0 copy-start.4
  169.3 1.3 copy-start.5
  180.6 46.4 %all-to-all-start.3 = ((f32[16,1,8192]{2,1,0:T(1,128)}), f32[16,1,8192]{2,1,0:T(1,128)S(1)}, u32[]{:S(2)}, u32[]{:S(2)}) async-start(f32[16,1,8192]{2,1,0:T(1,128)} %broadcast_in_dim.11), calls=%async_computation.3 | async-start | bytes 1048576 | tf_op jit(solution)/shard_map/all_to_all | solution.py:49
  208.6 2.0 copy-start.1
  210.5 9.6 %copy-start.7 = (bf16[64,1024]{1,0:T(8,128)(2,1)S(1)}, bf16[64,1024]{1,0:T(8,128)(2,1)}, u32[]{:S(2)}) copy-start(bf16[64,1024]{1,0:T(8,128)(2,1)} %get-tuple-element.22) | copy-start | bytes 393220
  227.0 0.9 copy-start.13
  230.9 1.5 copy-start.14
  232.5 2.0 copy-start.6
  266.3 45.6 %all-to-all-start.6 = ((f32[16,1,17408]{2,1,0:T(1,128)}), f32[16,1,17408]{2,1,0:T(1,128)S(1)}, u32[]{:S(2)}, u32[]{:S(2)}) async-start(f32[16,1,17408]{2,1,0:T(1,128)} %broadcast_in_dim.14), calls=%async_computation.6 | async-start | bytes 2228224 | tf_op jit(solution)/shard_map/all_to_all | solution.py:49
  270.6 2.2 copy-start.2
  296.3 2.0 copy-start.3

commit v8 on v5

--- a/solution.py
+++ b/solution.py
@@ -13,7 +13,7 @@
 TS = 1024
 K = 8
 NB = 16
-CS = 128
+CS = 256
 
 
 def gelu_slope(values):
@@ -132,28 +132,30 @@
 
     tile = tiles_ref[k * nt + t]
     start = pl.multiple_of(tile * TS, TS)
-    part = jnp.dot(counts_ref[0, 0], back_ref[...], preferred_element_type=jnp.float32)
-    tg_ref[pl.ds(start, TS), :] += part * agg_scale
+    part = lax.dot_general(
+        back_ref[...], counts_ref[0, 0], (((1,), (1,)), ((), ())), preferred_element_type=jnp.float32
+    )
+    tg_ref[:, pl.ds(start, TS)] += part * agg_scale
 
 
 def spread(counts, back, tiles_flat, table_grad, agg_scale):
     k_total, nt = counts.shape[:2]
-    source_total, columns = table_grad.shape
+    columns, source_total = table_grad.shape
     grid_spec = pltpu.PrefetchScalarGridSpec(
         num_scalar_prefetch=1,
         grid=(nt, k_total),
         in_specs=[
             pl.BlockSpec((1, 1, TS, TD), lambda t, k, tiles: (k, t, 0, 0)),
-            pl.BlockSpec((TD, columns), lambda t, k, tiles: (t, 0)),
-            pl.BlockSpec((source_total, columns), lambda t, k, tiles: (0, 0)),
-        ],
-        out_specs=pl.BlockSpec((source_total, columns), lambda t, k, tiles: (0, 0)),
+            pl.BlockSpec((columns, TD), lambda t, k, tiles: (0, t)),
+            pl.BlockSpec((columns, source_total), lambda t, k, tiles: (0, 0)),
+        ],
+        out_specs=pl.BlockSpec((columns, source_total), lambda t, k, tiles: (0, 0)),
     )
     work = k_total * nt * TD * TS
     return pl.pallas_call(
         functools.partial(spread_kernel, agg_scale, k_total, nt),
         grid_spec=grid_spec,
-        out_shape=jax.ShapeDtypeStruct((source_total, columns), jnp.float32),
+        out_shape=jax.ShapeDtypeStruct((columns, source_total), jnp.float32),
         input_output_aliases={3: 0},
         compiler_params=pltpu.CompilerParams(
             dimension_semantics=("arbitrary", "arbitrary"),
@@ -205,7 +207,7 @@
     down_sum = jnp.zeros(down_weight.shape, jnp.float32)
     self_sum = jnp.zeros((columns, H), jnp.float32)
     neighbor_sum = jnp.zeros((columns, H), jnp.float32)
-    table_grad = jnp.zeros((source_total, columns), jnp.float32)
+    table_grad = jnp.zeros((columns, source_total), jnp.float32)
     pending = []
     for m in range(micro_total):
         hidden = hidden_all[m]
@@ -219,11 +221,15 @@
         down_sum = down_sum + down_part
         self_sum = self_sum + jnp.dot(own_all[m].T, hidden_grad, preferred_element_type=jnp.float32)
         neighbor_sum = neighbor_sum + jnp.dot(agg_t, hidden_grad, preferred_element_type=jnp.float32)
-        back = jnp.dot(hidden_grad, neighbor_weight.T, preferred_element_type=jnp.float32).astype(jnp.bfloat16)
-        own_grad = jnp.dot(hidden_grad, self_weight.T, preferred_element_type=jnp.float32)
+        back = lax.dot_general(
+            neighbor_weight, hidden_grad, (((1,), (1,)), ((), ())), preferred_element_type=jnp.float32
+        ).astype(jnp.bfloat16)
+        own_grad = lax.dot_general(
+            self_weight, hidden_grad, (((1,), (1,)), ((), ())), preferred_element_type=jnp.float32
+        )
         if m + 1 < micro_total:
             table_grad = spread(counts_all[m][0], back, tiles_all[m], table_grad, agg_scale)
-            table_grad = table_grad.at[dest_rows[m]].add(own_grad)
+            table_grad = table_grad.at[:, dest_rows[m]].add(own_grad)
         else:
             pending.append((m, back, own_grad))
 
@@ -240,9 +246,9 @@
 
     for m, back, own_grad in pending:
         table_grad = spread(counts_all[m][0], back, tiles_all[m], table_grad, agg_scale)
-        table_grad = table_grad.at[dest_rows[m]].add(own_grad)
+        table_grad = table_grad.at[:, dest_rows[m]].add(own_grad)
     return (
-        table_grad.T,
+        table_grad,
         self_sum * norm_factor,
         neighbor_sum * norm_factor,
         up_sum * norm_factor,

time: 310 us -> 312 us (level)
  Pallas kernels: 133 us -> 128 us
    pallas_call x0 -> x2, local copies, waits for them, and re-layouts: none -> 5.43 us  [spread(): pl.pallas_call(functools.partial(spread_kernel, agg_scale, k_total, nt),...]
    unnamed x33 -> x51, local copies, waits for them, and re-layouts: 12.3 us -> 7.55 us
    pallas_call x2, Pallas kernels: 85.4 us -> 81.9 us  [aggregate(): pl.pallas_call(functools.partial(agg_kernel, agg_scale, k_total, nt), gri...]
  transfers between devices with their start and end apart: 6 -> 6, of which waited for: 2 -> 2; matrix products, arithmetic and copies ran while one was open for 20% -> 24% of each run, Pallas kernels for 43% -> 41%
where the time goes in v8:
time: 312 us; the launch traced here: 310 us
  Pallas kernels  128 us (41%)
  local copies, waits for them, and re-layouts  41.2 us (13%)
  starting transfers between devices  37.9 us (12%)
  blocking collectives  29.1 us (9%)
  other arithmetic  26.8 us (9%)
  matrix products  25.9 us (8%)
  waiting for transfers between devices  20 us (6%)
    pallas_call x2, Pallas kernels, aggregate(): pl.pallas_call(functools.partial(agg_kernel, agg_scale, k_total, nt), gri...  81.9 us
    pallas_call x2, Pallas kernels, spread(): pl.pallas_call(functools.partial(spread_kernel, agg_scale, k_total, nt),...  46.1 us
    all_to_all x1, blocking collectives, summed_over(): lax.all_to_all(flat, axis, 0, 0, tiled=True).reshape(n, -1).sum(axis=0)  29.1 us
    scatter-add x2, other arithmetic, local(): table_grad = table_grad.at[:, dest_rows[m]].add(own_grad)  19.6 us
    all_to_all x2, starting transfers between devices, summed_over(): lax.all_to_all(flat, axis, 0, 0, tiled=True).reshape(n, -1).sum(axis=0)  15.1 us
    all_to_all x2, waiting for transfers between devices, summed_over(): lax.all_to_all(flat, axis, 0, 0, tiled=True).reshape(n, -1).sum(axis=0)  14.2 us
    all_to_all x3, starting transfers between devices, summed_over(): lax.all_to_all(jnp.broadcast_to(mine[None], (n, mine.size)), axis, 0, 0,...  12.8 us
    all_to_all x1, starting transfers between devices, gathered_over(): lax.all_to_all(jnp.broadcast_to(x[None], (n, *x.shape)), axis, 0, 0, tile...  10 us
  transfers between devices with their start and end apart: 6, of which 2 were waited for; matrix products, arithmetic and copies ran while one was open for 24% of the time, Pallas kernels for 41%

profile of v8, /device:TPU:1, one launch (start us, length us, event | category | flops | bytes accessed | tf_op | source)
XLA Modules:
  0.0 310.2 jit_solution(9143273238285503377)
XLA Ops:
  2.4 10.0 %all-to-all-start = ((bf16[16,2,64,128]{3,2,1,0:T(8,128)(2,1)}), bf16[16,2,64,128]{3,2,1,0:T(8,128)(2,1)S(1)}, u32[]{:S(2)}, u32[]{:S(2)}) async-start(bf16[16,2,64,128]{3,2,1,0:T(8,128)(2,1)} %broadcast_in_dim.10), calls=%async_computation | async-start | bytes 1048576 | tf_op jit(solution)/shard_map/all_to_all | solution.py:51
  16.1 2.0 copy.68
  18.1 3.2 %gather_fusion.1 = bf16[1024,64]{1,0:T(8,128)(2,1)S(1)} fusion(bf16[8192,64]{1,0:T(8,128)(2,1)S(1)} %bitcast.83, s32[1024]{0:T(1024)S(1)} %broadcast_clamp_fusion), kind=kCustom, calls=%fused_computation.1 | custom fusion | bytes 266240 | tf_op jit(solution)/shard_map/gather | solution.py:198
  21.4 2.4 slice_bitcast_fusion
  23.7 40.9 %shard_map.147 = (bf16[8,4,1024,256]{3,2,1,0:T(8,128)(2,1)}, bf16[64,1024]{1,0:T(8,128)(2,1)}) custom-call(s32[32]{0:T(128)} %squeeze.32.tiles_ref, bf16[64,8192]{1,0:T(8,128)(2,1)} %emb_ref.3, s32[8,1,16,1024]{3,2,1,0:T(8,128)} %get-tuple-element.44.rows_ref, s32[8,1,1,1024]{3,2,1,0:T(1,128)} %get-tuple-element.57.mask_ref), custom_call_target="tpu_custom_call" | custom-call | flops 1610612736 | bytes 17825792 | tf_op jit(solution)/shard_map/pallas_call | solution.py:109
  64.8 2.0 convolution_add_fusion
  67.6 7.6 %all-to-all-start.3 = ((f32[16,1,8192]{2,1,0:T(1,128)}), f32[16,1,8192]{2,1,0:T(1,128)S(1)}, u32[]{:S(2)}, u32[]{:S(2)}) async-start(f32[16,1,8192]{2,1,0:T(1,128)} %bitcast.95), calls=%async_computation.3 | async-start | bytes 1048576 | tf_op jit(solution)/shard_map/all_to_all | solution.py:44
  75.8 3.2 %gather_fusion = bf16[1024,64]{1,0:T(8,128)(2,1)S(1)} fusion(bf16[8192,64]{1,0:T(8,128)(2,1)S(1)} %bitcast.84, s32[1024]{0:T(1024)S(1)} %broadcast_clamp_fusion.1), kind=kCustom, calls=%fused_computation | custom fusion | bytes 266240 | tf_op jit(solution)/shard_map/gather | solution.py:198
  79.1 41.0 %shard_map.146 = (bf16[8,4,1024,256]{3,2,1,0:T(8,128)(2,1)}, bf16[64,1024]{1,0:T(8,128)(2,1)}) custom-call(s32[32]{0:T(128)} %squeeze.28.tiles_ref, bf16[64,8192]{1,0:T(8,128)(2,1)} %emb_ref.3, s32[8,1,16,1024]{3,2,1,0:T(8,128)} %get-tuple-element.45.rows_ref, s32[8,1,1,1024]{3,2,1,0:T(1,128)} %get-tuple-element.56.mask_ref), custom_call_target="tpu_custom_call" | custom-call | flops 1610612736 | bytes 17825792 | tf_op jit(solution)/shard_map/pallas_call | solution.py:109
  120.3 2.0 convolution_add_fusion.1
  122.2 7.5 %all-to-all-start.1 = ((f32[16,1,8192]{2,1,0:T(1,128)}), f32[16,1,8192]{2,1,0:T(1,128)S(1)}, u32[]{:S(2)}, u32[]{:S(2)}) async-start(f32[16,1,8192]{2,1,0:T(1,128)} %bitcast.9), calls=%async_computation.1 | async-start | bytes 1048576 | tf_op jit(solution)/shard_map/all_to_all | solution.py:44
  130.1 14.2 %all-to-all-done.1 = f32[16,1,8192]{2,1,0:T(1,128)S(1)} async-done(((f32[16,1,8192]{2,1,0:T(1,128)}), f32[16,1,8192]{2,1,0:T(1,128)S(1)}, u32[]{:S(2)}, u32[]{:S(2)}) %all-to-all-start.1) | async-done | bytes 524320 | tf_op jit(solution)/shard_map/all_to_all | solution.py:44
  145.5 4.4 %all-to-all-start.4 = ((f32[16,1,8192]{2,1,0:T(1,128)}), f32[16,1,8192]{2,1,0:T(1,128)S(1)}, u32[]{:S(2)}, u32[]{:S(2)}) async-start(f32[16,1,8192]{2,1,0:T(1,128)} %broadcast_in_dim.12), calls=%async_computation.4 | async-start | bytes 1048576 | tf_op jit(solution)/shard_map/all_to_all | solution.py:45
  150.1 3.8 %scatter_custom_fusion = bf16[1024,128]{1,0:T(8,128)(2,1)} fusion(s32[1024]{0:T(1024)S(1)} %bitcast.104, bf16[1024,128]{1,0:T(8,128)(2,1)S(1)} %bitcast.98, bf16[]{:T(256)} %constant.12.clone.1), kind=kCustom, calls=%fused_computation.73 | custom fusion | bytes 262146 | tf_op jit(solution)/shard_map/scatter | solution.py:218
  153.9 3.2 %scatter_custom_fusion.1 = bf16[1024,128]{1,0:T(8,128)(2,1)S(1)} fusion(s32[1024]{0:T(1024)S(1)} %bitcast.103, bf16[1024,128]{1,0:T(8,128)(2,1)S(1)} %bitcast.97, bf16[]{:T(256)} %constant.12.clone.1), kind=kCustom, calls=%fused_computation.71 | custom fusion | bytes 262146 | tf_op jit(solution)/shard_map/scatter | solution.py:218
  157.5 5.8 %all-to-all-done.4 = f32[16,1,8192]{2,1,0:T(1,128)S(1)} async-done(((f32[16,1,8192]{2,1,0:T(1,128)}), f32[16,1,8192]{2,1,0:T(1,128)S(1)}, u32[]{:S(2)}, u32[]{:S(2)}) %all-to-all-start.4) | async-done | bytes 524320 | tf_op jit(solution)/shard_map/all_to_all | solution.py:45
  164.5 4.3 %all-to-all-start.2 = ((f32[16,1,8192]{2,1,0:T(1,128)}), f32[16,1,8192]{2,1,0:T(1,128)S(1)}, u32[]{:S(2)}, u32[]{:S(2)}) async-start(f32[16,1,8192]{2,1,0:T(1,128)} %broadcast_in_dim.11), calls=%async_computation.2 | async-start | bytes 1048576 | tf_op jit(solution)/shard_map/all_to_all | solution.py:45
  169.6 3.0 fusion.7
  175.5 23.0 %shard_map.148 = f32[64,8192]{1,0:T(8,128)S(1)} custom-call(s32[32]{0:T(128)S(1)} %copy-done.2, bf16[8,4,1024,256]{3,2,1,0:T(8,128)(2,1)} %get-tuple-element.13.counts_ref, bf16[64,1024]{1,0:T(8,128)(2,1)S(1)} %fusion.23.back_ref, f32[64,8192]{1,0:T(8,128)S(1)} %broadcast_in_dim.13.tg_in_ref), custom_call_target="tpu_custom_call", output_to_operand_aliasing={{}: (3, {})} | custom-call | flops 1073741824 | bytes 20971520 | tf_op jit(solution)/shard_map/pallas_call | solution.py:155
  198.6 2.7 copy.73
  201.3 10.0 %scatter_fusion = f32[64,8192]{0,1:T(8,128)} fusion(f32[64,8192]{0,1:T(8,128)} %copy.73, s32[1024]{0:T(1024)S(1)} %bitcast.102, f32[1024,64]{1,0:T(8,128)} %fusion.59), kind=kCustom, calls=%fused_computation.4 | custom fusion | flops 65536 | bytes 790528 | tf_op jit(solution)/shard_map/scatter-add | solution.py:232
  211.5 2.2 fusion.51
  213.7 3.7 %fusion.16 = f32[1024,128]{1,0:T(8,128)S(1)} fusion(bf16[1024,128]{1,0:T(8,128)(2,1)S(1)} %copy-done.20, f32[1024,1024]{1,0:T(8,128)} %copy-done.4), kind=kOutput, calls=%fused_computation.28 | convolution fusion | flops 277872640 | bytes 4980736 | tf_op jit(solution)/shard_map/dot_general | solution.py:30
  218.4 3.0 fusion.15
  225.3 29.1 %all_to_all.50 = f32[16,1,17408]{2,1,0:T(1,128)S(1)} all-to-all(f32[16,1,17408]{2,1,0:T(1,128)S(1)} %bitcast.93), channel_id=1, replica_groups=mesh['batch'=16,'feat'=16] {'batch'}, dimensions={0} | all-to-all | bytes 2228224 | tf_op jit(solution)/shard_map/all_to_all | solution.py:44
  256.8 4.1 %all-to-all-start.6 = ((f32[16,1,17408]{2,1,0:T(1,128)}), f32[16,1,17408]{2,1,0:T(1,128)S(1)}, u32[]{:S(2)}, u32[]{:S(2)}) async-start(f32[16,1,17408]{2,1,0:T(1,128)} %broadcast_in_dim.14), calls=%async_computation.6 | async-start | bytes 2228224 | tf_op jit(solution)/shard_map/all_to_all | solution.py:45
  260.8 2.8 copy.75.tg_in_ref
  264.8 23.0 %shard_map.149 = f32[64,8192]{1,0:T(8,128)S(1)} custom-call(s32[32]{0:T(128)S(1)} %copy-done.1, bf16[8,4,1024,256]{3,2,1,0:T(8,128)(2,1)} %get-tuple-element.11.counts_ref, bf16[64,1024]{1,0:T(8,128)(2,1)S(1)} %fusion.24.back_ref, f32[64,8192]{1,0:T(8,128)S(1)} %copy.75.tg_in_ref), custom_call_target="tpu_custom_call", output_to_operand_aliasing={{}: (3, {})} | custom-call | flops 1073741824 | bytes 20971520 | tf_op jit(solution)/shard_map/pallas_call | solution.py:155
  287.9 2.7 copy.76
  291.8 9.5 %scatter_fusion.1 = f32[64,8192]{0,1:T(8,128)} fusion(f32[64,8192]{0,1:T(8,128)} %copy.76, s32[1024]{0:T(1024)S(1)} %bitcast.100, f32[1024,64]{1,0:T(8,128)S(1)} %fusion.60), kind=kCustom, calls=%fused_computation.5 | custom fusion | flops 65536 | bytes 790528 | tf_op jit(solution)/shard_map/scatter-add | solution.py:249
  301.3 3.8 %copy.79 = f32[64,8192]{1,0:T(8,128)} copy(f32[64,8192]{0,1:T(8,128)} %scatter_fusion.1) | data formatting | bytes 4194304
  306.6 2.6 reduce.3
  (94 shorter events, 26.1 us)
Async XLA Ops:
  0.6 168.2 %copy-start = (bf16[128,1024]{1,0:T(8,128)(2,1)S(1)}, bf16[128,1024]{1,0:T(8,128)(2,1)}, u32[]{:S(2)}) copy-start(bf16[128,1024]{1,0:T(8,128)(2,1)} %param.14) | copy-start | bytes 786436
  2.4 64.4 %all-to-all-start = ((bf16[16,2,64,128]{3,2,1,0:T(8,128)(2,1)}), bf16[16,2,64,128]{3,2,1,0:T(8,128)(2,1)S(1)}, u32[]{:S(2)}, u32[]{:S(2)}) async-start(bf16[16,2,64,128]{3,2,1,0:T(8,128)(2,1)} %broadcast_in_dim.10), calls=%async_computation | async-start | bytes 1048576 | tf_op jit(solution)/shard_map/all_to_all | solution.py:51
  21.3 43.5 %copy-start.9 = (bf16[1024,64]{1,0:T(8,128)(2,1)}, bf16[1024,64]{1,0:T(8,128)(2,1)S(1)}, u32[]{:S(2)}) copy-start(bf16[1024,64]{1,0:T(8,128)(2,1)S(1)} %gather_fusion.1) | copy-start | bytes 393220
  21.3 43.3 %copy-start.17 = (bf16[64,128]{1,0:T(8,128)(2,1)S(1)}, bf16[64,128]{1,0:T(8,128)(2,1)}, u32[]{:S(2)}) copy-start(bf16[64,128]{1,0:T(8,128)(2,1)} %param.12) | copy-start | bytes 49156
  21.3 43.5 %copy-start.16 = (bf16[64,128]{1,0:T(8,128)(2,1)S(1)}, bf16[64,128]{1,0:T(8,128)(2,1)}, u32[]{:S(2)}) copy-start(bf16[64,128]{1,0:T(8,128)(2,1)} %param.13) | copy-start | bytes 49156
  66.8 0.8 copy-start.12
  67.6 54.6 %all-to-all-start.3 = ((f32[16,1,8192]{2,1,0:T(1,128)}), f32[16,1,8192]{2,1,0:T(1,128)S(1)}, u32[]{:S(2)}, u32[]{:S(2)}) async-start(f32[16,1,8192]{2,1,0:T(1,128)} %bitcast.95), calls=%async_computation.3 | async-start | bytes 1048576 | tf_op jit(solution)/shard_map/all_to_all | solution.py:44
  79.0 43.2 %copy-start.7 = (bf16[1024,64]{1,0:T(8,128)(2,1)}, bf16[1024,64]{1,0:T(8,128)(2,1)S(1)}, u32[]{:S(2)}) copy-start(bf16[1024,64]{1,0:T(8,128)(2,1)S(1)} %gather_fusion) | copy-start | bytes 393220
  79.1 70.9 %copy-start.21 = (s32[2,1,1024]{2,1,0:T(1,128)S(1)}, s32[2,1,1024]{2,1,0:T(1,128)}, u32[]{:S(2)}) copy-start(s32[2,1,1024]{2,1,0:T(1,128)} %param.20) | copy-start | bytes 24580
  79.1 70.9 %copy-start.13 = (bf16[16,2,64,128]{3,2,1,0:T(8,128)(2,1)S(1)}, bf16[16,2,64,128]{3,2,1,0:T(8,128)(2,1)}, u32[]{:S(2)}) copy-start(bf16[16,2,64,128]{3,2,1,0:T(8,128)(2,1)} %copy-done.12) | copy-start | bytes 1572868
  122.2 22.1 %all-to-all-start.1 = ((f32[16,1,8192]{2,1,0:T(1,128)}), f32[16,1,8192]{2,1,0:T(1,128)S(1)}, u32[]{:S(2)}, u32[]{:S(2)}) async-start(f32[16,1,8192]{2,1,0:T(1,128)} %bitcast.9), calls=%async_computation.1 | async-start | bytes 1048576 | tf_op jit(solution)/shard_map/all_to_all | solution.py:44
  145.5 17.8 %all-to-all-start.4 = ((f32[16,1,8192]{2,1,0:T(1,128)}), f32[16,1,8192]{2,1,0:T(1,128)S(1)}, u32[]{:S(2)}, u32[]{:S(2)}) async-start(f32[16,1,8192]{2,1,0:T(1,128)} %broadcast_in_dim.12), calls=%async_computation.4 | async-start | bytes 1048576 | tf_op jit(solution)/shard_map/all_to_all | solution.py:45
  150.0 19.5 %copy-start.22 = (bf16[1024,128]{1,0:T(8,128)(2,1)S(1)}, bf16[1024,128]{1,0:T(8,128)(2,1)}, u32[]{:S(2)}) copy-start(bf16[1024,128]{1,0:T(8,128)(2,1)} %param.15) | copy-start | bytes 786436
  157.1 15.5 %copy-start.19 = (bf16[1024,128]{1,0:T(8,128)(2,1)}, bf16[1024,128]{1,0:T(8,128)(2,1)S(1)}, u32[]{:S(2)}) copy-start(bf16[1024,128]{1,0:T(8,128)(2,1)S(1)} %scatter_custom_fusion.1) | copy-start | bytes 786436
  164.5 52.9 %all-to-all-start.2 = ((f32[16,1,8192]{2,1,0:T(1,128)}), f32[16,1,8192]{2,1,0:T(1,128)S(1)}, u32[]{:S(2)}, u32[]{:S(2)}) async-start(f32[16,1,8192]{2,1,0:T(1,128)} %broadcast_in_dim.11), calls=%async_computation.2 | async-start | bytes 1048576 | tf_op jit(solution)/shard_map/all_to_all | solution.py:45
  169.6 3.0 copy-start.4
  172.6 1.3 copy-start.11
  172.6 1.3 copy-start.10
  172.6 2.9 copy-start.2
  173.9 1.5 copy-start.5
  201.3 10.0 %copy-start.6 = (bf16[1024,128]{1,0:T(8,128)(2,1)S(1)}, bf16[1024,128]{1,0:T(8,128)(2,1)}, u32[]{:S(2)}) copy-start(bf16[1024,128]{1,0:T(8,128)(2,1)} %copy-done.5) | copy-start | bytes 786436
  201.3 10.0 %copy-start.15 = (bf16[64,1024]{1,0:T(8,128)(2,1)S(1)}, bf16[64,1024]{1,0:T(8,128)(2,1)}, u32[]{:S(2)}) copy-start(bf16[64,1024]{1,0:T(8,128)(2,1)} %get-tuple-element.14) | copy-start | bytes 393220
  201.3 12.4 %copy-start.20 = (bf16[1024,128]{1,0:T(8,128)(2,1)S(1)}, bf16[1024,128]{1,0:T(8,128)(2,1)}, u32[]{:S(2)}) copy-start(bf16[1024,128]{1,0:T(8,128)(2,1)} %copy-done.19) | copy-start | bytes 786436
  217.4 1.0 copy-start.18
  217.4 1.0 copy-start.23
  223.2 1.5 copy-start.8
  223.2 1.7 copy-start.14
  224.0 1.2 copy-start.3
  256.8 8.1 %copy-start.1 = (s32[32]{0:T(128)S(1)}, s32[32]{0:T(128)}, u32[]{:S(2)}) copy-start(s32[32]{0:T(128)} %squeeze.28.tiles_ref) | copy-start | bytes 388
  256.8 48.3 %all-to-all-start.6 = ((f32[16,1,17408]{2,1,0:T(1,128)}), f32[16,1,17408]{2,1,0:T(1,128)S(1)}, u32[]{:S(2)}, u32[]{:S(2)}) async-start(f32[16,1,17408]{2,1,0:T(1,128)} %broadcast_in_dim.14), calls=%async_computation.6 | async-start | bytes 2228224 | tf_op jit(solution)/shard_map/all_to_all | solution.py:45

commit v9 on v5

--- a/solution.py
+++ b/solution.py
@@ -13,7 +13,7 @@
 TS = 1024
 K = 8
 NB = 16
-CS = 128
+CS = 256
 
 
 def gelu_slope(values):
@@ -122,7 +122,7 @@
     )(tiles_flat, embedding, rows4, mask4)
 
 
-def spread_kernel(agg_scale, k_total, nt, tiles_ref, counts_ref, back_ref, tg_in_ref, tg_ref):
+def spread_kernel(agg_scale, k_total, nt, tiles_ref, counts_ref, back_ref, own_ref, tg_in_ref, tg_ref):
     t = pl.program_id(0)
     k = pl.program_id(1)
 
@@ -135,16 +135,29 @@
     part = jnp.dot(counts_ref[0, 0], back_ref[...], preferred_element_type=jnp.float32)
     tg_ref[pl.ds(start, TS), :] += part * agg_scale
 
-
-def spread(counts, back, tiles_flat, table_grad, agg_scale):
+    @pl.when((t == nt - 1) & (k == k_total - 1))
+    def _():
+        base = k_total * nt
+
+        def one_row(d, carry):
+            row = tiles_ref[base + d]
+            tg_ref[pl.ds(row, 1), :] += own_ref[pl.ds(d, 1), :]
+            return carry
+
+        lax.fori_loop(0, own_ref.shape[0], one_row, 0, unroll=8)
+
+
+def spread(counts, back, own_grad, dest, tiles_flat, table_grad, agg_scale):
     k_total, nt = counts.shape[:2]
     source_total, columns = table_grad.shape
+    prefetch = jnp.concatenate([tiles_flat, dest])
     grid_spec = pltpu.PrefetchScalarGridSpec(
         num_scalar_prefetch=1,
         grid=(nt, k_total),
         in_specs=[
             pl.BlockSpec((1, 1, TS, TD), lambda t, k, tiles: (k, t, 0, 0)),
             pl.BlockSpec((TD, columns), lambda t, k, tiles: (t, 0)),
+            pl.BlockSpec(own_grad.shape, lambda t, k, tiles: (0, 0)),
             pl.BlockSpec((source_total, columns), lambda t, k, tiles: (0, 0)),
         ],
         out_specs=pl.BlockSpec((source_total, columns), lambda t, k, tiles: (0, 0)),
@@ -154,7 +167,7 @@
         functools.partial(spread_kernel, agg_scale, k_total, nt),
         grid_spec=grid_spec,
         out_shape=jax.ShapeDtypeStruct((source_total, columns), jnp.float32),
-        input_output_aliases={3: 0},
+        input_output_aliases={4: 0},
         compiler_params=pltpu.CompilerParams(
             dimension_semantics=("arbitrary", "arbitrary"),
             vmem_limit_bytes=48 * 1024 * 1024,
@@ -164,7 +177,7 @@
             bytes_accessed=2 * work + 8 * source_total * columns,
             transcendentals=0,
         ),
-    )(tiles_flat, counts, back, table_grad)
+    )(prefetch, counts, back, own_grad, table_grad)
 
 
 def local(
@@ -222,8 +235,9 @@
         back = jnp.dot(hidden_grad, neighbor_weight.T, preferred_element_type=jnp.float32).astype(jnp.bfloat16)
         own_grad = jnp.dot(hidden_grad, self_weight.T, preferred_element_type=jnp.float32)
         if m + 1 < micro_total:
-            table_grad = spread(counts_all[m][0], back, tiles_all[m], table_grad, agg_scale)
-            table_grad = table_grad.at[dest_rows[m]].add(own_grad)
+            table_grad = spread(
+                counts_all[m][0], back, own_grad, dest_rows[m], tiles_all[m], table_grad, agg_scale
+            )
         else:
             pending.append((m, back, own_grad))
 
@@ -239,8 +253,9 @@
     neighbor_sum = line[ends[3] : ends[4]].reshape(columns, H)
 
     for m, back, own_grad in pending:
-        table_grad = spread(counts_all[m][0], back, tiles_all[m], table_grad, agg_scale)
-        table_grad = table_grad.at[dest_rows[m]].add(own_grad)
+        table_grad = spread(
+            counts_all[m][0], back, own_grad, dest_rows[m], tiles_all[m], table_grad, agg_scale
+        )
     return (
         table_grad.T,
         self_sum * norm_factor,

time: 310 us -> 292 us (0.942)
  other arithmetic: 26.4 us -> 7.37 us
  matrix products: 23.2 us -> 19.7 us
    scatter-add x2 -> x0, other arithmetic: 19.1 us -> none  [local(): table_grad = table_grad.at[dest_rows[m]].add(own_grad)]
    pallas_call x2, Pallas kernels: 47.2 us -> 53.3 us  [spread(): pl.pallas_call(functools.partial(spread_kernel, agg_scale, k_total, nt),...]
    pallas_call x2, Pallas kernels: 85.4 us -> 81.9 us  [aggregate(): pl.pallas_call(functools.partial(agg_kernel, agg_scale, k_total, nt), gri...]
    unnamed x33 -> x43, local copies, waits for them, and re-layouts: 12.3 us -> 13.1 us
  transfers between devices with their start and end apart: 6 -> 6, of which waited for: 2 -> 2; matrix products, arithmetic and copies ran while one was open for 20% -> 14% of each run, Pallas kernels for 43% -> 47%
where the time goes in v9:
time: 292 us; the launch traced here: 290 us
  Pallas kernels  135 us (46%)
  local copies, waits for them, and re-layouts  38.4 us (13%)
  starting transfers between devices  38 us (13%)
  blocking collectives  29.1 us (10%)
  waiting for transfers between devices  20.5 us (7%)
  matrix products  19.7 us (7%)
  other arithmetic  7.37 us (3%)
    pallas_call x2, Pallas kernels, aggregate(): pl.pallas_call(functools.partial(agg_kernel, agg_scale, k_total, nt), gri...  81.9 us
    pallas_call x2, Pallas kernels, spread(): pl.pallas_call(functools.partial(spread_kernel, agg_scale, k_total, nt),...  53.3 us
    all_to_all x1, blocking collectives, summed_over(): lax.all_to_all(flat, axis, 0, 0, tiled=True).reshape(n, -1).sum(axis=0)  29.1 us
    all_to_all x2, starting transfers between devices, summed_over(): lax.all_to_all(flat, axis, 0, 0, tiled=True).reshape(n, -1).sum(axis=0)  15.1 us
    all_to_all x2, waiting for transfers between devices, summed_over(): lax.all_to_all(flat, axis, 0, 0, tiled=True).reshape(n, -1).sum(axis=0)  14.2 us
    unnamed x43, local copies, waits for them, and re-layouts  13.1 us
    all_to_all x3, starting transfers between devices, summed_over(): lax.all_to_all(jnp.broadcast_to(mine[None], (n, mine.size)), axis, 0, 0,...  12.9 us
    all_to_all x1, starting transfers between devices, gathered_over(): lax.all_to_all(jnp.broadcast_to(x[None], (n, *x.shape)), axis, 0, 0, tile...  10 us
  transfers between devices with their start and end apart: 6, of which 2 were waited for; matrix products, arithmetic and copies ran while one was open for 14% of the time, Pallas kernels for 47%

profile of v9, /device:TPU:1, one launch (start us, length us, event | category | flops | bytes accessed | tf_op | source)
XLA Modules:
  0.0 289.5 jit_solution(16728524108265092179)
XLA Ops:
  0.6 1.7 broadcast_in_dim.10
  2.4 10.0 %all-to-all-start = ((bf16[16,2,64,128]{3,2,1,0:T(8,128)(2,1)}), bf16[16,2,64,128]{3,2,1,0:T(8,128)(2,1)S(1)}, u32[]{:S(2)}, u32[]{:S(2)}) async-start(bf16[16,2,64,128]{3,2,1,0:T(8,128)(2,1)} %broadcast_in_dim.10), calls=%async_computation | async-start | bytes 1048576 | tf_op jit(solution)/shard_map/all_to_all | solution.py:51
  16.2 2.0 copy.77
  18.2 3.2 %gather_fusion.1 = bf16[1024,64]{1,0:T(8,128)(2,1)S(1)} fusion(bf16[8192,64]{1,0:T(8,128)(2,1)S(1)} %bitcast.83, s32[1024]{0:T(1024)S(1)} %broadcast_clamp_fusion), kind=kCustom, calls=%fused_computation.1 | custom fusion | bytes 266240 | tf_op jit(solution)/shard_map/gather | solution.py:209
  21.4 2.3 slice_bitcast_fusion
  23.7 40.9 %shard_map.147 = (bf16[8,4,1024,256]{3,2,1,0:T(8,128)(2,1)}, bf16[64,1024]{1,0:T(8,128)(2,1)}) custom-call(s32[32]{0:T(128)} %squeeze.37.tiles_ref, bf16[64,8192]{1,0:T(8,128)(2,1)} %emb_ref.3, s32[8,1,16,1024]{3,2,1,0:T(8,128)} %get-tuple-element.49.rows_ref, s32[8,1,1,1024]{3,2,1,0:T(1,128)} %get-tuple-element.64.mask_ref), custom_call_target="tpu_custom_call" | custom-call | flops 1610612736 | bytes 17825792 | tf_op jit(solution)/shard_map/pallas_call | solution.py:109
  64.8 2.0 convolution_add_fusion
  67.5 7.6 %all-to-all-start.3 = ((f32[16,1,8192]{2,1,0:T(1,128)}), f32[16,1,8192]{2,1,0:T(1,128)S(1)}, u32[]{:S(2)}, u32[]{:S(2)}) async-start(f32[16,1,8192]{2,1,0:T(1,128)} %bitcast.95), calls=%async_computation.3 | async-start | bytes 1048576 | tf_op jit(solution)/shard_map/all_to_all | solution.py:44
  75.8 3.2 %gather_fusion = bf16[1024,64]{1,0:T(8,128)(2,1)S(1)} fusion(bf16[8192,64]{1,0:T(8,128)(2,1)S(1)} %bitcast.84, s32[1024]{0:T(1024)S(1)} %broadcast_clamp_fusion.1), kind=kCustom, calls=%fused_computation | custom fusion | bytes 266240 | tf_op jit(solution)/shard_map/gather | solution.py:209
  79.0 41.0 %shard_map.146 = (bf16[8,4,1024,256]{3,2,1,0:T(8,128)(2,1)}, bf16[64,1024]{1,0:T(8,128)(2,1)}) custom-call(s32[32]{0:T(128)} %squeeze.32.tiles_ref, bf16[64,8192]{1,0:T(8,128)(2,1)} %emb_ref.3, s32[8,1,16,1024]{3,2,1,0:T(8,128)} %get-tuple-element.50.rows_ref, s32[8,1,1,1024]{3,2,1,0:T(1,128)} %get-tuple-element.63.mask_ref), custom_call_target="tpu_custom_call" | custom-call | flops 1610612736 | bytes 17825792 | tf_op jit(solution)/shard_map/pallas_call | solution.py:109
  120.2 2.0 convolution_add_fusion.1
  122.2 7.6 %all-to-all-start.1 = ((f32[16,1,8192]{2,1,0:T(1,128)}), f32[16,1,8192]{2,1,0:T(1,128)S(1)}, u32[]{:S(2)}, u32[]{:S(2)}) async-start(f32[16,1,8192]{2,1,0:T(1,128)} %bitcast.10), calls=%async_computation.1 | async-start | bytes 1048576 | tf_op jit(solution)/shard_map/all_to_all | solution.py:44
  130.1 14.2 %all-to-all-done.1 = f32[16,1,8192]{2,1,0:T(1,128)S(1)} async-done(((f32[16,1,8192]{2,1,0:T(1,128)}), f32[16,1,8192]{2,1,0:T(1,128)S(1)}, u32[]{:S(2)}, u32[]{:S(2)}) %all-to-all-start.1) | async-done | bytes 524320 | tf_op jit(solution)/shard_map/all_to_all | solution.py:44
  145.5 4.4 %all-to-all-start.4 = ((f32[16,1,8192]{2,1,0:T(1,128)}), f32[16,1,8192]{2,1,0:T(1,128)S(1)}, u32[]{:S(2)}, u32[]{:S(2)}) async-start(f32[16,1,8192]{2,1,0:T(1,128)} %broadcast_in_dim.12), calls=%async_computation.4 | async-start | bytes 1048576 | tf_op jit(solution)/shard_map/all_to_all | solution.py:45
  150.2 3.2 %scatter_custom_fusion = bf16[1024,128]{1,0:T(8,128)(2,1)S(1)} fusion(s32[1024]{0:T(1024)S(1)} %bitcast.104, bf16[1024,128]{1,0:T(8,128)(2,1)S(1)} %bitcast.98, bf16[]{:T(256)} %constant.12.clone.1), kind=kCustom, calls=%fused_computation.69 | custom fusion | bytes 262146 | tf_op jit(solution)/shard_map/scatter | solution.py:229
  153.4 3.2 %scatter_custom_fusion.1 = bf16[1024,128]{1,0:T(8,128)(2,1)S(1)} fusion(s32[1024]{0:T(1024)S(1)} %bitcast.103, bf16[1024,128]{1,0:T(8,128)(2,1)S(1)} %bitcast.97, bf16[]{:T(256)} %constant.12.clone.1), kind=kCustom, calls=%fused_computation.67 | custom fusion | bytes 262146 | tf_op jit(solution)/shard_map/scatter | solution.py:229
  157.0 6.3 %all-to-all-done.4 = f32[16,1,8192]{2,1,0:T(1,128)S(1)} async-done(((f32[16,1,8192]{2,1,0:T(1,128)}), f32[16,1,8192]{2,1,0:T(1,128)S(1)}, u32[]{:S(2)}, u32[]{:S(2)}) %all-to-all-start.4) | async-done | bytes 524320 | tf_op jit(solution)/shard_map/all_to_all | solution.py:45
  164.5 4.3 %all-to-all-start.2 = ((f32[16,1,8192]{2,1,0:T(1,128)}), f32[16,1,8192]{2,1,0:T(1,128)S(1)}, u32[]{:S(2)}, u32[]{:S(2)}) async-start(f32[16,1,8192]{2,1,0:T(1,128)} %broadcast_in_dim.11), calls=%async_computation.2 | async-start | bytes 1048576 | tf_op jit(solution)/shard_map/all_to_all | solution.py:45
  169.6 3.0 %fusion.7 = bf16[1024,1024]{1,0:T(8,128)(2,1)S(1)} fusion(f32[1024,1024]{1,0:T(8,128)S(1)} %fusion.50, bf16[1024,128]{1,0:T(8,128)(2,1)S(1)} %scatter_custom_fusion.1, bf16[1024,128]{1,0:T(8,128)(2,1)S(1)} %copy-done.18), kind=kOutput, calls=%fused_computation.15 | convolution fusion | flops 288358400 | bytes 6815744 | tf_op jit(solution)/shard_map/dot_general | solution.py:32
  174.8 26.9 %shard_map.148.tg_in_ref = f32[8192,64]{1,0:T(8,128)S(1)} custom-call(s32[1056]{0:T(1024)S(1)} %pad_add_fusion.1.tiles_ref, bf16[8,4,1024,256]{3,2,1,0:T(8,128)(2,1)} %get-tuple-element.13.counts_ref, bf16[1024,64]{1,0:T(8,128)(2,1)S(1)} %copy.83.back_ref, f32[1024,64]{1,0:T(8,128)S(1)} %fusion.58.own_ref, ...), custom_call_target="tpu_custom_call", output_to_operand_aliasing={{}: (4, {})} | custom-call | flops 1073741824 | bytes 20971520 | tf_op jit(solution)/shard_map/pallas_call | solution.py:166
  201.7 1.9 copy-done.1
  204.2 1.7 fusion.16
  206.9 3.0 %fusion.15 = bf16[1024,1024]{1,0:T(8,128)(2,1)S(1)} fusion(f32[1024,1024]{1,0:T(8,128)S(1)} %fusion.51, bf16[1024,128]{1,0:T(8,128)(2,1)S(1)} %scatter_custom_fusion, bf16[1024,128]{1,0:T(8,128)(2,1)S(1)} %copy-done.19), kind=kOutput, calls=%fused_computation.23 | convolution fusion | flops 288358400 | bytes 6815744 | tf_op jit(solution)/shard_map/dot_general | solution.py:32
  209.9 1.7 fusion.19
  213.7 29.1 %all_to_all.50 = f32[16,1,17408]{2,1,0:T(1,128)S(1)} all-to-all(f32[16,1,17408]{2,1,0:T(1,128)S(1)} %bitcast.93), channel_id=1, replica_groups=mesh['batch'=16,'feat'=16] {'batch'}, dimensions={0} | all-to-all | bytes 2228224 | tf_op jit(solution)/shard_map/all_to_all | solution.py:44
  243.5 1.6 broadcast_in_dim.14
  245.2 4.1 %all-to-all-start.6 = ((f32[16,1,17408]{2,1,0:T(1,128)}), f32[16,1,17408]{2,1,0:T(1,128)S(1)}, u32[]{:S(2)}, u32[]{:S(2)}) async-start(f32[16,1,17408]{2,1,0:T(1,128)} %broadcast_in_dim.14), calls=%async_computation.6 | async-start | bytes 2228224 | tf_op jit(solution)/shard_map/all_to_all | solution.py:45
  250.0 2.2 copy-done.2
  252.2 26.4 %shard_map.149 = f32[8192,64]{1,0:T(8,128)S(1)} custom-call(s32[1056]{0:T(1024)S(1)} %pad_add_fusion.tiles_ref, bf16[8,4,1024,256]{3,2,1,0:T(8,128)(2,1)} %get-tuple-element.11.counts_ref, bf16[1024,64]{1,0:T(8,128)(2,1)S(1)} %copy.85.back_ref, f32[1024,64]{1,0:T(8,128)S(1)} %fusion.59.own_ref, f32[8192,64]{1,0:T(8,128)S(1)} %copy-done.2), custom_call_target="tpu_custom_call", output_to_operand_aliasing={{}: (4, {})} | custom-call | flops 1073741824 | bytes 20971520 | tf_op jit(solution)/shard_map/pallas_call | solution.py:166
  278.7 1.9 copy-done.3
  280.6 3.8 %copy.88 = f32[64,8192]{1,0:T(8,128)} copy(f32[64,8192]{0,1:T(8,128)} %bitcast.82) | data formatting | bytes 4194304
  285.9 2.6 reduce.3
  (86 shorter events, 19.1 us)
Async XLA Ops:
  0.6 168.2 %copy-start = (bf16[128,1024]{1,0:T(8,128)(2,1)S(1)}, bf16[128,1024]{1,0:T(8,128)(2,1)}, u32[]{:S(2)}) copy-start(bf16[128,1024]{1,0:T(8,128)(2,1)} %param.14) | copy-start | bytes 786436
  2.4 64.4 %all-to-all-start = ((bf16[16,2,64,128]{3,2,1,0:T(8,128)(2,1)}), bf16[16,2,64,128]{3,2,1,0:T(8,128)(2,1)S(1)}, u32[]{:S(2)}, u32[]{:S(2)}) async-start(bf16[16,2,64,128]{3,2,1,0:T(8,128)(2,1)} %broadcast_in_dim.10), calls=%async_computation | async-start | bytes 1048576 | tf_op jit(solution)/shard_map/all_to_all | solution.py:51
  21.4 43.2 %copy-start.13 = (bf16[64,128]{1,0:T(8,128)(2,1)S(1)}, bf16[64,128]{1,0:T(8,128)(2,1)}, u32[]{:S(2)}) copy-start(bf16[64,128]{1,0:T(8,128)(2,1)} %param.12) | copy-start | bytes 49156
  21.4 43.4 %copy-start.12 = (bf16[64,128]{1,0:T(8,128)(2,1)S(1)}, bf16[64,128]{1,0:T(8,128)(2,1)}, u32[]{:S(2)}) copy-start(bf16[64,128]{1,0:T(8,128)(2,1)} %param.13) | copy-start | bytes 49156
  66.7 0.8 copy-start.8
  67.5 54.7 %all-to-all-start.3 = ((f32[16,1,8192]{2,1,0:T(1,128)}), f32[16,1,8192]{2,1,0:T(1,128)S(1)}, u32[]{:S(2)}, u32[]{:S(2)}) async-start(f32[16,1,8192]{2,1,0:T(1,128)} %bitcast.95), calls=%async_computation.3 | async-start | bytes 1048576 | tf_op jit(solution)/shard_map/all_to_all | solution.py:44
  79.0 71.0 %copy-start.14 = (s32[2,1024]{1,0:T(2,128)S(1)}, s32[2,1024]{1,0:T(2,128)}, u32[]{:S(2)}) copy-start(s32[2,1024]{1,0:T(2,128)} %param.19) | copy-start | bytes 24580
  79.0 71.0 %copy-start.17 = (s32[32]{0:T(128)S(1)}, s32[32]{0:T(128)}, u32[]{:S(2)}) copy-start(s32[32]{0:T(128)} %squeeze.37.tiles_ref) | copy-start | bytes 388
  79.0 71.1 %copy-start.15 = (s32[2,1,1024]{2,1,0:T(1,128)S(1)}, s32[2,1,1024]{2,1,0:T(1,128)}, u32[]{:S(2)}) copy-start(s32[2,1,1024]{2,1,0:T(1,128)} %param.20) | copy-start | bytes 24580
  79.0 71.1 %copy-start.9 = (bf16[16,2,64,128]{3,2,1,0:T(8,128)(2,1)S(1)}, bf16[16,2,64,128]{3,2,1,0:T(8,128)(2,1)}, u32[]{:S(2)}) copy-start(bf16[16,2,64,128]{3,2,1,0:T(8,128)(2,1)} %copy-done.8) | copy-start | bytes 1572868
  122.2 22.1 %all-to-all-start.1 = ((f32[16,1,8192]{2,1,0:T(1,128)}), f32[16,1,8192]{2,1,0:T(1,128)S(1)}, u32[]{:S(2)}, u32[]{:S(2)}) async-start(f32[16,1,8192]{2,1,0:T(1,128)} %bitcast.10), calls=%async_computation.1 | async-start | bytes 1048576 | tf_op jit(solution)/shard_map/all_to_all | solution.py:44
  145.5 17.8 %all-to-all-start.4 = ((f32[16,1,8192]{2,1,0:T(1,128)}), f32[16,1,8192]{2,1,0:T(1,128)S(1)}, u32[]{:S(2)}, u32[]{:S(2)}) async-start(f32[16,1,8192]{2,1,0:T(1,128)} %broadcast_in_dim.12), calls=%async_computation.4 | async-start | bytes 1048576 | tf_op jit(solution)/shard_map/all_to_all | solution.py:45
  150.1 19.4 %copy-start.18 = (bf16[1024,128]{1,0:T(8,128)(2,1)S(1)}, bf16[1024,128]{1,0:T(8,128)(2,1)}, u32[]{:S(2)}) copy-start(bf16[1024,128]{1,0:T(8,128)(2,1)} %param.15) | copy-start | bytes 786436
  164.5 41.4 %all-to-all-start.2 = ((f32[16,1,8192]{2,1,0:T(1,128)}), f32[16,1,8192]{2,1,0:T(1,128)S(1)}, u32[]{:S(2)}, u32[]{:S(2)}) async-start(f32[16,1,8192]{2,1,0:T(1,128)} %broadcast_in_dim.11), calls=%async_computation.2 | async-start | bytes 1048576 | tf_op jit(solution)/shard_map/all_to_all | solution.py:45
  169.5 3.0 %copy-start.4 = (f32[1024,1024]{1,0:T(8,128)}, f32[1024,1024]{1,0:T(8,128)S(1)}, u32[]{:S(2)}) copy-start(f32[1024,1024]{1,0:T(8,128)S(1)} %fusion.50) | copy-start | bytes 12582916
  172.6 1.5 copy-start.6
  172.6 1.1 copy-start.11
  174.7 28.9 %copy-start.7 = (bf16[1024,1024]{1,0:T(8,128)(2,1)S(1)}, bf16[1024,1024]{1,0:T(8,128)(2,1)}, u32[]{:S(2)}) copy-start(bf16[1024,1024]{1,0:T(8,128)(2,1)} %copy-done.6) | copy-start | bytes 6291460
  174.8 29.4 %copy-start.5 = (f32[1024,1024]{1,0:T(8,128)S(1)}, f32[1024,1024]{1,0:T(8,128)}, u32[]{:S(2)}) copy-start(f32[1024,1024]{1,0:T(8,128)} %copy-done.4) | copy-start | bytes 12582916
  201.7 1.9 copy-start.1
  205.9 1.0 copy-start.19
  211.6 1.7 copy-start.10
  213.6 35.7 %copy-start.16 = (s32[32]{0:T(128)S(1)}, s32[32]{0:T(128)}, u32[]{:S(2)}) copy-start(s32[32]{0:T(128)} %squeeze.32.tiles_ref) | copy-start | bytes 388
  245.2 39.2 %all-to-all-start.6 = ((f32[16,1,17408]{2,1,0:T(1,128)}), f32[16,1,17408]{2,1,0:T(1,128)S(1)}, u32[]{:S(2)}, u32[]{:S(2)}) async-start(f32[16,1,17408]{2,1,0:T(1,128)} %broadcast_in_dim.14), calls=%async_computation.6 | async-start | bytes 2228224 | tf_op jit(solution)/shard_map/all_to_all | solution.py:45
  250.0 2.2 copy-start.2
  278.6 2.0 copy-start.3

commit v10 on v9

--- a/solution.py
+++ b/solution.py
@@ -71,9 +71,10 @@
         start = pl.multiple_of(c * CS, CS)
         local = (rows - start).astype(jnp.float32)
         cnt = zero
-        for j in range(NB):
+        for j in range(0, NB, 2):
             here = local[j : j + 1, :].astype(jnp.bfloat16)
-            cnt = cnt + jnp.where(here == local_iota, one, zero)
+            there = local[j + 1 : j + 2, :].astype(jnp.bfloat16)
+            cnt = cnt + (jnp.where(here == local_iota, one, zero) + jnp.where(there == local_iota, one, zero))
         counts_ref[0, 0, pl.ds(start, CS), :] = cnt * msk
         return carry
 

time: 292 us -> 291 us (level)
  no operation moved by 1% of the time
where the time goes in v10:
time: 291 us; the launch traced here: 289 us
  Pallas kernels  135 us (46%)
  local copies, waits for them, and re-layouts  38.4 us (13%)
  starting transfers between devices  38 us (13%)
  blocking collectives  29.1 us (10%)
  waiting for transfers between devices  20.5 us (7%)
  matrix products  19.6 us (7%)
  other arithmetic  7.37 us (3%)
    pallas_call x2, Pallas kernels, aggregate(): pl.pallas_call(functools.partial(agg_kernel, agg_scale, k_total, nt), gri...  81.2 us
    pallas_call x2, Pallas kernels, spread(): pl.pallas_call(functools.partial(spread_kernel, agg_scale, k_total, nt),...  53.3 us
    all_to_all x1, blocking collectives, summed_over(): lax.all_to_all(flat, axis, 0, 0, tiled=True).reshape(n, -1).sum(axis=0)  29.1 us
    all_to_all x2, starting transfers between devices, summed_over(): lax.all_to_all(flat, axis, 0, 0, tiled=True).reshape(n, -1).sum(axis=0)  15.1 us
    all_to_all x2, waiting for transfers between devices, summed_over(): lax.all_to_all(flat, axis, 0, 0, tiled=True).reshape(n, -1).sum(axis=0)  14.2 us
    unnamed x43, local copies, waits for them, and re-layouts  13.1 us
    all_to_all x3, starting transfers between devices, summed_over(): lax.all_to_all(jnp.broadcast_to(mine[None], (n, mine.size)), axis, 0, 0,...  12.9 us
    all_to_all x1, starting transfers between devices, gathered_over(): lax.all_to_all(jnp.broadcast_to(x[None], (n, *x.shape)), axis, 0, 0, tile...  10 us
  transfers between devices with their start and end apart: 6, of which 2 were waited for; matrix products, arithmetic and copies ran while one was open for 14% of the time, Pallas kernels for 47%

profile of v10, /device:TPU:1, one launch (start us, length us, event | category | flops | bytes accessed | tf_op | source)
XLA Modules:
  0.0 288.9 jit_solution(11916163727988590951)
XLA Ops:
  0.6 1.7 broadcast_in_dim.10
  2.4 10.0 %all-to-all-start = ((bf16[16,2,64,128]{3,2,1,0:T(8,128)(2,1)}), bf16[16,2,64,128]{3,2,1,0:T(8,128)(2,1)S(1)}, u32[]{:S(2)}, u32[]{:S(2)}) async-start(bf16[16,2,64,128]{3,2,1,0:T(8,128)(2,1)} %broadcast_in_dim.10), calls=%async_computation | async-start | bytes 1048576 | tf_op jit(solution)/shard_map/all_to_all | solution.py:51
  16.2 2.0 copy.77
  18.2 3.2 %gather_fusion.1 = bf16[1024,64]{1,0:T(8,128)(2,1)S(1)} fusion(bf16[8192,64]{1,0:T(8,128)(2,1)S(1)} %bitcast.83, s32[1024]{0:T(1024)S(1)} %broadcast_clamp_fusion), kind=kCustom, calls=%fused_computation.1 | custom fusion | bytes 266240 | tf_op jit(solution)/shard_map/gather | solution.py:210
  21.4 2.3 slice_bitcast_fusion
  23.7 40.5 %shard_map.147 = (bf16[8,4,1024,256]{3,2,1,0:T(8,128)(2,1)}, bf16[64,1024]{1,0:T(8,128)(2,1)}) custom-call(s32[32]{0:T(128)} %squeeze.37.tiles_ref, bf16[64,8192]{1,0:T(8,128)(2,1)} %emb_ref.3, s32[8,1,16,1024]{3,2,1,0:T(8,128)} %get-tuple-element.49.rows_ref, s32[8,1,1,1024]{3,2,1,0:T(1,128)} %get-tuple-element.64.mask_ref), custom_call_target="tpu_custom_call" | custom-call | flops 1610612736 | bytes 17825792 | tf_op jit(solution)/shard_map/pallas_call | solution.py:110
  64.5 2.0 convolution_add_fusion
  67.2 7.6 %all-to-all-start.3 = ((f32[16,1,8192]{2,1,0:T(1,128)}), f32[16,1,8192]{2,1,0:T(1,128)S(1)}, u32[]{:S(2)}, u32[]{:S(2)}) async-start(f32[16,1,8192]{2,1,0:T(1,128)} %bitcast.95), calls=%async_computation.3 | async-start | bytes 1048576 | tf_op jit(solution)/shard_map/all_to_all | solution.py:44
  75.5 3.2 %gather_fusion = bf16[1024,64]{1,0:T(8,128)(2,1)S(1)} fusion(bf16[8192,64]{1,0:T(8,128)(2,1)S(1)} %bitcast.84, s32[1024]{0:T(1024)S(1)} %broadcast_clamp_fusion.1), kind=kCustom, calls=%fused_computation | custom fusion | bytes 266240 | tf_op jit(solution)/shard_map/gather | solution.py:210
  78.7 40.7 %shard_map.146 = (bf16[8,4,1024,256]{3,2,1,0:T(8,128)(2,1)}, bf16[64,1024]{1,0:T(8,128)(2,1)}) custom-call(s32[32]{0:T(128)} %squeeze.32.tiles_ref, bf16[64,8192]{1,0:T(8,128)(2,1)} %emb_ref.3, s32[8,1,16,1024]{3,2,1,0:T(8,128)} %get-tuple-element.50.rows_ref, s32[8,1,1,1024]{3,2,1,0:T(1,128)} %get-tuple-element.63.mask_ref), custom_call_target="tpu_custom_call" | custom-call | flops 1610612736 | bytes 17825792 | tf_op jit(solution)/shard_map/pallas_call | solution.py:110
  119.6 2.0 convolution_add_fusion.1
  121.6 7.6 %all-to-all-start.1 = ((f32[16,1,8192]{2,1,0:T(1,128)}), f32[16,1,8192]{2,1,0:T(1,128)S(1)}, u32[]{:S(2)}, u32[]{:S(2)}) async-start(f32[16,1,8192]{2,1,0:T(1,128)} %bitcast.10), calls=%async_computation.1 | async-start | bytes 1048576 | tf_op jit(solution)/shard_map/all_to_all | solution.py:44
  129.5 14.2 %all-to-all-done.1 = f32[16,1,8192]{2,1,0:T(1,128)S(1)} async-done(((f32[16,1,8192]{2,1,0:T(1,128)}), f32[16,1,8192]{2,1,0:T(1,128)S(1)}, u32[]{:S(2)}, u32[]{:S(2)}) %all-to-all-start.1) | async-done | bytes 524320 | tf_op jit(solution)/shard_map/all_to_all | solution.py:44
  144.9 4.4 %all-to-all-start.4 = ((f32[16,1,8192]{2,1,0:T(1,128)}), f32[16,1,8192]{2,1,0:T(1,128)S(1)}, u32[]{:S(2)}, u32[]{:S(2)}) async-start(f32[16,1,8192]{2,1,0:T(1,128)} %broadcast_in_dim.12), calls=%async_computation.4 | async-start | bytes 1048576 | tf_op jit(solution)/shard_map/all_to_all | solution.py:45
  149.5 3.2 %scatter_custom_fusion = bf16[1024,128]{1,0:T(8,128)(2,1)S(1)} fusion(s32[1024]{0:T(1024)S(1)} %bitcast.104, bf16[1024,128]{1,0:T(8,128)(2,1)S(1)} %bitcast.98, bf16[]{:T(256)} %constant.12.clone.1), kind=kCustom, calls=%fused_computation.69 | custom fusion | bytes 262146 | tf_op jit(solution)/shard_map/scatter | solution.py:230
  152.7 3.2 %scatter_custom_fusion.1 = bf16[1024,128]{1,0:T(8,128)(2,1)S(1)} fusion(s32[1024]{0:T(1024)S(1)} %bitcast.103, bf16[1024,128]{1,0:T(8,128)(2,1)S(1)} %bitcast.97, bf16[]{:T(256)} %constant.12.clone.1), kind=kCustom, calls=%fused_computation.67 | custom fusion | bytes 262146 | tf_op jit(solution)/shard_map/scatter | solution.py:230
  156.3 6.3 %all-to-all-done.4 = f32[16,1,8192]{2,1,0:T(1,128)S(1)} async-done(((f32[16,1,8192]{2,1,0:T(1,128)}), f32[16,1,8192]{2,1,0:T(1,128)S(1)}, u32[]{:S(2)}, u32[]{:S(2)}) %all-to-all-start.4) | async-done | bytes 524320 | tf_op jit(solution)/shard_map/all_to_all | solution.py:45
  163.9 4.3 %all-to-all-start.2 = ((f32[16,1,8192]{2,1,0:T(1,128)}), f32[16,1,8192]{2,1,0:T(1,128)S(1)}, u32[]{:S(2)}, u32[]{:S(2)}) async-start(f32[16,1,8192]{2,1,0:T(1,128)} %broadcast_in_dim.11), calls=%async_computation.2 | async-start | bytes 1048576 | tf_op jit(solution)/shard_map/all_to_all | solution.py:45
  168.9 3.0 %fusion.7 = bf16[1024,1024]{1,0:T(8,128)(2,1)S(1)} fusion(f32[1024,1024]{1,0:T(8,128)S(1)} %fusion.50, bf16[1024,128]{1,0:T(8,128)(2,1)S(1)} %scatter_custom_fusion.1, bf16[1024,128]{1,0:T(8,128)(2,1)S(1)} %copy-done.18), kind=kOutput, calls=%fused_computation.15 | convolution fusion | flops 288358400 | bytes 6815744 | tf_op jit(solution)/shard_map/dot_general | solution.py:32
  174.1 26.9 %shard_map.148.tg_in_ref = f32[8192,64]{1,0:T(8,128)S(1)} custom-call(s32[1056]{0:T(1024)S(1)} %pad_add_fusion.1.tiles_ref, bf16[8,4,1024,256]{3,2,1,0:T(8,128)(2,1)} %get-tuple-element.13.counts_ref, bf16[1024,64]{1,0:T(8,128)(2,1)S(1)} %copy.83.back_ref, f32[1024,64]{1,0:T(8,128)S(1)} %fusion.58.own_ref, ...), custom_call_target="tpu_custom_call", output_to_operand_aliasing={{}: (4, {})} | custom-call | flops 1073741824 | bytes 20971520 | tf_op jit(solution)/shard_map/pallas_call | solution.py:167
  201.0 1.9 copy-done.1
  203.6 1.7 fusion.16
  206.3 3.0 %fusion.15 = bf16[1024,1024]{1,0:T(8,128)(2,1)S(1)} fusion(f32[1024,1024]{1,0:T(8,128)S(1)} %fusion.51, bf16[1024,128]{1,0:T(8,128)(2,1)S(1)} %scatter_custom_fusion, bf16[1024,128]{1,0:T(8,128)(2,1)S(1)} %copy-done.19), kind=kOutput, calls=%fused_computation.23 | convolution fusion | flops 288358400 | bytes 6815744 | tf_op jit(solution)/shard_map/dot_general | solution.py:32
  209.2 1.7 fusion.19
  213.1 29.1 %all_to_all.50 = f32[16,1,17408]{2,1,0:T(1,128)S(1)} all-to-all(f32[16,1,17408]{2,1,0:T(1,128)S(1)} %bitcast.93), channel_id=1, replica_groups=mesh['batch'=16,'feat'=16] {'batch'}, dimensions={0} | all-to-all | bytes 2228224 | tf_op jit(solution)/shard_map/all_to_all | solution.py:44
  242.9 1.6 broadcast_in_dim.14
  244.5 4.1 %all-to-all-start.6 = ((f32[16,1,17408]{2,1,0:T(1,128)}), f32[16,1,17408]{2,1,0:T(1,128)S(1)}, u32[]{:S(2)}, u32[]{:S(2)}) async-start(f32[16,1,17408]{2,1,0:T(1,128)} %broadcast_in_dim.14), calls=%async_computation.6 | async-start | bytes 2228224 | tf_op jit(solution)/shard_map/all_to_all | solution.py:45
  249.3 2.2 copy-done.2
  251.5 26.4 %shard_map.149 = f32[8192,64]{1,0:T(8,128)S(1)} custom-call(s32[1056]{0:T(1024)S(1)} %pad_add_fusion.tiles_ref, bf16[8,4,1024,256]{3,2,1,0:T(8,128)(2,1)} %get-tuple-element.11.counts_ref, bf16[1024,64]{1,0:T(8,128)(2,1)S(1)} %copy.85.back_ref, f32[1024,64]{1,0:T(8,128)S(1)} %fusion.59.own_ref, f32[8192,64]{1,0:T(8,128)S(1)} %copy-done.2), custom_call_target="tpu_custom_call", output_to_operand_aliasing={{}: (4, {})} | custom-call | flops 1073741824 | bytes 20971520 | tf_op jit(solution)/shard_map/pallas_call | solution.py:167
  278.0 1.9 copy-done.3
  279.9 3.8 %copy.88 = f32[64,8192]{1,0:T(8,128)} copy(f32[64,8192]{0,1:T(8,128)} %bitcast.82) | data formatting | bytes 4194304
  285.2 2.6 reduce.3
  (86 shorter events, 19.0 us)
Async XLA Ops:
  0.6 167.5 %copy-start = (bf16[128,1024]{1,0:T(8,128)(2,1)S(1)}, bf16[128,1024]{1,0:T(8,128)(2,1)}, u32[]{:S(2)}) copy-start(bf16[128,1024]{1,0:T(8,128)(2,1)} %param.14) | copy-start | bytes 786436
  2.4 64.1 %all-to-all-start = ((bf16[16,2,64,128]{3,2,1,0:T(8,128)(2,1)}), bf16[16,2,64,128]{3,2,1,0:T(8,128)(2,1)S(1)}, u32[]{:S(2)}, u32[]{:S(2)}) async-start(bf16[16,2,64,128]{3,2,1,0:T(8,128)(2,1)} %broadcast_in_dim.10), calls=%async_computation | async-start | bytes 1048576 | tf_op jit(solution)/shard_map/all_to_all | solution.py:51
  21.4 42.9 %copy-start.13 = (bf16[64,128]{1,0:T(8,128)(2,1)S(1)}, bf16[64,128]{1,0:T(8,128)(2,1)}, u32[]{:S(2)}) copy-start(bf16[64,128]{1,0:T(8,128)(2,1)} %param.12) | copy-start | bytes 49156
  21.4 43.0 %copy-start.12 = (bf16[64,128]{1,0:T(8,128)(2,1)S(1)}, bf16[64,128]{1,0:T(8,128)(2,1)}, u32[]{:S(2)}) copy-start(bf16[64,128]{1,0:T(8,128)(2,1)} %param.13) | copy-start | bytes 49156
  66.4 0.8 copy-start.8
  67.2 54.3 %all-to-all-start.3 = ((f32[16,1,8192]{2,1,0:T(1,128)}), f32[16,1,8192]{2,1,0:T(1,128)S(1)}, u32[]{:S(2)}, u32[]{:S(2)}) async-start(f32[16,1,8192]{2,1,0:T(1,128)} %bitcast.95), calls=%async_computation.3 | async-start | bytes 1048576 | tf_op jit(solution)/shard_map/all_to_all | solution.py:44
  78.7 70.7 %copy-start.14 = (s32[2,1024]{1,0:T(2,128)S(1)}, s32[2,1024]{1,0:T(2,128)}, u32[]{:S(2)}) copy-start(s32[2,1024]{1,0:T(2,128)} %param.19) | copy-start | bytes 24580
  78.7 70.7 %copy-start.17 = (s32[32]{0:T(128)S(1)}, s32[32]{0:T(128)}, u32[]{:S(2)}) copy-start(s32[32]{0:T(128)} %squeeze.37.tiles_ref) | copy-start | bytes 388
  78.7 70.7 %copy-start.15 = (s32[2,1,1024]{2,1,0:T(1,128)S(1)}, s32[2,1,1024]{2,1,0:T(1,128)}, u32[]{:S(2)}) copy-start(s32[2,1,1024]{2,1,0:T(1,128)} %param.20) | copy-start | bytes 24580
  78.7 70.7 %copy-start.9 = (bf16[16,2,64,128]{3,2,1,0:T(8,128)(2,1)S(1)}, bf16[16,2,64,128]{3,2,1,0:T(8,128)(2,1)}, u32[]{:S(2)}) copy-start(bf16[16,2,64,128]{3,2,1,0:T(8,128)(2,1)} %copy-done.8) | copy-start | bytes 1572868
  121.6 22.1 %all-to-all-start.1 = ((f32[16,1,8192]{2,1,0:T(1,128)}), f32[16,1,8192]{2,1,0:T(1,128)S(1)}, u32[]{:S(2)}, u32[]{:S(2)}) async-start(f32[16,1,8192]{2,1,0:T(1,128)} %bitcast.10), calls=%async_computation.1 | async-start | bytes 1048576 | tf_op jit(solution)/shard_map/all_to_all | solution.py:44
  144.9 17.8 %all-to-all-start.4 = ((f32[16,1,8192]{2,1,0:T(1,128)}), f32[16,1,8192]{2,1,0:T(1,128)S(1)}, u32[]{:S(2)}, u32[]{:S(2)}) async-start(f32[16,1,8192]{2,1,0:T(1,128)} %broadcast_in_dim.12), calls=%async_computation.4 | async-start | bytes 1048576 | tf_op jit(solution)/shard_map/all_to_all | solution.py:45
  149.5 19.4 %copy-start.18 = (bf16[1024,128]{1,0:T(8,128)(2,1)S(1)}, bf16[1024,128]{1,0:T(8,128)(2,1)}, u32[]{:S(2)}) copy-start(bf16[1024,128]{1,0:T(8,128)(2,1)} %param.15) | copy-start | bytes 786436
  163.9 41.4 %all-to-all-start.2 = ((f32[16,1,8192]{2,1,0:T(1,128)}), f32[16,1,8192]{2,1,0:T(1,128)S(1)}, u32[]{:S(2)}, u32[]{:S(2)}) async-start(f32[16,1,8192]{2,1,0:T(1,128)} %broadcast_in_dim.11), calls=%async_computation.2 | async-start | bytes 1048576 | tf_op jit(solution)/shard_map/all_to_all | solution.py:45
  168.9 3.0 %copy-start.4 = (f32[1024,1024]{1,0:T(8,128)}, f32[1024,1024]{1,0:T(8,128)S(1)}, u32[]{:S(2)}) copy-start(f32[1024,1024]{1,0:T(8,128)S(1)} %fusion.50) | copy-start | bytes 12582916
  171.9 1.5 copy-start.6
  171.9 1.1 copy-start.11
  174.1 28.9 %copy-start.7 = (bf16[1024,1024]{1,0:T(8,128)(2,1)S(1)}, bf16[1024,1024]{1,0:T(8,128)(2,1)}, u32[]{:S(2)}) copy-start(bf16[1024,1024]{1,0:T(8,128)(2,1)} %copy-done.6) | copy-start | bytes 6291460
  174.1 29.4 %copy-start.5 = (f32[1024,1024]{1,0:T(8,128)S(1)}, f32[1024,1024]{1,0:T(8,128)}, u32[]{:S(2)}) copy-start(f32[1024,1024]{1,0:T(8,128)} %copy-done.4) | copy-start | bytes 12582916
  201.0 1.9 copy-start.1
  205.3 1.0 copy-start.19
  211.0 1.7 copy-start.10
  213.0 35.7 %copy-start.16 = (s32[32]{0:T(128)S(1)}, s32[32]{0:T(128)}, u32[]{:S(2)}) copy-start(s32[32]{0:T(128)} %squeeze.32.tiles_ref) | copy-start | bytes 388
  244.5 39.2 %all-to-all-start.6 = ((f32[16,1,17408]{2,1,0:T(1,128)}), f32[16,1,17408]{2,1,0:T(1,128)S(1)}, u32[]{:S(2)}, u32[]{:S(2)}) async-start(f32[16,1,17408]{2,1,0:T(1,128)} %broadcast_in_dim.14), calls=%async_computation.6 | async-start | bytes 2228224 | tf_op jit(solution)/shard_map/all_to_all | solution.py:45
  249.3 2.2 copy-start.2
  278.0 2.0 copy-start.3

commit v11 on v10

--- a/solution.py
+++ b/solution.py
@@ -123,13 +123,17 @@
     )(tiles_flat, embedding, rows4, mask4)
 
 
-def spread_kernel(agg_scale, k_total, nt, tiles_ref, counts_ref, back_ref, own_ref, tg_in_ref, tg_ref):
+def spread_kernel(agg_scale, k_total, nt, tiles_ref, counts_ref, back_ref, own_ref, *refs):
+    tg_ref = refs[-1]
     t = pl.program_id(0)
     k = pl.program_id(1)
 
     @pl.when((t == 0) & (k == 0))
     def _():
-        tg_ref[...] = tg_in_ref[...]
+        if len(refs) == 2:
+            tg_ref[...] = refs[0][...]
+        else:
+            tg_ref[...] = jnp.zeros_like(tg_ref)
 
     tile = tiles_ref[k * nt + t]
     start = pl.multiple_of(tile * TS, TS)
@@ -148,19 +152,25 @@
         lax.fori_loop(0, own_ref.shape[0], one_row, 0, unroll=8)
 
 
-def spread(counts, back, own_grad, dest, tiles_flat, table_grad, agg_scale):
+def spread(counts, back, own_grad, dest, tiles_flat, table_grad, agg_scale, source_total):
     k_total, nt = counts.shape[:2]
-    source_total, columns = table_grad.shape
+    columns = back.shape[1]
     prefetch = jnp.concatenate([tiles_flat, dest])
+    in_specs = [
+        pl.BlockSpec((1, 1, TS, TD), lambda t, k, tiles: (k, t, 0, 0)),
+        pl.BlockSpec((TD, columns), lambda t, k, tiles: (t, 0)),
+        pl.BlockSpec(own_grad.shape, lambda t, k, tiles: (0, 0)),
+    ]
+    operands = [prefetch, counts, back, own_grad]
+    aliases = {}
+    if table_grad is not None:
+        in_specs.append(pl.BlockSpec((source_total, columns), lambda t, k, tiles: (0, 0)))
+        operands.append(table_grad)
+        aliases = {4: 0}
     grid_spec = pltpu.PrefetchScalarGridSpec(
         num_scalar_prefetch=1,
         grid=(nt, k_total),
-        in_specs=[
-            pl.BlockSpec((1, 1, TS, TD), lambda t, k, tiles: (k, t, 0, 0)),
-            pl.BlockSpec((TD, columns), lambda t, k, tiles: (t, 0)),
-            pl.BlockSpec(own_grad.shape, lambda t, k, tiles: (0, 0)),
-            pl.BlockSpec((source_total, columns), lambda t, k, tiles: (0, 0)),
-        ],
+        in_specs=in_specs,
         out_specs=pl.BlockSpec((source_total, columns), lambda t, k, tiles: (0, 0)),
     )
     work = k_total * nt * TD * TS
@@ -168,7 +178,7 @@
         functools.partial(spread_kernel, agg_scale, k_total, nt),
         grid_spec=grid_spec,
         out_shape=jax.ShapeDtypeStruct((source_total, columns), jnp.float32),
-        input_output_aliases={4: 0},
+        input_output_aliases=aliases,
         compiler_params=pltpu.CompilerParams(
             dimension_semantics=("arbitrary", "arbitrary"),
             vmem_limit_bytes=48 * 1024 * 1024,
@@ -178,7 +188,7 @@
             bytes_accessed=2 * work + 8 * source_total * columns,
             transcendentals=0,
         ),
-    )(prefetch, counts, back, own_grad, table_grad)
+    )(*operands)
 
 
 def local(
@@ -219,7 +229,7 @@
     down_sum = jnp.zeros(down_weight.shape, jnp.float32)
     self_sum = jnp.zeros((columns, H), jnp.float32)
     neighbor_sum = jnp.zeros((columns, H), jnp.float32)
-    table_grad = jnp.zeros((source_total, columns), jnp.float32)
+    table_grad = None
     pending = []
     for m in range(micro_total):
         hidden = hidden_all[m]
@@ -237,7 +247,7 @@
         own_grad = jnp.dot(hidden_grad, self_weight.T, preferred_element_type=jnp.float32)
         if m + 1 < micro_total:
             table_grad = spread(
-                counts_all[m][0], back, own_grad, dest_rows[m], tiles_all[m], table_grad, agg_scale
+                counts_all[m][0], back, own_grad, dest_rows[m], tiles_all[m], table_grad, agg_scale, source_total
             )
         else:
             pending.append((m, back, own_grad))
@@ -255,7 +265,7 @@
 
     for m, back, own_grad in pending:
         table_grad = spread(
-            counts_all[m][0], back, own_grad, dest_rows[m], tiles_all[m], table_grad, agg_scale
+            counts_all[m][0], back, own_grad, dest_rows[m], tiles_all[m], table_grad, agg_scale, source_total
         )
     return (
         table_grad.T,

time: 291 us -> 290 us (level)
  no operation moved by 1% of the time
where the time goes in v11:
time: 290 us; the launch traced here: 288 us
  Pallas kernels  134 us (46%)
  local copies, waits for them, and re-layouts  38.1 us (13%)
  starting transfers between devices  37.8 us (13%)
  blocking collectives  29.1 us (10%)
  waiting for transfers between devices  20.5 us (7%)
  matrix products  19.6 us (7%)
  other arithmetic  7.37 us (3%)
    pallas_call x2, Pallas kernels, aggregate(): pl.pallas_call(functools.partial(agg_kernel, agg_scale, k_total, nt), gri...  81.2 us
    pallas_call x2, Pallas kernels, spread(): pl.pallas_call(functools.partial(spread_kernel, agg_scale, k_total, nt),...  53.2 us
    all_to_all x1, blocking collectives, summed_over(): lax.all_to_all(flat, axis, 0, 0, tiled=True).reshape(n, -1).sum(axis=0)  29.1 us
    all_to_all x2, starting transfers between devices, summed_over(): lax.all_to_all(flat, axis, 0, 0, tiled=True).reshape(n, -1).sum(axis=0)  15.1 us
    all_to_all x2, waiting for transfers between devices, summed_over(): lax.all_to_all(flat, axis, 0, 0, tiled=True).reshape(n, -1).sum(axis=0)  14.2 us
    unnamed x43, local copies, waits for them, and re-layouts  13.1 us
    all_to_all x3, starting transfers between devices, summed_over(): lax.all_to_all(jnp.broadcast_to(mine[None], (n, mine.size)), axis, 0, 0,...  12.7 us
    all_to_all x1, starting transfers between devices, gathered_over(): lax.all_to_all(jnp.broadcast_to(x[None], (n, *x.shape)), axis, 0, 0, tile...  10 us
  transfers between devices with their start and end apart: 6, of which 2 were waited for; matrix products, arithmetic and copies ran while one was open for 14% of the time, Pallas kernels for 47%

profile of v11, /device:TPU:1, one launch (start us, length us, event | category | flops | bytes accessed | tf_op | source)
XLA Modules:
  0.0 288.2 jit_solution(12836256966144684456)
XLA Ops:
  0.6 1.7 broadcast_in_dim.8
  2.4 10.0 %all-to-all-start = ((bf16[16,2,64,128]{3,2,1,0:T(8,128)(2,1)}), bf16[16,2,64,128]{3,2,1,0:T(8,128)(2,1)S(1)}, u32[]{:S(2)}, u32[]{:S(2)}) async-start(bf16[16,2,64,128]{3,2,1,0:T(8,128)(2,1)} %broadcast_in_dim.8), calls=%async_computation | async-start | bytes 1048576 | tf_op jit(solution)/shard_map/all_to_all | solution.py:51
  16.2 2.0 copy.76
  18.2 3.2 %gather_fusion.1 = bf16[1024,64]{1,0:T(8,128)(2,1)S(1)} fusion(bf16[8192,64]{1,0:T(8,128)(2,1)S(1)} %bitcast.83, s32[1024]{0:T(1024)S(1)} %broadcast_clamp_fusion), kind=kCustom, calls=%fused_computation.1 | custom fusion | bytes 266240 | tf_op jit(solution)/shard_map/gather | solution.py:220
  21.4 2.3 slice_bitcast_fusion
  23.7 40.5 %shard_map.147 = (bf16[8,4,1024,256]{3,2,1,0:T(8,128)(2,1)}, bf16[64,1024]{1,0:T(8,128)(2,1)}) custom-call(s32[32]{0:T(128)} %squeeze.37.tiles_ref, bf16[64,8192]{1,0:T(8,128)(2,1)} %emb_ref.3, s32[8,1,16,1024]{3,2,1,0:T(8,128)} %get-tuple-element.49.rows_ref, s32[8,1,1,1024]{3,2,1,0:T(1,128)} %get-tuple-element.64.mask_ref), custom_call_target="tpu_custom_call" | custom-call | flops 1610612736 | bytes 17825792 | tf_op jit(solution)/shard_map/pallas_call | solution.py:110
  64.5 2.0 convolution_add_fusion
  67.2 7.6 %all-to-all-start.3 = ((f32[16,1,8192]{2,1,0:T(1,128)}), f32[16,1,8192]{2,1,0:T(1,128)S(1)}, u32[]{:S(2)}, u32[]{:S(2)}) async-start(f32[16,1,8192]{2,1,0:T(1,128)} %bitcast.95), calls=%async_computation.3 | async-start | bytes 1048576 | tf_op jit(solution)/shard_map/all_to_all | solution.py:44
  75.5 3.2 %gather_fusion = bf16[1024,64]{1,0:T(8,128)(2,1)S(1)} fusion(bf16[8192,64]{1,0:T(8,128)(2,1)S(1)} %bitcast.84, s32[1024]{0:T(1024)S(1)} %broadcast_clamp_fusion.1), kind=kCustom, calls=%fused_computation | custom fusion | bytes 266240 | tf_op jit(solution)/shard_map/gather | solution.py:220
  78.7 40.7 %shard_map.146 = (bf16[8,4,1024,256]{3,2,1,0:T(8,128)(2,1)}, bf16[64,1024]{1,0:T(8,128)(2,1)}) custom-call(s32[32]{0:T(128)} %squeeze.32.tiles_ref, bf16[64,8192]{1,0:T(8,128)(2,1)} %emb_ref.3, s32[8,1,16,1024]{3,2,1,0:T(8,128)} %get-tuple-element.50.rows_ref, s32[8,1,1,1024]{3,2,1,0:T(1,128)} %get-tuple-element.63.mask_ref), custom_call_target="tpu_custom_call" | custom-call | flops 1610612736 | bytes 17825792 | tf_op jit(solution)/shard_map/pallas_call | solution.py:110
  119.6 2.0 convolution_add_fusion.1
  121.6 7.6 %all-to-all-start.1 = ((f32[16,1,8192]{2,1,0:T(1,128)}), f32[16,1,8192]{2,1,0:T(1,128)S(1)}, u32[]{:S(2)}, u32[]{:S(2)}) async-start(f32[16,1,8192]{2,1,0:T(1,128)} %bitcast.10), calls=%async_computation.1 | async-start | bytes 1048576 | tf_op jit(solution)/shard_map/all_to_all | solution.py:44
  129.5 14.2 %all-to-all-done.1 = f32[16,1,8192]{2,1,0:T(1,128)S(1)} async-done(((f32[16,1,8192]{2,1,0:T(1,128)}), f32[16,1,8192]{2,1,0:T(1,128)S(1)}, u32[]{:S(2)}, u32[]{:S(2)}) %all-to-all-start.1) | async-done | bytes 524320 | tf_op jit(solution)/shard_map/all_to_all | solution.py:44
  144.8 4.5 %all-to-all-start.4 = ((f32[16,1,8192]{2,1,0:T(1,128)}), f32[16,1,8192]{2,1,0:T(1,128)S(1)}, u32[]{:S(2)}, u32[]{:S(2)}) async-start(f32[16,1,8192]{2,1,0:T(1,128)} %broadcast_in_dim.10), calls=%async_computation.4 | async-start | bytes 1048576 | tf_op jit(solution)/shard_map/all_to_all | solution.py:45
  149.5 3.2 %scatter_custom_fusion = bf16[1024,128]{1,0:T(8,128)(2,1)S(1)} fusion(s32[1024]{0:T(1024)S(1)} %bitcast.104, bf16[1024,128]{1,0:T(8,128)(2,1)S(1)} %bitcast.98, bf16[]{:T(256)} %constant.12.clone.1), kind=kCustom, calls=%fused_computation.69 | custom fusion | bytes 262146 | tf_op jit(solution)/shard_map/scatter | solution.py:240
  152.7 3.2 %scatter_custom_fusion.1 = bf16[1024,128]{1,0:T(8,128)(2,1)S(1)} fusion(s32[1024]{0:T(1024)S(1)} %bitcast.103, bf16[1024,128]{1,0:T(8,128)(2,1)S(1)} %bitcast.97, bf16[]{:T(256)} %constant.12.clone.1), kind=kCustom, calls=%fused_computation.67 | custom fusion | bytes 262146 | tf_op jit(solution)/shard_map/scatter | solution.py:240
  156.3 6.3 %all-to-all-done.4 = f32[16,1,8192]{2,1,0:T(1,128)S(1)} async-done(((f32[16,1,8192]{2,1,0:T(1,128)}), f32[16,1,8192]{2,1,0:T(1,128)S(1)}, u32[]{:S(2)}, u32[]{:S(2)}) %all-to-all-start.4) | async-done | bytes 524320 | tf_op jit(solution)/shard_map/all_to_all | solution.py:45
  163.9 4.3 %all-to-all-start.2 = ((f32[16,1,8192]{2,1,0:T(1,128)}), f32[16,1,8192]{2,1,0:T(1,128)S(1)}, u32[]{:S(2)}, u32[]{:S(2)}) async-start(f32[16,1,8192]{2,1,0:T(1,128)} %broadcast_in_dim.9), calls=%async_computation.2 | async-start | bytes 1048576 | tf_op jit(solution)/shard_map/all_to_all | solution.py:45
  168.9 3.0 %fusion.7 = bf16[1024,1024]{1,0:T(8,128)(2,1)S(1)} fusion(f32[1024,1024]{1,0:T(8,128)S(1)} %fusion.50, bf16[1024,128]{1,0:T(8,128)(2,1)S(1)} %scatter_custom_fusion.1, bf16[1024,128]{1,0:T(8,128)(2,1)S(1)} %copy-done.18), kind=kOutput, calls=%fused_computation.15 | convolution fusion | flops 288358400 | bytes 6815744 | tf_op jit(solution)/shard_map/dot_general | solution.py:32
  173.8 26.6 %shard_map.148.refs_0_ = f32[8192,64]{1,0:T(8,128)S(1)} custom-call(s32[1056]{0:T(1024)S(1)} %pad_add_fusion.1.tiles_ref, bf16[8,4,1024,256]{3,2,1,0:T(8,128)(2,1)} %get-tuple-element.13.counts_ref, bf16[1024,64]{1,0:T(8,128)(2,1)S(1)} %copy.81.back_ref, f32[1024,64]{1,0:T(8,128)S(1)} %fusion.58.own_ref), custom_call_target="tpu_custom_call" | custom-call | flops 1073741824 | bytes 20971520 | tf_op jit(solution)/shard_map/pallas_call | solution.py:177
  200.4 1.9 copy-done.1
  203.0 1.7 fusion.16
  205.7 3.0 %fusion.15 = bf16[1024,1024]{1,0:T(8,128)(2,1)S(1)} fusion(f32[1024,1024]{1,0:T(8,128)S(1)} %fusion.51, bf16[1024,128]{1,0:T(8,128)(2,1)S(1)} %scatter_custom_fusion, bf16[1024,128]{1,0:T(8,128)(2,1)S(1)} %copy-done.19), kind=kOutput, calls=%fused_computation.23 | convolution fusion | flops 288358400 | bytes 6815744 | tf_op jit(solution)/shard_map/dot_general | solution.py:32
  208.7 1.7 fusion.19
  212.5 29.1 %all_to_all.50 = f32[16,1,17408]{2,1,0:T(1,128)S(1)} all-to-all(f32[16,1,17408]{2,1,0:T(1,128)S(1)} %bitcast.93), channel_id=1, replica_groups=mesh['batch'=16,'feat'=16] {'batch'}, dimensions={0} | all-to-all | bytes 2228224 | tf_op jit(solution)/shard_map/all_to_all | solution.py:44
  242.3 1.6 broadcast_in_dim.11
  243.9 3.9 %all-to-all-start.6 = ((f32[16,1,17408]{2,1,0:T(1,128)}), f32[16,1,17408]{2,1,0:T(1,128)S(1)}, u32[]{:S(2)}, u32[]{:S(2)}) async-start(f32[16,1,17408]{2,1,0:T(1,128)} %broadcast_in_dim.11), calls=%async_computation.6 | async-start | bytes 2228224 | tf_op jit(solution)/shard_map/all_to_all | solution.py:45
  248.6 2.2 copy-done.2
  250.7 26.6 %shard_map.149 = f32[8192,64]{1,0:T(8,128)S(1)} custom-call(s32[1056]{0:T(1024)S(1)} %pad_add_fusion.tiles_ref, bf16[8,4,1024,256]{3,2,1,0:T(8,128)(2,1)} %get-tuple-element.11.counts_ref, bf16[1024,64]{1,0:T(8,128)(2,1)S(1)} %copy.83.back_ref, f32[1024,64]{1,0:T(8,128)S(1)} %fusion.59.own_ref, f32[8192,64]{1,0:T(8,128)S(1)} %copy-done.2), custom_call_target="tpu_custom_call", output_to_operand_aliasing={{}: (4, {})} | custom-call | flops 1073741824 | bytes 20971520 | tf_op jit(solution)/shard_map/pallas_call | solution.py:177
  277.3 1.9 copy-done.3
  279.3 3.8 %copy.86 = f32[64,8192]{1,0:T(8,128)} copy(f32[64,8192]{0,1:T(8,128)} %bitcast.82) | data formatting | bytes 4194304
  284.5 2.6 reduce.3
  (85 shorter events, 18.8 us)
Async XLA Ops:
  0.6 167.5 %copy-start = (bf16[128,1024]{1,0:T(8,128)(2,1)S(1)}, bf16[128,1024]{1,0:T(8,128)(2,1)}, u32[]{:S(2)}) copy-start(bf16[128,1024]{1,0:T(8,128)(2,1)} %param.14) | copy-start | bytes 786436
  2.4 64.1 %all-to-all-start = ((bf16[16,2,64,128]{3,2,1,0:T(8,128)(2,1)}), bf16[16,2,64,128]{3,2,1,0:T(8,128)(2,1)S(1)}, u32[]{:S(2)}, u32[]{:S(2)}) async-start(bf16[16,2,64,128]{3,2,1,0:T(8,128)(2,1)} %broadcast_in_dim.8), calls=%async_computation | async-start | bytes 1048576 | tf_op jit(solution)/shard_map/all_to_all | solution.py:51
  21.4 42.9 %copy-start.13 = (bf16[64,128]{1,0:T(8,128)(2,1)S(1)}, bf16[64,128]{1,0:T(8,128)(2,1)}, u32[]{:S(2)}) copy-start(bf16[64,128]{1,0:T(8,128)(2,1)} %param.12) | copy-start | bytes 49156
  21.4 43.0 %copy-start.12 = (bf16[64,128]{1,0:T(8,128)(2,1)S(1)}, bf16[64,128]{1,0:T(8,128)(2,1)}, u32[]{:S(2)}) copy-start(bf16[64,128]{1,0:T(8,128)(2,1)} %param.13) | copy-start | bytes 49156
  66.4 0.8 copy-start.8
  67.2 54.4 %all-to-all-start.3 = ((f32[16,1,8192]{2,1,0:T(1,128)}), f32[16,1,8192]{2,1,0:T(1,128)S(1)}, u32[]{:S(2)}, u32[]{:S(2)}) async-start(f32[16,1,8192]{2,1,0:T(1,128)} %bitcast.95), calls=%async_computation.3 | async-start | bytes 1048576 | tf_op jit(solution)/shard_map/all_to_all | solution.py:44
  78.7 70.6 %copy-start.14 = (s32[2,1024]{1,0:T(2,128)S(1)}, s32[2,1024]{1,0:T(2,128)}, u32[]{:S(2)}) copy-start(s32[2,1024]{1,0:T(2,128)} %param.19) | copy-start | bytes 24580
  78.7 70.7 %copy-start.17 = (s32[32]{0:T(128)S(1)}, s32[32]{0:T(128)}, u32[]{:S(2)}) copy-start(s32[32]{0:T(128)} %squeeze.37.tiles_ref) | copy-start | bytes 388
  78.7 70.7 %copy-start.15 = (s32[2,1,1024]{2,1,0:T(1,128)S(1)}, s32[2,1,1024]{2,1,0:T(1,128)}, u32[]{:S(2)}) copy-start(s32[2,1,1024]{2,1,0:T(1,128)} %param.20) | copy-start | bytes 24580
  78.7 70.7 %copy-start.9 = (bf16[16,2,64,128]{3,2,1,0:T(8,128)(2,1)S(1)}, bf16[16,2,64,128]{3,2,1,0:T(8,128)(2,1)}, u32[]{:S(2)}) copy-start(bf16[16,2,64,128]{3,2,1,0:T(8,128)(2,1)} %copy-done.8) | copy-start | bytes 1572868
  121.6 22.1 %all-to-all-start.1 = ((f32[16,1,8192]{2,1,0:T(1,128)}), f32[16,1,8192]{2,1,0:T(1,128)S(1)}, u32[]{:S(2)}, u32[]{:S(2)}) async-start(f32[16,1,8192]{2,1,0:T(1,128)} %bitcast.10), calls=%async_computation.1 | async-start | bytes 1048576 | tf_op jit(solution)/shard_map/all_to_all | solution.py:44
  144.8 17.8 %all-to-all-start.4 = ((f32[16,1,8192]{2,1,0:T(1,128)}), f32[16,1,8192]{2,1,0:T(1,128)S(1)}, u32[]{:S(2)}, u32[]{:S(2)}) async-start(f32[16,1,8192]{2,1,0:T(1,128)} %broadcast_in_dim.10), calls=%async_computation.4 | async-start | bytes 1048576 | tf_op jit(solution)/shard_map/all_to_all | solution.py:45
  149.5 19.4 %copy-start.18 = (bf16[1024,128]{1,0:T(8,128)(2,1)S(1)}, bf16[1024,128]{1,0:T(8,128)(2,1)}, u32[]{:S(2)}) copy-start(bf16[1024,128]{1,0:T(8,128)(2,1)} %param.15) | copy-start | bytes 786436
  163.9 40.9 %all-to-all-start.2 = ((f32[16,1,8192]{2,1,0:T(1,128)}), f32[16,1,8192]{2,1,0:T(1,128)S(1)}, u32[]{:S(2)}, u32[]{:S(2)}) async-start(f32[16,1,8192]{2,1,0:T(1,128)} %broadcast_in_dim.9), calls=%async_computation.2 | async-start | bytes 1048576 | tf_op jit(solution)/shard_map/all_to_all | solution.py:45
  168.9 3.0 %copy-start.4 = (f32[1024,1024]{1,0:T(8,128)}, f32[1024,1024]{1,0:T(8,128)S(1)}, u32[]{:S(2)}) copy-start(f32[1024,1024]{1,0:T(8,128)S(1)} %fusion.50) | copy-start | bytes 12582916
  171.9 1.5 copy-start.6
  171.9 1.1 copy-start.11
  173.8 28.6 %copy-start.7 = (bf16[1024,1024]{1,0:T(8,128)(2,1)S(1)}, bf16[1024,1024]{1,0:T(8,128)(2,1)}, u32[]{:S(2)}) copy-start(bf16[1024,1024]{1,0:T(8,128)(2,1)} %copy-done.6) | copy-start | bytes 6291460
  173.8 29.2 %copy-start.5 = (f32[1024,1024]{1,0:T(8,128)S(1)}, f32[1024,1024]{1,0:T(8,128)}, u32[]{:S(2)}) copy-start(f32[1024,1024]{1,0:T(8,128)} %copy-done.4) | copy-start | bytes 12582916
  200.4 1.9 copy-start.1
  204.7 1.0 copy-start.19
  210.4 1.7 copy-start.10
  212.4 35.5 %copy-start.16 = (s32[32]{0:T(128)S(1)}, s32[32]{0:T(128)}, u32[]{:S(2)}) copy-start(s32[32]{0:T(128)} %squeeze.32.tiles_ref) | copy-start | bytes 388
  243.9 39.1 %all-to-all-start.6 = ((f32[16,1,17408]{2,1,0:T(1,128)}), f32[16,1,17408]{2,1,0:T(1,128)S(1)}, u32[]{:S(2)}, u32[]{:S(2)}) async-start(f32[16,1,17408]{2,1,0:T(1,128)} %broadcast_in_dim.11), calls=%async_computation.6 | async-start | bytes 2228224 | tf_op jit(solution)/shard_map/all_to_all | solution.py:45
  248.6 2.2 copy-start.2
  277.3 2.0 copy-start.3

commit v12 on v11

--- a/solution.py
+++ b/solution.py
@@ -123,14 +123,14 @@
     )(tiles_flat, embedding, rows4, mask4)
 
 
-def spread_kernel(agg_scale, k_total, nt, tiles_ref, counts_ref, back_ref, own_ref, *refs):
+def spread_kernel(agg_scale, k_total, nt, final, tiles_ref, counts_ref, back_ref, own_ref, *refs):
     tg_ref = refs[-1]
     t = pl.program_id(0)
     k = pl.program_id(1)
 
     @pl.when((t == 0) & (k == 0))
     def _():
-        if len(refs) == 2:
+        if len(refs) >= 2:
             tg_ref[...] = refs[0][...]
         else:
             tg_ref[...] = jnp.zeros_like(tg_ref)
@@ -150,9 +150,13 @@
             return carry
 
         lax.fori_loop(0, own_ref.shape[0], one_row, 0, unroll=8)
-
-
-def spread(counts, back, own_grad, dest, tiles_flat, table_grad, agg_scale, source_total):
+        if final:
+            out_ref = refs[1]
+            for i in range(tg_ref.shape[0] // TS):
+                out_ref[:, i * TS : (i + 1) * TS] = tg_ref[i * TS : (i + 1) * TS, :].T
+
+
+def spread(counts, back, own_grad, dest, tiles_flat, table_grad, agg_scale, source_total, final=False):
     k_total, nt = counts.shape[:2]
     columns = back.shape[1]
     prefetch = jnp.concatenate([tiles_flat, dest])
@@ -166,18 +170,25 @@
     if table_grad is not None:
         in_specs.append(pl.BlockSpec((source_total, columns), lambda t, k, tiles: (0, 0)))
         operands.append(table_grad)
-        aliases = {4: 0}
+        aliases = {} if final else {4: 0}
     grid_spec = pltpu.PrefetchScalarGridSpec(
         num_scalar_prefetch=1,
         grid=(nt, k_total),
         in_specs=in_specs,
-        out_specs=pl.BlockSpec((source_total, columns), lambda t, k, tiles: (0, 0)),
+        out_specs=(
+            pl.BlockSpec((columns, source_total), lambda t, k, tiles: (0, 0))
+            if final
+            else pl.BlockSpec((source_total, columns), lambda t, k, tiles: (0, 0))
+        ),
+        scratch_shapes=[pltpu.VMEM((source_total, columns), jnp.float32)] if final else [],
     )
     work = k_total * nt * TD * TS
     return pl.pallas_call(
-        functools.partial(spread_kernel, agg_scale, k_total, nt),
+        functools.partial(spread_kernel, agg_scale, k_total, nt, final),
         grid_spec=grid_spec,
-        out_shape=jax.ShapeDtypeStruct((source_total, columns), jnp.float32),
+        out_shape=jax.ShapeDtypeStruct(
+            (columns, source_total) if final else (source_total, columns), jnp.float32
+        ),
         input_output_aliases=aliases,
         compiler_params=pltpu.CompilerParams(
             dimension_semantics=("arbitrary", "arbitrary"),
@@ -265,10 +276,11 @@
 
     for m, back, own_grad in pending:
         table_grad = spread(
-            counts_all[m][0], back, own_grad, dest_rows[m], tiles_all[m], table_grad, agg_scale, source_total
+            counts_all[m][0], back, own_grad, dest_rows[m], tiles_all[m], table_grad, agg_scale, source_total,
+            final=True,
         )
     return (
-        table_grad.T,
+        table_grad,
         self_sum * norm_factor,
         neighbor_sum * norm_factor,
         up_sum * norm_factor,

time: 290 us -> 286 us (0.986)
  local copies, waits for them, and re-layouts: 38.1 us -> 32.6 us
  Pallas kernels: 134 us -> 137 us
    unnamed x43 -> x36, local copies, waits for them, and re-layouts: 13.1 us -> 6.54 us
  transfers between devices with their start and end apart: 6 -> 6, of which waited for: 2 -> 2; matrix products, arithmetic and copies ran while one was open for 14% -> 13% of each run, Pallas kernels for 47% -> 48%
where the time goes in v12:
time: 286 us; the launch traced here: 284 us
  Pallas kernels  137 us (48%)
  starting transfers between devices  37.8 us (13%)
  local copies, waits for them, and re-layouts  32.6 us (11%)
  blocking collectives  29.1 us (10%)
  matrix products  19.7 us (7%)
  waiting for transfers between devices  19.5 us (7%)
  other arithmetic  7.37 us (3%)
    pallas_call x2, Pallas kernels, aggregate(): pl.pallas_call(functools.partial(agg_kernel, agg_scale, k_total, nt), gri...  81.2 us
    pallas_call x2, Pallas kernels, spread(): pl.pallas_call(functools.partial(spread_kernel, agg_scale, k_total, nt, f...  55.7 us
    all_to_all x1, blocking collectives, summed_over(): lax.all_to_all(flat, axis, 0, 0, tiled=True).reshape(n, -1).sum(axis=0)  29.1 us
    all_to_all x2, starting transfers between devices, summed_over(): lax.all_to_all(flat, axis, 0, 0, tiled=True).reshape(n, -1).sum(axis=0)  15.1 us
    all_to_all x2, waiting for transfers between devices, summed_over(): lax.all_to_all(flat, axis, 0, 0, tiled=True).reshape(n, -1).sum(axis=0)  14.2 us
    all_to_all x3, starting transfers between devices, summed_over(): lax.all_to_all(jnp.broadcast_to(mine[None], (n, mine.size)), axis, 0, 0,...  12.6 us
    all_to_all x1, starting transfers between devices, gathered_over(): lax.all_to_all(jnp.broadcast_to(x[None], (n, *x.shape)), axis, 0, 0, tile...  10.1 us
    unnamed x36, local copies, waits for them, and re-layouts  6.54 us
  transfers between devices with their start and end apart: 6, of which 2 were waited for; matrix products, arithmetic and copies ran while one was open for 13% of the time, Pallas kernels for 48%

profile of v12, /device:TPU:1, one launch (start us, length us, event | category | flops | bytes accessed | tf_op | source)
XLA Modules:
  0.0 284.1 jit_solution(9628587134407521242)
XLA Ops:
  0.6 1.7 broadcast_in_dim.8
  2.4 10.1 %all-to-all-start = ((bf16[16,2,64,128]{3,2,1,0:T(8,128)(2,1)}), bf16[16,2,64,128]{3,2,1,0:T(8,128)(2,1)}, u32[]{:S(2)}, u32[]{:S(2)}) async-start(bf16[16,2,64,128]{3,2,1,0:T(8,128)(2,1)} %broadcast_in_dim.8), calls=%async_computation | async-start | bytes 1048576 | tf_op jit(solution)/shard_map/all_to_all | solution.py:51
  16.2 2.0 copy.70
  18.2 3.2 %gather_fusion.1 = bf16[1024,64]{1,0:T(8,128)(2,1)S(1)} fusion(bf16[8192,64]{1,0:T(8,128)(2,1)S(1)} %bitcast.81, s32[1024]{0:T(1024)S(1)} %broadcast_clamp_fusion), kind=kCustom, calls=%fused_computation.1 | custom fusion | bytes 266240 | tf_op jit(solution)/shard_map/gather | solution.py:231
  21.4 2.3 slice_bitcast_fusion
  23.7 40.5 %shard_map.147 = (bf16[8,4,1024,256]{3,2,1,0:T(8,128)(2,1)}, bf16[64,1024]{1,0:T(8,128)(2,1)}) custom-call(s32[32]{0:T(128)} %squeeze.37.tiles_ref, bf16[64,8192]{1,0:T(8,128)(2,1)} %emb_ref.3, s32[8,1,16,1024]{3,2,1,0:T(8,128)} %get-tuple-element.19.rows_ref, s32[8,1,1,1024]{3,2,1,0:T(1,128)} %get-tuple-element.33.mask_ref), custom_call_target="tpu_custom_call" | custom-call | flops 1610612736 | bytes 17825792 | tf_op jit(solution)/shard_map/pallas_call | solution.py:110
  64.5 2.0 convolution_add_fusion
  66.5 7.5 %all-to-all-start.3 = ((f32[16,1,8192]{2,1,0:T(1,128)}), f32[16,1,8192]{2,1,0:T(1,128)S(1)}, u32[]{:S(2)}, u32[]{:S(2)}) async-start(f32[16,1,8192]{2,1,0:T(1,128)} %bitcast.93), calls=%async_computation.3 | async-start | bytes 1048576 | tf_op jit(solution)/shard_map/all_to_all | solution.py:44
  74.7 3.2 %gather_fusion = bf16[1024,64]{1,0:T(8,128)(2,1)S(1)} fusion(bf16[8192,64]{1,0:T(8,128)(2,1)S(1)} %bitcast.82, s32[1024]{0:T(1024)S(1)} %broadcast_clamp_fusion.1), kind=kCustom, calls=%fused_computation | custom fusion | bytes 266240 | tf_op jit(solution)/shard_map/gather | solution.py:231
  77.9 40.7 %shard_map.146 = (bf16[8,4,1024,256]{3,2,1,0:T(8,128)(2,1)}, bf16[64,1024]{1,0:T(8,128)(2,1)}) custom-call(s32[32]{0:T(128)} %squeeze.32.tiles_ref, bf16[64,8192]{1,0:T(8,128)(2,1)} %emb_ref.3, s32[8,1,16,1024]{3,2,1,0:T(8,128)} %get-tuple-element.20.rows_ref, s32[8,1,1,1024]{3,2,1,0:T(1,128)} %get-tuple-element.34.mask_ref), custom_call_target="tpu_custom_call" | custom-call | flops 1610612736 | bytes 17825792 | tf_op jit(solution)/shard_map/pallas_call | solution.py:110
  118.8 2.0 convolution_add_fusion.1
  120.7 7.5 %all-to-all-start.1 = ((f32[16,1,8192]{2,1,0:T(1,128)}), f32[16,1,8192]{2,1,0:T(1,128)S(1)}, u32[]{:S(2)}, u32[]{:S(2)}) async-start(f32[16,1,8192]{2,1,0:T(1,128)} %bitcast.10), calls=%async_computation.1 | async-start | bytes 1048576 | tf_op jit(solution)/shard_map/all_to_all | solution.py:44
  128.7 14.2 %all-to-all-done.1 = f32[16,1,8192]{2,1,0:T(1,128)S(1)} async-done(((f32[16,1,8192]{2,1,0:T(1,128)}), f32[16,1,8192]{2,1,0:T(1,128)S(1)}, u32[]{:S(2)}, u32[]{:S(2)}) %all-to-all-start.1) | async-done | bytes 524320 | tf_op jit(solution)/shard_map/all_to_all | solution.py:44
  142.9 1.2 broadcast_in_dim.10
  144.1 4.4 %all-to-all-start.4 = ((f32[16,1,8192]{2,1,0:T(1,128)}), f32[16,1,8192]{2,1,0:T(1,128)S(1)}, u32[]{:S(2)}, u32[]{:S(2)}) async-start(f32[16,1,8192]{2,1,0:T(1,128)} %broadcast_in_dim.10), calls=%async_computation.4 | async-start | bytes 1048576 | tf_op jit(solution)/shard_map/all_to_all | solution.py:45
  149.7 3.2 %scatter_custom_fusion = bf16[1024,128]{1,0:T(8,128)(2,1)S(1)} fusion(s32[1024]{0:T(1024)S(1)} %bitcast.101, bf16[1024,128]{1,0:T(8,128)(2,1)S(1)} %bitcast.95, bf16[]{:T(256)} %constant.12.clone.1), kind=kCustom, calls=%fused_computation.69 | custom fusion | bytes 262146 | tf_op jit(solution)/shard_map/scatter | solution.py:251
  153.0 3.2 %scatter_custom_fusion.1 = bf16[1024,128]{1,0:T(8,128)(2,1)S(1)} fusion(s32[1024]{0:T(1024)S(1)} %bitcast.100, bf16[1024,128]{1,0:T(8,128)(2,1)S(1)} %bitcast.94, bf16[]{:T(256)} %constant.12.clone.1), kind=kCustom, calls=%fused_computation.67 | custom fusion | bytes 262146 | tf_op jit(solution)/shard_map/scatter | solution.py:251
  156.6 5.3 %all-to-all-done.4 = f32[16,1,8192]{2,1,0:T(1,128)S(1)} async-done(((f32[16,1,8192]{2,1,0:T(1,128)}), f32[16,1,8192]{2,1,0:T(1,128)S(1)}, u32[]{:S(2)}, u32[]{:S(2)}) %all-to-all-start.4) | async-done | bytes 524320 | tf_op jit(solution)/shard_map/all_to_all | solution.py:45
  161.9 1.2 broadcast_in_dim.9
  163.1 4.3 %all-to-all-start.2 = ((f32[16,1,8192]{2,1,0:T(1,128)}), f32[16,1,8192]{2,1,0:T(1,128)S(1)}, u32[]{:S(2)}, u32[]{:S(2)}) async-start(f32[16,1,8192]{2,1,0:T(1,128)} %broadcast_in_dim.9), calls=%async_computation.2 | async-start | bytes 1048576 | tf_op jit(solution)/shard_map/all_to_all | solution.py:45
  168.1 3.0 %fusion.7 = bf16[1024,1024]{1,0:T(8,128)(2,1)S(1)} fusion(f32[1024,1024]{1,0:T(8,128)S(1)} %fusion.50, bf16[1024,128]{1,0:T(8,128)(2,1)S(1)} %scatter_custom_fusion.1, bf16[1024,128]{1,0:T(8,128)(2,1)S(1)} %copy-done.15), kind=kOutput, calls=%fused_computation.15 | convolution fusion | flops 288358400 | bytes 6815744 | tf_op jit(solution)/shard_map/dot_general | solution.py:32
  173.0 26.6 %shard_map.148.refs_0_ = f32[8192,64]{1,0:T(8,128)S(1)} custom-call(s32[1056]{0:T(1024)S(1)} %pad_add_fusion.1.tiles_ref, bf16[8,4,1024,256]{3,2,1,0:T(8,128)(2,1)} %get-tuple-element.13.counts_ref, bf16[1024,64]{1,0:T(8,128)(2,1)S(1)} %copy.75.back_ref, f32[1024,64]{1,0:T(8,128)S(1)} %fusion.58.own_ref), custom_call_target="tpu_custom_call" | custom-call | flops 1073741824 | bytes 20971520 | tf_op jit(solution)/shard_map/pallas_call | solution.py:186
  199.6 1.9 copy-done.1
  202.2 1.7 fusion.16
  204.9 3.0 %fusion.15 = bf16[1024,1024]{1,0:T(8,128)(2,1)S(1)} fusion(f32[1024,1024]{1,0:T(8,128)S(1)} %fusion.51, bf16[1024,128]{1,0:T(8,128)(2,1)S(1)} %scatter_custom_fusion, bf16[1024,128]{1,0:T(8,128)(2,1)S(1)} %copy-done.16), kind=kOutput, calls=%fused_computation.23 | convolution fusion | flops 288358400 | bytes 6815744 | tf_op jit(solution)/shard_map/dot_general | solution.py:32
  207.8 1.7 fusion.19
  211.7 29.1 %all_to_all.50 = f32[16,1,17408]{2,1,0:T(1,128)S(1)} all-to-all(f32[16,1,17408]{2,1,0:T(1,128)S(1)} %bitcast.91), channel_id=1, replica_groups=mesh['batch'=16,'feat'=16] {'batch'}, dimensions={0} | all-to-all | bytes 2228224 | tf_op jit(solution)/shard_map/all_to_all | solution.py:44
  241.5 1.6 broadcast_in_dim.11
  243.1 3.9 %all-to-all-start.6 = ((f32[16,1,17408]{2,1,0:T(1,128)}), f32[16,1,17408]{2,1,0:T(1,128)S(1)}, u32[]{:S(2)}, u32[]{:S(2)}) async-start(f32[16,1,17408]{2,1,0:T(1,128)} %broadcast_in_dim.11), calls=%async_computation.6 | async-start | bytes 2228224 | tf_op jit(solution)/shard_map/all_to_all | solution.py:45
  247.7 2.2 copy-done.2
  249.9 29.1 %shard_map.149 = f32[64,8192]{1,0:T(8,128)} custom-call(s32[1056]{0:T(1024)S(1)} %pad_add_fusion.tiles_ref, bf16[8,4,1024,256]{3,2,1,0:T(8,128)(2,1)} %get-tuple-element.11.counts_ref, bf16[1024,64]{1,0:T(8,128)(2,1)S(1)} %copy.77.back_ref, f32[1024,64]{1,0:T(8,128)S(1)} %fusion.59.own_ref, f32[8192,64]{1,0:T(8,128)S(1)} %copy-done.2), custom_call_target="tpu_custom_call" | custom-call | flops 1073741824 | bytes 20971520 | tf_op jit(solution)/shard_map/pallas_call | solution.py:186
  280.5 2.6 reduce.3
  (78 shorter events, 16.6 us)
Async XLA Ops:
  0.6 166.7 %copy-start = (bf16[128,1024]{1,0:T(8,128)(2,1)S(1)}, bf16[128,1024]{1,0:T(8,128)(2,1)}, u32[]{:S(2)}) copy-start(bf16[128,1024]{1,0:T(8,128)(2,1)} %param.14) | copy-start | bytes 786436
  2.4 64.1 %all-to-all-start = ((bf16[16,2,64,128]{3,2,1,0:T(8,128)(2,1)}), bf16[16,2,64,128]{3,2,1,0:T(8,128)(2,1)}, u32[]{:S(2)}, u32[]{:S(2)}) async-start(bf16[16,2,64,128]{3,2,1,0:T(8,128)(2,1)} %broadcast_in_dim.8), calls=%async_computation | async-start | bytes 1048576 | tf_op jit(solution)/shard_map/all_to_all | solution.py:51
  21.4 42.9 %copy-start.10 = (bf16[64,128]{1,0:T(8,128)(2,1)S(1)}, bf16[64,128]{1,0:T(8,128)(2,1)}, u32[]{:S(2)}) copy-start(bf16[64,128]{1,0:T(8,128)(2,1)} %param.12) | copy-start | bytes 49156
  21.4 43.0 %copy-start.9 = (bf16[64,128]{1,0:T(8,128)(2,1)S(1)}, bf16[64,128]{1,0:T(8,128)(2,1)}, u32[]{:S(2)}) copy-start(bf16[64,128]{1,0:T(8,128)(2,1)} %param.13) | copy-start | bytes 49156
  66.5 54.3 %all-to-all-start.3 = ((f32[16,1,8192]{2,1,0:T(1,128)}), f32[16,1,8192]{2,1,0:T(1,128)S(1)}, u32[]{:S(2)}, u32[]{:S(2)}) async-start(f32[16,1,8192]{2,1,0:T(1,128)} %bitcast.93), calls=%async_computation.3 | async-start | bytes 1048576 | tf_op jit(solution)/shard_map/all_to_all | solution.py:44
  77.9 70.6 %copy-start.11 = (s32[2,1024]{1,0:T(2,128)S(1)}, s32[2,1024]{1,0:T(2,128)}, u32[]{:S(2)}) copy-start(s32[2,1024]{1,0:T(2,128)} %param.19) | copy-start | bytes 24580
  77.9 70.6 %copy-start.14 = (s32[32]{0:T(128)S(1)}, s32[32]{0:T(128)}, u32[]{:S(2)}) copy-start(s32[32]{0:T(128)} %squeeze.37.tiles_ref) | copy-start | bytes 388
  77.9 70.7 %copy-start.12 = (s32[2,1,1024]{2,1,0:T(1,128)S(1)}, s32[2,1,1024]{2,1,0:T(1,128)}, u32[]{:S(2)}) copy-start(s32[2,1,1024]{2,1,0:T(1,128)} %param.20) | copy-start | bytes 24580
  120.7 22.1 %all-to-all-start.1 = ((f32[16,1,8192]{2,1,0:T(1,128)}), f32[16,1,8192]{2,1,0:T(1,128)S(1)}, u32[]{:S(2)}, u32[]{:S(2)}) async-start(f32[16,1,8192]{2,1,0:T(1,128)} %bitcast.10), calls=%async_computation.1 | async-start | bytes 1048576 | tf_op jit(solution)/shard_map/all_to_all | solution.py:44
  144.1 17.8 %all-to-all-start.4 = ((f32[16,1,8192]{2,1,0:T(1,128)}), f32[16,1,8192]{2,1,0:T(1,128)S(1)}, u32[]{:S(2)}, u32[]{:S(2)}) async-start(f32[16,1,8192]{2,1,0:T(1,128)} %broadcast_in_dim.10), calls=%async_computation.4 | async-start | bytes 1048576 | tf_op jit(solution)/shard_map/all_to_all | solution.py:45
  148.6 19.5 %copy-start.15 = (bf16[1024,128]{1,0:T(8,128)(2,1)S(1)}, bf16[1024,128]{1,0:T(8,128)(2,1)}, u32[]{:S(2)}) copy-start(bf16[1024,128]{1,0:T(8,128)(2,1)} %param.15) | copy-start | bytes 786436
  163.1 40.9 %all-to-all-start.2 = ((f32[16,1,8192]{2,1,0:T(1,128)}), f32[16,1,8192]{2,1,0:T(1,128)S(1)}, u32[]{:S(2)}, u32[]{:S(2)}) async-start(f32[16,1,8192]{2,1,0:T(1,128)} %broadcast_in_dim.9), calls=%async_computation.2 | async-start | bytes 1048576 | tf_op jit(solution)/shard_map/all_to_all | solution.py:45
  168.1 3.0 %copy-start.3 = (f32[1024,1024]{1,0:T(8,128)}, f32[1024,1024]{1,0:T(8,128)S(1)}, u32[]{:S(2)}) copy-start(f32[1024,1024]{1,0:T(8,128)S(1)} %fusion.50) | copy-start | bytes 12582916
  171.1 1.5 copy-start.5
  171.1 1.1 copy-start.8
  173.0 28.6 %copy-start.6 = (bf16[1024,1024]{1,0:T(8,128)(2,1)S(1)}, bf16[1024,1024]{1,0:T(8,128)(2,1)}, u32[]{:S(2)}) copy-start(bf16[1024,1024]{1,0:T(8,128)(2,1)} %copy-done.5) | copy-start | bytes 6291460
  173.0 29.2 %copy-start.4 = (f32[1024,1024]{1,0:T(8,128)S(1)}, f32[1024,1024]{1,0:T(8,128)}, u32[]{:S(2)}) copy-start(f32[1024,1024]{1,0:T(8,128)} %copy-done.3) | copy-start | bytes 12582916
  199.6 1.9 copy-start.1
  203.9 1.0 copy-start.16
  209.6 1.7 copy-start.7
  211.6 35.5 %copy-start.13 = (s32[32]{0:T(128)S(1)}, s32[32]{0:T(128)}, u32[]{:S(2)}) copy-start(s32[32]{0:T(128)} %squeeze.32.tiles_ref) | copy-start | bytes 388
  243.1 35.9 %all-to-all-start.6 = ((f32[16,1,17408]{2,1,0:T(1,128)}), f32[16,1,17408]{2,1,0:T(1,128)S(1)}, u32[]{:S(2)}, u32[]{:S(2)}) async-start(f32[16,1,17408]{2,1,0:T(1,128)} %broadcast_in_dim.11), calls=%async_computation.6 | async-start | bytes 2228224 | tf_op jit(solution)/shard_map/all_to_all | solution.py:45
  247.7 2.2 copy-start.2

commit v13 on v12

--- a/solution.py
+++ b/solution.py
@@ -224,12 +224,13 @@
     tiles_all = source_tiles.reshape(micro_total, -1)
 
     target_all = gathered_over(output_grad, "feat", 1)
-    table = embedding.T
     counts_all, own_all, hidden_all = [], [], []
     for m in range(micro_total):
         counts, agg_t = aggregate(embedding, tiles_all[m], neighbor_rows[m], slot_mask[m], agg_scale)
-        own = table[dest_rows[m]]
-        partial = jnp.dot(own, self_weight, preferred_element_type=jnp.float32) + lax.dot_general(
+        own = jnp.take(embedding, dest_rows[m], axis=1)
+        partial = lax.dot_general(
+            own, self_weight, (((0,), (0,)), ((), ())), preferred_element_type=jnp.float32
+        ) + lax.dot_general(
             agg_t, neighbor_weight, (((0,), (0,)), ((), ())), preferred_element_type=jnp.float32
         )
         counts_all.append((counts, agg_t))
@@ -252,7 +253,7 @@
         hidden_grad, up_part, down_part = mlp_pass(hidden, target, up_weight, down_weight)
         up_sum = up_sum + up_part
         down_sum = down_sum + down_part
-        self_sum = self_sum + jnp.dot(own_all[m].T, hidden_grad, preferred_element_type=jnp.float32)
+        self_sum = self_sum + jnp.dot(own_all[m], hidden_grad, preferred_element_type=jnp.float32)
         neighbor_sum = neighbor_sum + jnp.dot(agg_t, hidden_grad, preferred_element_type=jnp.float32)
         back = jnp.dot(hidden_grad, neighbor_weight.T, preferred_element_type=jnp.float32).astype(jnp.bfloat16)
         own_grad = jnp.dot(hidden_grad, self_weight.T, preferred_element_type=jnp.float32)

time: 286 us -> 288 us (level)
    unnamed x36 -> x38, local copies, waits for them, and re-layouts: 6.54 us -> 6.62 us
where the time goes in v13:
time: 288 us; the launch traced here: 286 us
  Pallas kernels  137 us (48%)
  starting transfers between devices  37.8 us (13%)
  local copies, waits for them, and re-layouts  33.5 us (12%)
  blocking collectives  29.1 us (10%)
  waiting for transfers between devices  20.5 us (7%)
  matrix products  20.2 us (7%)
  other arithmetic  6.61 us (2%)
    pallas_call x2, Pallas kernels, aggregate(): pl.pallas_call(functools.partial(agg_kernel, agg_scale, k_total, nt), gri...  81.2 us
    pallas_call x2, Pallas kernels, spread(): pl.pallas_call(functools.partial(spread_kernel, agg_scale, k_total, nt, f...  55.7 us
    all_to_all x1, blocking collectives, summed_over(): lax.all_to_all(flat, axis, 0, 0, tiled=True).reshape(n, -1).sum(axis=0)  29.1 us
    all_to_all x2, starting transfers between devices, summed_over(): lax.all_to_all(flat, axis, 0, 0, tiled=True).reshape(n, -1).sum(axis=0)  15.1 us
    all_to_all x2, waiting for transfers between devices, summed_over(): lax.all_to_all(flat, axis, 0, 0, tiled=True).reshape(n, -1).sum(axis=0)  14.2 us
    all_to_all x3, starting transfers between devices, summed_over(): lax.all_to_all(jnp.broadcast_to(mine[None], (n, mine.size)), axis, 0, 0,...  12.7 us
    all_to_all x1, starting transfers between devices, gathered_over(): lax.all_to_all(jnp.broadcast_to(x[None], (n, *x.shape)), axis, 0, 0, tile...  10 us
    gather x2, local copies, waits for them, and re-layouts, local(): own = jnp.take(embedding, dest_rows[m], axis=1)  7.51 us
  transfers between devices with their start and end apart: 6, of which 2 were waited for; matrix products, arithmetic and copies ran while one was open for 13% of the time, Pallas kernels for 48%

profile of v13, /device:TPU:1, one launch (start us, length us, event | category | flops | bytes accessed | tf_op | source)
XLA Modules:
  0.0 285.9 jit_solution(15260561295523582970)
XLA Ops:
  0.6 1.7 broadcast_in_dim.17
  2.4 10.0 %all-to-all-start = ((bf16[16,2,64,128]{3,2,1,0:T(8,128)(2,1)}), bf16[16,2,64,128]{3,2,1,0:T(8,128)(2,1)S(1)}, u32[]{:S(2)}, u32[]{:S(2)}) async-start(bf16[16,2,64,128]{3,2,1,0:T(8,128)(2,1)} %broadcast_in_dim.17), calls=%async_computation | async-start | bytes 1048576 | tf_op jit(solution)/shard_map/all_to_all | solution.py:51
  14.0 2.3 slice_bitcast_fusion
  18.4 2.0 copy.75
  20.5 3.2 %gather_fusion.1 = bf16[1024,64]{1,0:T(8,128)(2,1)S(1)} fusion(bf16[64,8192]{0,1:T(8,128)(2,1)S(1)} %copy.75, s32[1024]{0:T(1024)S(1)} %fusion.49), kind=kCustom, calls=%fused_computation.1.clone | custom fusion | bytes 266240 | tf_op jit(solution)/shard_map/jit(_take)/gather | solution.py:230
  23.7 40.5 %shard_map.147 = (bf16[8,4,1024,256]{3,2,1,0:T(8,128)(2,1)}, bf16[64,1024]{1,0:T(8,128)(2,1)}) custom-call(s32[32]{0:T(128)} %squeeze.32.tiles_ref, bf16[64,8192]{1,0:T(8,128)(2,1)} %emb_ref.3, s32[8,1,16,1024]{3,2,1,0:T(8,128)} %get-tuple-element.20.rows_ref, s32[8,1,1,1024]{3,2,1,0:T(1,128)} %get-tuple-element.32.mask_ref), custom_call_target="tpu_custom_call" | custom-call | flops 1610612736 | bytes 17825792 | tf_op jit(solution)/shard_map/pallas_call | solution.py:110
  64.6 2.0 convolution_add_fusion
  66.6 7.6 %all-to-all-start.3 = ((f32[16,1,8192]{2,1,0:T(1,128)}), f32[16,1,8192]{2,1,0:T(1,128)S(1)}, u32[]{:S(2)}, u32[]{:S(2)}) async-start(f32[16,1,8192]{2,1,0:T(1,128)} %bitcast.17), calls=%async_computation.3 | async-start | bytes 1048576 | tf_op jit(solution)/shard_map/all_to_all | solution.py:44
  74.8 4.3 %gather_fusion = bf16[1024,64]{1,0:T(8,128)(2,1)} fusion(bf16[64,8192]{0,1:T(8,128)(2,1)S(1)} %copy.75, s32[1024]{0:T(1024)S(1)} %fusion.48), kind=kCustom, calls=%fused_computation.clone | custom fusion | bytes 266240 | tf_op jit(solution)/shard_map/jit(_take)/gather | solution.py:230
  79.1 40.7 %shard_map.146 = (bf16[8,4,1024,256]{3,2,1,0:T(8,128)(2,1)}, bf16[64,1024]{1,0:T(8,128)(2,1)}) custom-call(s32[32]{0:T(128)} %squeeze.28.tiles_ref, bf16[64,8192]{1,0:T(8,128)(2,1)} %emb_ref.3, s32[8,1,16,1024]{3,2,1,0:T(8,128)} %get-tuple-element.21.rows_ref, s32[8,1,1,1024]{3,2,1,0:T(1,128)} %get-tuple-element.33.mask_ref), custom_call_target="tpu_custom_call" | custom-call | flops 1610612736 | bytes 17825792 | tf_op jit(solution)/shard_map/pallas_call | solution.py:110
  120.1 2.0 convolution_add_fusion.1
  122.1 7.6 %all-to-all-start.1 = ((f32[16,1,8192]{2,1,0:T(1,128)}), f32[16,1,8192]{2,1,0:T(1,128)S(1)}, u32[]{:S(2)}, u32[]{:S(2)}) async-start(f32[16,1,8192]{2,1,0:T(1,128)} %bitcast.8), calls=%async_computation.1 | async-start | bytes 1048576 | tf_op jit(solution)/shard_map/all_to_all | solution.py:44
  130.0 14.2 %all-to-all-done.1 = f32[16,1,8192]{2,1,0:T(1,128)S(1)} async-done(((f32[16,1,8192]{2,1,0:T(1,128)}), f32[16,1,8192]{2,1,0:T(1,128)S(1)}, u32[]{:S(2)}, u32[]{:S(2)}) %all-to-all-start.1) | async-done | bytes 524320 | tf_op jit(solution)/shard_map/all_to_all | solution.py:44
  144.2 1.2 broadcast_in_dim.19
  145.4 4.5 %all-to-all-start.4 = ((f32[16,1,8192]{2,1,0:T(1,128)}), f32[16,1,8192]{2,1,0:T(1,128)S(1)}, u32[]{:S(2)}, u32[]{:S(2)}) async-start(f32[16,1,8192]{2,1,0:T(1,128)} %broadcast_in_dim.19), calls=%async_computation.4 | async-start | bytes 1048576 | tf_op jit(solution)/shard_map/all_to_all | solution.py:45
  150.0 3.2 %scatter_custom_fusion = bf16[1024,128]{1,0:T(8,128)(2,1)S(1)} fusion(s32[1024]{0:T(1024)S(1)} %bitcast.100, bf16[1024,128]{1,0:T(8,128)(2,1)S(1)} %bitcast.92, bf16[]{:T(256)} %constant.19.clone.1), kind=kCustom, calls=%fused_computation.78 | custom fusion | bytes 262146 | tf_op jit(solution)/shard_map/scatter | solution.py:252
  153.2 3.2 %scatter_custom_fusion.1 = bf16[1024,128]{1,0:T(8,128)(2,1)S(1)} fusion(s32[1024]{0:T(1024)S(1)} %bitcast.99, bf16[1024,128]{1,0:T(8,128)(2,1)S(1)} %bitcast.91, bf16[]{:T(256)} %constant.19.clone.1), kind=kCustom, calls=%fused_computation.76 | custom fusion | bytes 262146 | tf_op jit(solution)/shard_map/scatter | solution.py:252
  156.8 6.4 %all-to-all-done.4 = f32[16,1,8192]{2,1,0:T(1,128)S(1)} async-done(((f32[16,1,8192]{2,1,0:T(1,128)}), f32[16,1,8192]{2,1,0:T(1,128)S(1)}, u32[]{:S(2)}, u32[]{:S(2)}) %all-to-all-start.4) | async-done | bytes 524320 | tf_op jit(solution)/shard_map/all_to_all | solution.py:45
  163.2 1.2 broadcast_in_dim.18
  164.4 4.3 %all-to-all-start.2 = ((f32[16,1,8192]{2,1,0:T(1,128)}), f32[16,1,8192]{2,1,0:T(1,128)S(1)}, u32[]{:S(2)}, u32[]{:S(2)}) async-start(f32[16,1,8192]{2,1,0:T(1,128)} %broadcast_in_dim.18), calls=%async_computation.2 | async-start | bytes 1048576 | tf_op jit(solution)/shard_map/all_to_all | solution.py:45
  169.4 3.0 %fusion.7 = bf16[1024,1024]{1,0:T(8,128)(2,1)S(1)} fusion(f32[1024,1024]{1,0:T(8,128)S(1)} %fusion.63, bf16[1024,128]{1,0:T(8,128)(2,1)S(1)} %scatter_custom_fusion.1, bf16[1024,128]{1,0:T(8,128)(2,1)S(1)} %copy-done.17), kind=kOutput, calls=%fused_computation.15 | convolution fusion | flops 288358400 | bytes 6815744 | tf_op jit(solution)/shard_map/dot_general | solution.py:32
  174.8 26.6 %shard_map.148.refs_0_ = f32[8192,64]{1,0:T(8,128)S(1)} custom-call(s32[1056]{0:T(1024)S(1)} %pad_add_fusion.1.tiles_ref, bf16[8,4,1024,256]{3,2,1,0:T(8,128)(2,1)} %get-tuple-element.14.counts_ref, bf16[1024,64]{1,0:T(8,128)(2,1)S(1)} %copy.81.back_ref, f32[1024,64]{1,0:T(8,128)S(1)} %fusion.69.own_ref), custom_call_target="tpu_custom_call" | custom-call | flops 1073741824 | bytes 20971520 | tf_op jit(solution)/shard_map/pallas_call | solution.py:186
  201.5 1.9 copy-done.1
  204.0 1.7 fusion.16
  206.4 3.0 %fusion.15 = bf16[1024,1024]{1,0:T(8,128)(2,1)S(1)} fusion(f32[1024,1024]{1,0:T(8,128)S(1)} %fusion.64, bf16[1024,128]{1,0:T(8,128)(2,1)S(1)} %scatter_custom_fusion, bf16[1024,128]{1,0:T(8,128)(2,1)S(1)} %copy-done.17), kind=kOutput, calls=%fused_computation.23 | convolution fusion | flops 288358400 | bytes 6815744 | tf_op jit(solution)/shard_map/dot_general | solution.py:32
  209.4 1.7 fusion.19
  213.4 29.1 %all_to_all.50 = f32[16,1,17408]{2,1,0:T(1,128)S(1)} all-to-all(f32[16,1,17408]{2,1,0:T(1,128)S(1)} %bitcast.88), channel_id=1, replica_groups=mesh['batch'=16,'feat'=16] {'batch'}, dimensions={0} | all-to-all | bytes 2228224 | tf_op jit(solution)/shard_map/all_to_all | solution.py:44
  243.3 1.6 broadcast_in_dim.20
  244.9 3.9 %all-to-all-start.6 = ((f32[16,1,17408]{2,1,0:T(1,128)}), f32[16,1,17408]{2,1,0:T(1,128)S(1)}, u32[]{:S(2)}, u32[]{:S(2)}) async-start(f32[16,1,17408]{2,1,0:T(1,128)} %broadcast_in_dim.20), calls=%async_computation.6 | async-start | bytes 2228224 | tf_op jit(solution)/shard_map/all_to_all | solution.py:45
  249.5 2.2 copy-done.2
  251.7 29.1 %shard_map.149 = f32[64,8192]{1,0:T(8,128)} custom-call(s32[1056]{0:T(1024)S(1)} %pad_add_fusion.tiles_ref, bf16[8,4,1024,256]{3,2,1,0:T(8,128)(2,1)} %get-tuple-element.12.counts_ref, bf16[1024,64]{1,0:T(8,128)(2,1)S(1)} %copy.83.back_ref, f32[1024,64]{1,0:T(8,128)S(1)} %fusion.70.own_ref, f32[8192,64]{1,0:T(8,128)S(1)} %copy-done.2), custom_call_target="tpu_custom_call" | custom-call | flops 1073741824 | bytes 20971520 | tf_op jit(solution)/shard_map/pallas_call | solution.py:186
  282.2 2.6 reduce.3
  (81 shorter events, 16.2 us)
Async XLA Ops:
  0.6 168.1 %copy-start = (bf16[128,1024]{1,0:T(8,128)(2,1)S(1)}, bf16[128,1024]{1,0:T(8,128)(2,1)}, u32[]{:S(2)}) copy-start(bf16[128,1024]{1,0:T(8,128)(2,1)} %param.16) | copy-start | bytes 786436
  2.4 64.2 %all-to-all-start = ((bf16[16,2,64,128]{3,2,1,0:T(8,128)(2,1)}), bf16[16,2,64,128]{3,2,1,0:T(8,128)(2,1)S(1)}, u32[]{:S(2)}, u32[]{:S(2)}) async-start(bf16[16,2,64,128]{3,2,1,0:T(8,128)(2,1)} %broadcast_in_dim.17), calls=%async_computation | async-start | bytes 1048576 | tf_op jit(solution)/shard_map/all_to_all | solution.py:51
  20.4 43.8 %copy-start.13 = (bf16[64,128]{1,0:T(8,128)(2,1)S(1)}, bf16[64,128]{1,0:T(8,128)(2,1)}, u32[]{:S(2)}) copy-start(bf16[64,128]{1,0:T(8,128)(2,1)} %param.14) | copy-start | bytes 49156
  20.5 44.1 %copy-start.12 = (bf16[64,128]{1,0:T(8,128)(2,1)S(1)}, bf16[64,128]{1,0:T(8,128)(2,1)}, u32[]{:S(2)}) copy-start(bf16[64,128]{1,0:T(8,128)(2,1)} %param.15) | copy-start | bytes 49156
  23.7 42.9 %copy-start.8 = (bf16[1024,64]{1,0:T(8,128)(2,1)}, bf16[1024,64]{1,0:T(8,128)(2,1)S(1)}, u32[]{:S(2)}) copy-start(bf16[1024,64]{1,0:T(8,128)(2,1)S(1)} %gather_fusion.1) | copy-start | bytes 393220
  66.6 55.5 %all-to-all-start.3 = ((f32[16,1,8192]{2,1,0:T(1,128)}), f32[16,1,8192]{2,1,0:T(1,128)S(1)}, u32[]{:S(2)}, u32[]{:S(2)}) async-start(f32[16,1,8192]{2,1,0:T(1,128)} %bitcast.17), calls=%async_computation.3 | async-start | bytes 1048576 | tf_op jit(solution)/shard_map/all_to_all | solution.py:44
  79.1 40.7 %copy-start.7 = (bf16[1024,64]{1,0:T(8,128)(2,1)S(1)}, bf16[1024,64]{1,0:T(8,128)(2,1)}, u32[]{:S(2)}) copy-start(bf16[1024,64]{1,0:T(8,128)(2,1)} %gather_fusion) | copy-start | bytes 393220
  79.1 70.7 %copy-start.16 = (s32[32]{0:T(128)S(1)}, s32[32]{0:T(128)}, u32[]{:S(2)}) copy-start(s32[32]{0:T(128)} %squeeze.32.tiles_ref) | copy-start | bytes 388
  79.1 70.8 %copy-start.14 = (s32[2,1,1024]{2,1,0:T(1,128)S(1)}, s32[2,1,1024]{2,1,0:T(1,128)}, u32[]{:S(2)}) copy-start(s32[2,1,1024]{2,1,0:T(1,128)} %param.22) | copy-start | bytes 24580
  122.1 22.1 %all-to-all-start.1 = ((f32[16,1,8192]{2,1,0:T(1,128)}), f32[16,1,8192]{2,1,0:T(1,128)S(1)}, u32[]{:S(2)}, u32[]{:S(2)}) async-start(f32[16,1,8192]{2,1,0:T(1,128)} %bitcast.8), calls=%async_computation.1 | async-start | bytes 1048576 | tf_op jit(solution)/shard_map/all_to_all | solution.py:44
  145.4 17.8 %all-to-all-start.4 = ((f32[16,1,8192]{2,1,0:T(1,128)}), f32[16,1,8192]{2,1,0:T(1,128)S(1)}, u32[]{:S(2)}, u32[]{:S(2)}) async-start(f32[16,1,8192]{2,1,0:T(1,128)} %broadcast_in_dim.19), calls=%async_computation.4 | async-start | bytes 1048576 | tf_op jit(solution)/shard_map/all_to_all | solution.py:45
  149.9 19.5 %copy-start.17 = (bf16[1024,128]{1,0:T(8,128)(2,1)S(1)}, bf16[1024,128]{1,0:T(8,128)(2,1)}, u32[]{:S(2)}) copy-start(bf16[1024,128]{1,0:T(8,128)(2,1)} %param.17) | copy-start | bytes 786436
  164.4 41.3 %all-to-all-start.2 = ((f32[16,1,8192]{2,1,0:T(1,128)}), f32[16,1,8192]{2,1,0:T(1,128)S(1)}, u32[]{:S(2)}, u32[]{:S(2)}) async-start(f32[16,1,8192]{2,1,0:T(1,128)} %broadcast_in_dim.18), calls=%async_computation.2 | async-start | bytes 1048576 | tf_op jit(solution)/shard_map/all_to_all | solution.py:45
  169.4 3.0 %copy-start.3 = (f32[1024,1024]{1,0:T(8,128)}, f32[1024,1024]{1,0:T(8,128)S(1)}, u32[]{:S(2)}) copy-start(f32[1024,1024]{1,0:T(8,128)S(1)} %fusion.63) | copy-start | bytes 12582916
  172.4 2.0 copy-start.5
  172.5 1.1 copy-start.9
  172.5 1.5 copy-start.11
  174.8 28.6 %copy-start.6 = (bf16[1024,1024]{1,0:T(8,128)(2,1)S(1)}, bf16[1024,1024]{1,0:T(8,128)(2,1)}, u32[]{:S(2)}) copy-start(bf16[1024,1024]{1,0:T(8,128)(2,1)} %copy-done.5) | copy-start | bytes 6291460
  174.8 29.2 %copy-start.4 = (f32[1024,1024]{1,0:T(8,128)S(1)}, f32[1024,1024]{1,0:T(8,128)}, u32[]{:S(2)}) copy-start(f32[1024,1024]{1,0:T(8,128)} %copy-done.3) | copy-start | bytes 12582916
  201.4 1.9 copy-start.1
  211.2 1.9 copy-start.10
  213.3 35.5 %copy-start.15 = (s32[32]{0:T(128)S(1)}, s32[32]{0:T(128)}, u32[]{:S(2)}) copy-start(s32[32]{0:T(128)} %squeeze.28.tiles_ref) | copy-start | bytes 388
  244.9 35.9 %all-to-all-start.6 = ((f32[16,1,17408]{2,1,0:T(1,128)}), f32[16,1,17408]{2,1,0:T(1,128)S(1)}, u32[]{:S(2)}, u32[]{:S(2)}) async-start(f32[16,1,17408]{2,1,0:T(1,128)} %broadcast_in_dim.20), calls=%async_computation.6 | async-start | bytes 2228224 | tf_op jit(solution)/shard_map/all_to_all | solution.py:45
  249.5 2.2 copy-start.2

commit v14 on v12

--- a/solution.py
+++ b/solution.py
@@ -74,7 +74,7 @@
         for j in range(0, NB, 2):
             here = local[j : j + 1, :].astype(jnp.bfloat16)
             there = local[j + 1 : j + 2, :].astype(jnp.bfloat16)
-            cnt = cnt + (jnp.where(here == local_iota, one, zero) + jnp.where(there == local_iota, one, zero))
+            cnt = cnt + ((here == local_iota).astype(jnp.bfloat16) + (there == local_iota).astype(jnp.bfloat16))
         counts_ref[0, 0, pl.ds(start, CS), :] = cnt * msk
         return carry
 

time: 286 us -> 459 us (1.60)
  Pallas kernels: 137 us -> 310 us
    pallas_call x2, Pallas kernels: 81.2 us -> 254 us  [aggregate(): pl.pallas_call(functools.partial(agg_kernel, agg_scale, k_total, nt), gri...]
  transfers between devices with their start and end apart: 6 -> 6, of which waited for: 2 -> 2; matrix products, arithmetic and copies ran while one was open for 13% -> 8% of each run, Pallas kernels for 48% -> 68%
where the time goes in v14:
time: 459 us; the launch traced here: 457 us
  Pallas kernels  310 us (68%)
  starting transfers between devices  37.8 us (8%)
  local copies, waits for them, and re-layouts  32.6 us (7%)
  blocking collectives  29.1 us (6%)
  matrix products  19.7 us (4%)
  waiting for transfers between devices  19.5 us (4%)
  other arithmetic  7.37 us (2%)
    pallas_call x2, Pallas kernels, aggregate(): pl.pallas_call(functools.partial(agg_kernel, agg_scale, k_total, nt), gri...  254 us
    pallas_call x2, Pallas kernels, spread(): pl.pallas_call(functools.partial(spread_kernel, agg_scale, k_total, nt, f...  55.7 us
    all_to_all x1, blocking collectives, summed_over(): lax.all_to_all(flat, axis, 0, 0, tiled=True).reshape(n, -1).sum(axis=0)  29.1 us
    all_to_all x2, starting transfers between devices, summed_over(): lax.all_to_all(flat, axis, 0, 0, tiled=True).reshape(n, -1).sum(axis=0)  15.1 us
    all_to_all x2, waiting for transfers between devices, summed_over(): lax.all_to_all(flat, axis, 0, 0, tiled=True).reshape(n, -1).sum(axis=0)  14.2 us
    all_to_all x3, starting transfers between devices, summed_over(): lax.all_to_all(jnp.broadcast_to(mine[None], (n, mine.size)), axis, 0, 0,...  12.6 us
    all_to_all x1, starting transfers between devices, gathered_over(): lax.all_to_all(jnp.broadcast_to(x[None], (n, *x.shape)), axis, 0, 0, tile...  10.1 us
  transfers between devices with their start and end apart: 6, of which 2 were waited for; matrix products, arithmetic and copies ran while one was open for 8% of the time, Pallas kernels for 68%

profile of v14, /device:TPU:1, one launch (start us, length us, event | category | flops | bytes accessed | tf_op | source)
XLA Modules:
  0.0 457.2 jit_solution(1087411453206130885)
XLA Ops:
  0.6 1.7 broadcast_in_dim.8
  2.4 10.1 %all-to-all-start = ((bf16[16,2,64,128]{3,2,1,0:T(8,128)(2,1)}), bf16[16,2,64,128]{3,2,1,0:T(8,128)(2,1)}, u32[]{:S(2)}, u32[]{:S(2)}) async-start(bf16[16,2,64,128]{3,2,1,0:T(8,128)(2,1)} %broadcast_in_dim.8), calls=%async_computation | async-start | bytes 1048576 | tf_op jit(solution)/shard_map/all_to_all | solution.py:51
  16.2 2.0 copy.70
  18.2 3.2 gather_fusion.1
  21.4 2.3 slice_bitcast_fusion
  23.7 127.1 %shard_map.147 = (bf16[8,4,1024,256]{3,2,1,0:T(8,128)(2,1)}, bf16[64,1024]{1,0:T(8,128)(2,1)}) custom-call(s32[32]{0:T(128)} %squeeze.37.tiles_ref, bf16[64,8192]{1,0:T(8,128)(2,1)} %emb_ref.3, s32[8,1,16,1024]{3,2,1,0:T(8,128)} %get-tuple-element.19.rows_ref, s32[8,1,1,1024]{3,2,1,0:T(1,128)} %get-tuple-element.33.mask_ref), custom_call_target="tpu_custom_call" | custom-call | flops 1610612736 | bytes 17825792 | tf_op jit(solution)/shard_map/pallas_call | solution.py:110
  151.0 2.0 convolution_add_fusion
  153.0 7.5 %all-to-all-start.3 = ((f32[16,1,8192]{2,1,0:T(1,128)}), f32[16,1,8192]{2,1,0:T(1,128)S(1)}, u32[]{:S(2)}, u32[]{:S(2)}) async-start(f32[16,1,8192]{2,1,0:T(1,128)} %bitcast.93), calls=%async_computation.3 | async-start | bytes 1048576 | tf_op jit(solution)/shard_map/all_to_all | solution.py:44
  161.2 3.2 gather_fusion
  164.4 127.2 %shard_map.146 = (bf16[8,4,1024,256]{3,2,1,0:T(8,128)(2,1)}, bf16[64,1024]{1,0:T(8,128)(2,1)}) custom-call(s32[32]{0:T(128)} %squeeze.32.tiles_ref, bf16[64,8192]{1,0:T(8,128)(2,1)} %emb_ref.3, s32[8,1,16,1024]{3,2,1,0:T(8,128)} %get-tuple-element.20.rows_ref, s32[8,1,1,1024]{3,2,1,0:T(1,128)} %get-tuple-element.34.mask_ref), custom_call_target="tpu_custom_call" | custom-call | flops 1610612736 | bytes 17825792 | tf_op jit(solution)/shard_map/pallas_call | solution.py:110
  291.9 2.0 convolution_add_fusion.1
  293.8 7.6 %all-to-all-start.1 = ((f32[16,1,8192]{2,1,0:T(1,128)}), f32[16,1,8192]{2,1,0:T(1,128)S(1)}, u32[]{:S(2)}, u32[]{:S(2)}) async-start(f32[16,1,8192]{2,1,0:T(1,128)} %bitcast.10), calls=%async_computation.1 | async-start | bytes 1048576 | tf_op jit(solution)/shard_map/all_to_all | solution.py:44
  301.8 14.2 %all-to-all-done.1 = f32[16,1,8192]{2,1,0:T(1,128)S(1)} async-done(((f32[16,1,8192]{2,1,0:T(1,128)}), f32[16,1,8192]{2,1,0:T(1,128)S(1)}, u32[]{:S(2)}, u32[]{:S(2)}) %all-to-all-start.1) | async-done | bytes 524320 | tf_op jit(solution)/shard_map/all_to_all | solution.py:44
  316.0 1.2 broadcast_in_dim.10
  317.2 4.4 all-to-all-start.4
  322.9 3.2 scatter_custom_fusion
  326.1 3.2 scatter_custom_fusion.1
  329.7 5.3 %all-to-all-done.4 = f32[16,1,8192]{2,1,0:T(1,128)S(1)} async-done(((f32[16,1,8192]{2,1,0:T(1,128)}), f32[16,1,8192]{2,1,0:T(1,128)S(1)}, u32[]{:S(2)}, u32[]{:S(2)}) %all-to-all-start.4) | async-done | bytes 524320 | tf_op jit(solution)/shard_map/all_to_all | solution.py:45
  335.0 1.2 broadcast_in_dim.9
  336.2 4.3 all-to-all-start.2
  341.2 3.0 fusion.7
  346.1 26.6 %shard_map.148.refs_0_ = f32[8192,64]{1,0:T(8,128)S(1)} custom-call(s32[1056]{0:T(1024)S(1)} %pad_add_fusion.1.tiles_ref, bf16[8,4,1024,256]{3,2,1,0:T(8,128)(2,1)} %get-tuple-element.13.counts_ref, bf16[1024,64]{1,0:T(8,128)(2,1)S(1)} %copy.75.back_ref, f32[1024,64]{1,0:T(8,128)S(1)} %fusion.58.own_ref), custom_call_target="tpu_custom_call" | custom-call | flops 1073741824 | bytes 20971520 | tf_op jit(solution)/shard_map/pallas_call | solution.py:186
  372.8 1.9 copy-done.1
  375.3 1.7 fusion.16
  378.0 3.0 fusion.15
  381.0 1.7 fusion.19
  384.8 29.1 %all_to_all.50 = f32[16,1,17408]{2,1,0:T(1,128)S(1)} all-to-all(f32[16,1,17408]{2,1,0:T(1,128)S(1)} %bitcast.91), channel_id=1, replica_groups=mesh['batch'=16,'feat'=16] {'batch'}, dimensions={0} | all-to-all | bytes 2228224 | tf_op jit(solution)/shard_map/all_to_all | solution.py:44
  414.6 1.6 broadcast_in_dim.11
  416.2 3.9 all-to-all-start.6
  420.8 2.2 copy-done.2
  423.0 29.1 %shard_map.149 = f32[64,8192]{1,0:T(8,128)} custom-call(s32[1056]{0:T(1024)S(1)} %pad_add_fusion.tiles_ref, bf16[8,4,1024,256]{3,2,1,0:T(8,128)(2,1)} %get-tuple-element.11.counts_ref, bf16[1024,64]{1,0:T(8,128)(2,1)S(1)} %copy.77.back_ref, f32[1024,64]{1,0:T(8,128)S(1)} %fusion.59.own_ref, f32[8192,64]{1,0:T(8,128)S(1)} %copy-done.2), custom_call_target="tpu_custom_call" | custom-call | flops 1073741824 | bytes 20971520 | tf_op jit(solution)/shard_map/pallas_call | solution.py:186
  453.6 2.6 reduce.3
  (78 shorter events, 16.6 us)
Async XLA Ops:
  0.6 339.8 %copy-start = (bf16[128,1024]{1,0:T(8,128)(2,1)S(1)}, bf16[128,1024]{1,0:T(8,128)(2,1)}, u32[]{:S(2)}) copy-start(bf16[128,1024]{1,0:T(8,128)(2,1)} %param.14) | copy-start | bytes 786436
  2.4 150.7 %all-to-all-start = ((bf16[16,2,64,128]{3,2,1,0:T(8,128)(2,1)}), bf16[16,2,64,128]{3,2,1,0:T(8,128)(2,1)}, u32[]{:S(2)}, u32[]{:S(2)}) async-start(bf16[16,2,64,128]{3,2,1,0:T(8,128)(2,1)} %broadcast_in_dim.8), calls=%async_computation | async-start | bytes 1048576 | tf_op jit(solution)/shard_map/all_to_all | solution.py:51
  21.4 129.4 %copy-start.10 = (bf16[64,128]{1,0:T(8,128)(2,1)S(1)}, bf16[64,128]{1,0:T(8,128)(2,1)}, u32[]{:S(2)}) copy-start(bf16[64,128]{1,0:T(8,128)(2,1)} %param.12) | copy-start | bytes 49156
  21.4 129.6 %copy-start.9 = (bf16[64,128]{1,0:T(8,128)(2,1)S(1)}, bf16[64,128]{1,0:T(8,128)(2,1)}, u32[]{:S(2)}) copy-start(bf16[64,128]{1,0:T(8,128)(2,1)} %param.13) | copy-start | bytes 49156
  153.0 140.8 %all-to-all-start.3 = ((f32[16,1,8192]{2,1,0:T(1,128)}), f32[16,1,8192]{2,1,0:T(1,128)S(1)}, u32[]{:S(2)}, u32[]{:S(2)}) async-start(f32[16,1,8192]{2,1,0:T(1,128)} %bitcast.93), calls=%async_computation.3 | async-start | bytes 1048576 | tf_op jit(solution)/shard_map/all_to_all | solution.py:44
  164.4 157.2 %copy-start.11 = (s32[2,1024]{1,0:T(2,128)S(1)}, s32[2,1024]{1,0:T(2,128)}, u32[]{:S(2)}) copy-start(s32[2,1024]{1,0:T(2,128)} %param.19) | copy-start | bytes 24580
  164.4 157.2 %copy-start.14 = (s32[32]{0:T(128)S(1)}, s32[32]{0:T(128)}, u32[]{:S(2)}) copy-start(s32[32]{0:T(128)} %squeeze.37.tiles_ref) | copy-start | bytes 388
  164.4 157.3 %copy-start.12 = (s32[2,1,1024]{2,1,0:T(1,128)S(1)}, s32[2,1,1024]{2,1,0:T(1,128)}, u32[]{:S(2)}) copy-start(s32[2,1,1024]{2,1,0:T(1,128)} %param.20) | copy-start | bytes 24580
  293.8 22.2 %all-to-all-start.1 = ((f32[16,1,8192]{2,1,0:T(1,128)}), f32[16,1,8192]{2,1,0:T(1,128)S(1)}, u32[]{:S(2)}, u32[]{:S(2)}) async-start(f32[16,1,8192]{2,1,0:T(1,128)} %bitcast.10), calls=%async_computation.1 | async-start | bytes 1048576 | tf_op jit(solution)/shard_map/all_to_all | solution.py:44
  317.2 17.8 %all-to-all-start.4 = ((f32[16,1,8192]{2,1,0:T(1,128)}), f32[16,1,8192]{2,1,0:T(1,128)S(1)}, u32[]{:S(2)}, u32[]{:S(2)}) async-start(f32[16,1,8192]{2,1,0:T(1,128)} %broadcast_in_dim.10), calls=%async_computation.4 | async-start | bytes 1048576 | tf_op jit(solution)/shard_map/all_to_all | solution.py:45
  321.7 19.5 %copy-start.15 = (bf16[1024,128]{1,0:T(8,128)(2,1)S(1)}, bf16[1024,128]{1,0:T(8,128)(2,1)}, u32[]{:S(2)}) copy-start(bf16[1024,128]{1,0:T(8,128)(2,1)} %param.15) | copy-start | bytes 786436
  336.2 40.8 %all-to-all-start.2 = ((f32[16,1,8192]{2,1,0:T(1,128)}), f32[16,1,8192]{2,1,0:T(1,128)S(1)}, u32[]{:S(2)}, u32[]{:S(2)}) async-start(f32[16,1,8192]{2,1,0:T(1,128)} %broadcast_in_dim.9), calls=%async_computation.2 | async-start | bytes 1048576 | tf_op jit(solution)/shard_map/all_to_all | solution.py:45
  341.2 3.0 copy-start.3
  344.2 1.5 copy-start.5
  344.2 1.1 copy-start.8
  346.1 28.6 %copy-start.6 = (bf16[1024,1024]{1,0:T(8,128)(2,1)S(1)}, bf16[1024,1024]{1,0:T(8,128)(2,1)}, u32[]{:S(2)}) copy-start(bf16[1024,1024]{1,0:T(8,128)(2,1)} %copy-done.5) | copy-start | bytes 6291460
  346.1 29.2 %copy-start.4 = (f32[1024,1024]{1,0:T(8,128)S(1)}, f32[1024,1024]{1,0:T(8,128)}, u32[]{:S(2)}) copy-start(f32[1024,1024]{1,0:T(8,128)} %copy-done.3) | copy-start | bytes 12582916
  372.7 1.9 copy-start.1
  377.0 1.0 copy-start.16
  382.7 1.7 copy-start.7
  384.7 35.4 %copy-start.13 = (s32[32]{0:T(128)S(1)}, s32[32]{0:T(128)}, u32[]{:S(2)}) copy-start(s32[32]{0:T(128)} %squeeze.32.tiles_ref) | copy-start | bytes 388
  416.2 35.9 %all-to-all-start.6 = ((f32[16,1,17408]{2,1,0:T(1,128)}), f32[16,1,17408]{2,1,0:T(1,128)S(1)}, u32[]{:S(2)}, u32[]{:S(2)}) async-start(f32[16,1,17408]{2,1,0:T(1,128)} %broadcast_in_dim.11), calls=%async_computation.6 | async-start | bytes 2228224 | tf_op jit(solution)/shard_map/all_to_all | solution.py:45
  420.8 2.2 copy-start.2

commit v15 on v12

--- a/solution.py
+++ b/solution.py
@@ -149,7 +149,7 @@
             tg_ref[pl.ds(row, 1), :] += own_ref[pl.ds(d, 1), :]
             return carry
 
-        lax.fori_loop(0, own_ref.shape[0], one_row, 0, unroll=8)
+        lax.fori_loop(0, own_ref.shape[0], one_row, 0, unroll=32)
         if final:
             out_ref = refs[1]
             for i in range(tg_ref.shape[0] // TS):

time: 286 us -> 287 us (level)
  no operation moved by 1% of the time
where the time goes in v15:
time: 287 us; the launch traced here: 285 us
  Pallas kernels  137 us (48%)
  starting transfers between devices  37.8 us (13%)
  local copies, waits for them, and re-layouts  32.6 us (11%)
  blocking collectives  29.1 us (10%)
  matrix products  19.7 us (7%)
  waiting for transfers between devices  19.5 us (7%)
  other arithmetic  7.37 us (3%)
    pallas_call x2, Pallas kernels, aggregate(): pl.pallas_call(functools.partial(agg_kernel, agg_scale, k_total, nt), gri...  81.2 us
    pallas_call x2, Pallas kernels, spread(): pl.pallas_call(functools.partial(spread_kernel, agg_scale, k_total, nt, f...  56.3 us
    all_to_all x1, blocking collectives, summed_over(): lax.all_to_all(flat, axis, 0, 0, tiled=True).reshape(n, -1).sum(axis=0)  29.1 us
    all_to_all x2, starting transfers between devices, summed_over(): lax.all_to_all(flat, axis, 0, 0, tiled=True).reshape(n, -1).sum(axis=0)  15.1 us
    all_to_all x2, waiting for transfers between devices, summed_over(): lax.all_to_all(flat, axis, 0, 0, tiled=True).reshape(n, -1).sum(axis=0)  14.2 us
    all_to_all x3, starting transfers between devices, summed_over(): lax.all_to_all(jnp.broadcast_to(mine[None], (n, mine.size)), axis, 0, 0,...  12.6 us
    all_to_all x1, starting transfers between devices, gathered_over(): lax.all_to_all(jnp.broadcast_to(x[None], (n, *x.shape)), axis, 0, 0, tile...  10.1 us
    unnamed x36, local copies, waits for them, and re-layouts  6.54 us
  transfers between devices with their start and end apart: 6, of which 2 were waited for; matrix products, arithmetic and copies ran while one was open for 13% of the time, Pallas kernels for 48%

profile of v15, /device:TPU:1, one launch (start us, length us, event | category | flops | bytes accessed | tf_op | source)
XLA Modules:
  0.0 284.7 jit_solution(17105025586886005502)
XLA Ops:
  0.6 1.7 broadcast_in_dim.8
  2.4 10.1 %all-to-all-start = ((bf16[16,2,64,128]{3,2,1,0:T(8,128)(2,1)}), bf16[16,2,64,128]{3,2,1,0:T(8,128)(2,1)}, u32[]{:S(2)}, u32[]{:S(2)}) async-start(bf16[16,2,64,128]{3,2,1,0:T(8,128)(2,1)} %broadcast_in_dim.8), calls=%async_computation | async-start | bytes 1048576 | tf_op jit(solution)/shard_map/all_to_all | solution.py:51
  16.2 2.0 copy.70
  18.2 3.2 %gather_fusion.1 = bf16[1024,64]{1,0:T(8,128)(2,1)S(1)} fusion(bf16[8192,64]{1,0:T(8,128)(2,1)S(1)} %bitcast.81, s32[1024]{0:T(1024)S(1)} %broadcast_clamp_fusion), kind=kCustom, calls=%fused_computation.1 | custom fusion | bytes 266240 | tf_op jit(solution)/shard_map/gather | solution.py:231
  21.4 2.3 slice_bitcast_fusion
  23.7 40.5 %shard_map.147 = (bf16[8,4,1024,256]{3,2,1,0:T(8,128)(2,1)}, bf16[64,1024]{1,0:T(8,128)(2,1)}) custom-call(s32[32]{0:T(128)} %squeeze.37.tiles_ref, bf16[64,8192]{1,0:T(8,128)(2,1)} %emb_ref.3, s32[8,1,16,1024]{3,2,1,0:T(8,128)} %get-tuple-element.19.rows_ref, s32[8,1,1,1024]{3,2,1,0:T(1,128)} %get-tuple-element.33.mask_ref), custom_call_target="tpu_custom_call" | custom-call | flops 1610612736 | bytes 17825792 | tf_op jit(solution)/shard_map/pallas_call | solution.py:110
  64.5 2.0 convolution_add_fusion
  66.5 7.5 %all-to-all-start.3 = ((f32[16,1,8192]{2,1,0:T(1,128)}), f32[16,1,8192]{2,1,0:T(1,128)S(1)}, u32[]{:S(2)}, u32[]{:S(2)}) async-start(f32[16,1,8192]{2,1,0:T(1,128)} %bitcast.93), calls=%async_computation.3 | async-start | bytes 1048576 | tf_op jit(solution)/shard_map/all_to_all | solution.py:44
  74.7 3.2 %gather_fusion = bf16[1024,64]{1,0:T(8,128)(2,1)S(1)} fusion(bf16[8192,64]{1,0:T(8,128)(2,1)S(1)} %bitcast.82, s32[1024]{0:T(1024)S(1)} %broadcast_clamp_fusion.1), kind=kCustom, calls=%fused_computation | custom fusion | bytes 266240 | tf_op jit(solution)/shard_map/gather | solution.py:231
  77.9 40.7 %shard_map.146 = (bf16[8,4,1024,256]{3,2,1,0:T(8,128)(2,1)}, bf16[64,1024]{1,0:T(8,128)(2,1)}) custom-call(s32[32]{0:T(128)} %squeeze.32.tiles_ref, bf16[64,8192]{1,0:T(8,128)(2,1)} %emb_ref.3, s32[8,1,16,1024]{3,2,1,0:T(8,128)} %get-tuple-element.20.rows_ref, s32[8,1,1,1024]{3,2,1,0:T(1,128)} %get-tuple-element.34.mask_ref), custom_call_target="tpu_custom_call" | custom-call | flops 1610612736 | bytes 17825792 | tf_op jit(solution)/shard_map/pallas_call | solution.py:110
  118.8 2.0 convolution_add_fusion.1
  120.7 7.6 %all-to-all-start.1 = ((f32[16,1,8192]{2,1,0:T(1,128)}), f32[16,1,8192]{2,1,0:T(1,128)S(1)}, u32[]{:S(2)}, u32[]{:S(2)}) async-start(f32[16,1,8192]{2,1,0:T(1,128)} %bitcast.10), calls=%async_computation.1 | async-start | bytes 1048576 | tf_op jit(solution)/shard_map/all_to_all | solution.py:44
  128.7 14.2 %all-to-all-done.1 = f32[16,1,8192]{2,1,0:T(1,128)S(1)} async-done(((f32[16,1,8192]{2,1,0:T(1,128)}), f32[16,1,8192]{2,1,0:T(1,128)S(1)}, u32[]{:S(2)}, u32[]{:S(2)}) %all-to-all-start.1) | async-done | bytes 524320 | tf_op jit(solution)/shard_map/all_to_all | solution.py:44
  142.9 1.2 broadcast_in_dim.10
  144.1 4.4 %all-to-all-start.4 = ((f32[16,1,8192]{2,1,0:T(1,128)}), f32[16,1,8192]{2,1,0:T(1,128)S(1)}, u32[]{:S(2)}, u32[]{:S(2)}) async-start(f32[16,1,8192]{2,1,0:T(1,128)} %broadcast_in_dim.10), calls=%async_computation.4 | async-start | bytes 1048576 | tf_op jit(solution)/shard_map/all_to_all | solution.py:45
  149.7 3.2 %scatter_custom_fusion = bf16[1024,128]{1,0:T(8,128)(2,1)S(1)} fusion(s32[1024]{0:T(1024)S(1)} %bitcast.101, bf16[1024,128]{1,0:T(8,128)(2,1)S(1)} %bitcast.95, bf16[]{:T(256)} %constant.12.clone.1), kind=kCustom, calls=%fused_computation.69 | custom fusion | bytes 262146 | tf_op jit(solution)/shard_map/scatter | solution.py:251
  153.0 3.2 %scatter_custom_fusion.1 = bf16[1024,128]{1,0:T(8,128)(2,1)S(1)} fusion(s32[1024]{0:T(1024)S(1)} %bitcast.100, bf16[1024,128]{1,0:T(8,128)(2,1)S(1)} %bitcast.94, bf16[]{:T(256)} %constant.12.clone.1), kind=kCustom, calls=%fused_computation.67 | custom fusion | bytes 262146 | tf_op jit(solution)/shard_map/scatter | solution.py:251
  156.6 5.3 %all-to-all-done.4 = f32[16,1,8192]{2,1,0:T(1,128)S(1)} async-done(((f32[16,1,8192]{2,1,0:T(1,128)}), f32[16,1,8192]{2,1,0:T(1,128)S(1)}, u32[]{:S(2)}, u32[]{:S(2)}) %all-to-all-start.4) | async-done | bytes 524320 | tf_op jit(solution)/shard_map/all_to_all | solution.py:45
  161.9 1.2 broadcast_in_dim.9
  163.1 4.3 %all-to-all-start.2 = ((f32[16,1,8192]{2,1,0:T(1,128)}), f32[16,1,8192]{2,1,0:T(1,128)S(1)}, u32[]{:S(2)}, u32[]{:S(2)}) async-start(f32[16,1,8192]{2,1,0:T(1,128)} %broadcast_in_dim.9), calls=%async_computation.2 | async-start | bytes 1048576 | tf_op jit(solution)/shard_map/all_to_all | solution.py:45
  168.1 3.0 %fusion.7 = bf16[1024,1024]{1,0:T(8,128)(2,1)S(1)} fusion(f32[1024,1024]{1,0:T(8,128)S(1)} %fusion.50, bf16[1024,128]{1,0:T(8,128)(2,1)S(1)} %scatter_custom_fusion.1, bf16[1024,128]{1,0:T(8,128)(2,1)S(1)} %copy-done.15), kind=kOutput, calls=%fused_computation.15 | convolution fusion | flops 288358400 | bytes 6815744 | tf_op jit(solution)/shard_map/dot_general | solution.py:32
  173.0 28.0 %shard_map.148.refs_0_ = f32[8192,64]{1,0:T(8,128)S(1)} custom-call(s32[1056]{0:T(1024)S(1)} %pad_add_fusion.1.tiles_ref, bf16[8,4,1024,256]{3,2,1,0:T(8,128)(2,1)} %get-tuple-element.13.counts_ref, bf16[1024,64]{1,0:T(8,128)(2,1)S(1)} %copy.75.back_ref, f32[1024,64]{1,0:T(8,128)S(1)} %fusion.58.own_ref), custom_call_target="tpu_custom_call" | custom-call | flops 1073741824 | bytes 20971520 | tf_op jit(solution)/shard_map/pallas_call | solution.py:186
  201.0 1.9 copy-done.1
  203.6 1.7 fusion.16
  206.3 3.0 %fusion.15 = bf16[1024,1024]{1,0:T(8,128)(2,1)S(1)} fusion(f32[1024,1024]{1,0:T(8,128)S(1)} %fusion.51, bf16[1024,128]{1,0:T(8,128)(2,1)S(1)} %scatter_custom_fusion, bf16[1024,128]{1,0:T(8,128)(2,1)S(1)} %copy-done.16), kind=kOutput, calls=%fused_computation.23 | convolution fusion | flops 288358400 | bytes 6815744 | tf_op jit(solution)/shard_map/dot_general | solution.py:32
  209.3 1.7 fusion.19
  213.1 29.1 %all_to_all.50 = f32[16,1,17408]{2,1,0:T(1,128)S(1)} all-to-all(f32[16,1,17408]{2,1,0:T(1,128)S(1)} %bitcast.91), channel_id=1, replica_groups=mesh['batch'=16,'feat'=16] {'batch'}, dimensions={0} | all-to-all | bytes 2228224 | tf_op jit(solution)/shard_map/all_to_all | solution.py:44
  242.9 1.6 broadcast_in_dim.11
  244.5 3.9 %all-to-all-start.6 = ((f32[16,1,17408]{2,1,0:T(1,128)}), f32[16,1,17408]{2,1,0:T(1,128)S(1)}, u32[]{:S(2)}, u32[]{:S(2)}) async-start(f32[16,1,17408]{2,1,0:T(1,128)} %broadcast_in_dim.11), calls=%async_computation.6 | async-start | bytes 2228224 | tf_op jit(solution)/shard_map/all_to_all | solution.py:45
  249.1 2.2 copy-done.2
  251.3 28.3 %shard_map.149 = f32[64,8192]{1,0:T(8,128)} custom-call(s32[1056]{0:T(1024)S(1)} %pad_add_fusion.tiles_ref, bf16[8,4,1024,256]{3,2,1,0:T(8,128)(2,1)} %get-tuple-element.11.counts_ref, bf16[1024,64]{1,0:T(8,128)(2,1)S(1)} %copy.77.back_ref, f32[1024,64]{1,0:T(8,128)S(1)} %fusion.59.own_ref, f32[8192,64]{1,0:T(8,128)S(1)} %copy-done.2), custom_call_target="tpu_custom_call" | custom-call | flops 1073741824 | bytes 20971520 | tf_op jit(solution)/shard_map/pallas_call | solution.py:186
  281.1 2.6 reduce.3
  (78 shorter events, 16.6 us)
Async XLA Ops:
  0.6 166.7 %copy-start = (bf16[128,1024]{1,0:T(8,128)(2,1)S(1)}, bf16[128,1024]{1,0:T(8,128)(2,1)}, u32[]{:S(2)}) copy-start(bf16[128,1024]{1,0:T(8,128)(2,1)} %param.14) | copy-start | bytes 786436
  2.4 64.1 %all-to-all-start = ((bf16[16,2,64,128]{3,2,1,0:T(8,128)(2,1)}), bf16[16,2,64,128]{3,2,1,0:T(8,128)(2,1)}, u32[]{:S(2)}, u32[]{:S(2)}) async-start(bf16[16,2,64,128]{3,2,1,0:T(8,128)(2,1)} %broadcast_in_dim.8), calls=%async_computation | async-start | bytes 1048576 | tf_op jit(solution)/shard_map/all_to_all | solution.py:51
  21.4 42.9 %copy-start.10 = (bf16[64,128]{1,0:T(8,128)(2,1)S(1)}, bf16[64,128]{1,0:T(8,128)(2,1)}, u32[]{:S(2)}) copy-start(bf16[64,128]{1,0:T(8,128)(2,1)} %param.12) | copy-start | bytes 49156
  21.4 43.0 %copy-start.9 = (bf16[64,128]{1,0:T(8,128)(2,1)S(1)}, bf16[64,128]{1,0:T(8,128)(2,1)}, u32[]{:S(2)}) copy-start(bf16[64,128]{1,0:T(8,128)(2,1)} %param.13) | copy-start | bytes 49156
  66.5 54.3 %all-to-all-start.3 = ((f32[16,1,8192]{2,1,0:T(1,128)}), f32[16,1,8192]{2,1,0:T(1,128)S(1)}, u32[]{:S(2)}, u32[]{:S(2)}) async-start(f32[16,1,8192]{2,1,0:T(1,128)} %bitcast.93), calls=%async_computation.3 | async-start | bytes 1048576 | tf_op jit(solution)/shard_map/all_to_all | solution.py:44
  77.9 70.6 %copy-start.11 = (s32[2,1024]{1,0:T(2,128)S(1)}, s32[2,1024]{1,0:T(2,128)}, u32[]{:S(2)}) copy-start(s32[2,1024]{1,0:T(2,128)} %param.19) | copy-start | bytes 24580
  77.9 70.6 %copy-start.14 = (s32[32]{0:T(128)S(1)}, s32[32]{0:T(128)}, u32[]{:S(2)}) copy-start(s32[32]{0:T(128)} %squeeze.37.tiles_ref) | copy-start | bytes 388
  77.9 70.7 %copy-start.12 = (s32[2,1,1024]{2,1,0:T(1,128)S(1)}, s32[2,1,1024]{2,1,0:T(1,128)}, u32[]{:S(2)}) copy-start(s32[2,1,1024]{2,1,0:T(1,128)} %param.20) | copy-start | bytes 24580
  120.7 22.1 %all-to-all-start.1 = ((f32[16,1,8192]{2,1,0:T(1,128)}), f32[16,1,8192]{2,1,0:T(1,128)S(1)}, u32[]{:S(2)}, u32[]{:S(2)}) async-start(f32[16,1,8192]{2,1,0:T(1,128)} %bitcast.10), calls=%async_computation.1 | async-start | bytes 1048576 | tf_op jit(solution)/shard_map/all_to_all | solution.py:44
  144.1 17.8 %all-to-all-start.4 = ((f32[16,1,8192]{2,1,0:T(1,128)}), f32[16,1,8192]{2,1,0:T(1,128)S(1)}, u32[]{:S(2)}, u32[]{:S(2)}) async-start(f32[16,1,8192]{2,1,0:T(1,128)} %broadcast_in_dim.10), calls=%async_computation.4 | async-start | bytes 1048576 | tf_op jit(solution)/shard_map/all_to_all | solution.py:45
  148.6 19.5 %copy-start.15 = (bf16[1024,128]{1,0:T(8,128)(2,1)S(1)}, bf16[1024,128]{1,0:T(8,128)(2,1)}, u32[]{:S(2)}) copy-start(bf16[1024,128]{1,0:T(8,128)(2,1)} %param.15) | copy-start | bytes 786436
  163.1 42.3 %all-to-all-start.2 = ((f32[16,1,8192]{2,1,0:T(1,128)}), f32[16,1,8192]{2,1,0:T(1,128)S(1)}, u32[]{:S(2)}, u32[]{:S(2)}) async-start(f32[16,1,8192]{2,1,0:T(1,128)} %broadcast_in_dim.9), calls=%async_computation.2 | async-start | bytes 1048576 | tf_op jit(solution)/shard_map/all_to_all | solution.py:45
  168.1 3.0 %copy-start.3 = (f32[1024,1024]{1,0:T(8,128)}, f32[1024,1024]{1,0:T(8,128)S(1)}, u32[]{:S(2)}) copy-start(f32[1024,1024]{1,0:T(8,128)S(1)} %fusion.50) | copy-start | bytes 12582916
  171.1 1.5 copy-start.5
  171.1 1.1 copy-start.8
  173.0 30.0 %copy-start.6 = (bf16[1024,1024]{1,0:T(8,128)(2,1)S(1)}, bf16[1024,1024]{1,0:T(8,128)(2,1)}, u32[]{:S(2)}) copy-start(bf16[1024,1024]{1,0:T(8,128)(2,1)} %copy-done.5) | copy-start | bytes 6291460
  173.0 30.6 %copy-start.4 = (f32[1024,1024]{1,0:T(8,128)S(1)}, f32[1024,1024]{1,0:T(8,128)}, u32[]{:S(2)}) copy-start(f32[1024,1024]{1,0:T(8,128)} %copy-done.3) | copy-start | bytes 12582916
  201.0 1.9 copy-start.1
  205.3 1.0 copy-start.16
  211.0 1.7 copy-start.7
  213.0 35.4 %copy-start.13 = (s32[32]{0:T(128)S(1)}, s32[32]{0:T(128)}, u32[]{:S(2)}) copy-start(s32[32]{0:T(128)} %squeeze.32.tiles_ref) | copy-start | bytes 388
  244.5 35.1 %all-to-all-start.6 = ((f32[16,1,17408]{2,1,0:T(1,128)}), f32[16,1,17408]{2,1,0:T(1,128)S(1)}, u32[]{:S(2)}, u32[]{:S(2)}) async-start(f32[16,1,17408]{2,1,0:T(1,128)} %broadcast_in_dim.11), calls=%async_computation.6 | async-start | bytes 2228224 | tf_op jit(solution)/shard_map/all_to_all | solution.py:45
  249.1 2.2 copy-start.2
